TPU v7x, 32 devices: a whole 2x2x4 slice. The times are simulated.
32 devices in a mesh: ctx: 8 (over z, y), fsdp: 4 (over x, core).
Axes of the slice: x: 2, y: 2, z: 4, core: 2. Of those that a mesh axis runs over, the one named last changes fastest.
Arguments:
- tokens: bfloat16 [6144, 768], P(('ctx', 'fsdp')), may hold values from -6 to 6
- document_starts: int32 [8], replicated, may hold values from 0 to 6143, as said below
- attend_weight: bfloat16 [768, 2304], P('fsdp'), may hold values from -0.3125 to 0.3125
- attend_bias: bfloat16 [1536], P('fsdp'), may hold values from -3 to 3
- project_weight: bfloat16 [768, 768], P('fsdp'), may hold values from -4 to 4
- project_bias: bfloat16 [768], P('fsdp'), may hold values from -4 to 4
- expand_weight: bfloat16 [768, 3072], P('fsdp'), may hold values from -0.21875 to 0.21875
- expand_bias: bfloat16 [3072], P('fsdp'), may hold values from -3 to 3
- contract_weight: bfloat16 [3072, 768], P('fsdp'), may hold values from -0.75 to 0.75
- contract_bias: bfloat16 [768], P('fsdp'), may hold values from -4 to 4
- gain_first: bfloat16 [768], P('fsdp'), may hold values from 0.5 to 1.5
- shift_first: bfloat16 [768], P('fsdp'), may hold values from -2 to 2
- gain_second: bfloat16 [768], P('fsdp'), may hold values from 0.5 to 1.5
- shift_second: bfloat16 [768], P('fsdp'), may hold values from -2 to 2
- cotangent: bfloat16 [6144, 768], P(('ctx', 'fsdp')), may hold values from -6 to 6
Outputs:
- block_output: bfloat16 [6144, 768], P(('ctx', 'fsdp'))
- tokens_grad: bfloat16 [6144, 768], P(('ctx', 'fsdp'))
- attend_grad: float32 [768, 2304], P('fsdp')
- attbias_grad: float32 [1536], P('fsdp')
- project_grad: float32 [768, 768], P('fsdp')
- projbias_grad: float32 [768], P('fsdp')
- expand_grad: float32 [768, 3072], P('fsdp')
- expbias_grad: float32 [3072], P('fsdp')
- contract_grad: float32 [3072, 768], P('fsdp')
- conbias_grad: float32 [768], P('fsdp')
- gainone_grad: float32 [768], P('fsdp')
- shiftone_grad: float32 [768], P('fsdp')
- gaintwo_grad: float32 [768], P('fsdp')
- shifttwo_grad: float32 [768], P('fsdp')
Inputs may be any that keep to these rules, and one draw needn't show every extreme that they name: document_starts is strictly increasing and its first entry is 0; a document runs from its start to the next start, the last one to the end of the stream.
All inputs are finite; a program needn't handle non-finite values.
Results may differ from a plain program's by a relative error of at most 0.017.
Values may be sent and summed in bfloat16 or wider, within the bound.
A program may use at most 320 MiB of HBM per device.

v0:
```python
import jax
import jax.numpy as jnp
from jax import lax
from jax.sharding import PartitionSpec as P

D = 768
H = 12
HD = 64


EPS = 1e-05
SCALE = 0.125
BRANCH = 48.0 ** (-0.5)
NEG = -1e30


def passed_along(value, axis, by):
    count = lax.axis_size(axis)
    return lax.ppermute(value, axis, [(i, (i + by) % count) for i in range(count)])


def normalize(rows_in, gain, shift):
    mean = jnp.mean(rows_in, axis=1, keepdims=True)
    centered = rows_in - mean
    inverse = lax.rsqrt(jnp.mean(centered * centered, axis=1, keepdims=True) + EPS)
    unit = centered * inverse
    return (unit * gain + shift, unit, inverse)


def normalize_back(incoming, unit, inverse, gain):
    scaled = incoming * gain
    spread = (
        scaled
        - jnp.mean(scaled, axis=1, keepdims=True)
        - unit * jnp.mean(scaled * unit, axis=1, keepdims=True)
    )
    return (inverse * spread, jnp.sum(incoming * unit, axis=0), jnp.sum(incoming, axis=0))


def first_position(places, starts):
    below = starts[None, :] <= places[:, None]
    return jnp.max(jnp.where(below, starts[None, :], 0), axis=1)


def visible(query_places, query_begins, key_places):
    later = key_places[None, :] <= query_places[:, None]
    inside = key_places[None, :] >= query_begins[:, None]
    return (later & inside)[None]


def split_rows(array_in, width):
    return array_in.reshape((array_in.shape[0] // width, width) + array_in.shape[1:])


def in_blocks(step, carry, piece, start):
    count = jax.tree.leaves(piece)[0].shape[0]
    width = max((size for size in range(1, min(count, 1024) + 1) if count % size == 0))
    if width == count:
        return step(carry, piece, start)
    pieces = jax.tree.map(lambda array_in: split_rows(array_in, width), piece)

    def turn(state, operands):
        number, block = operands
        return (step(state, block, start + number * width), None)

    numbers = jnp.arange(count // width, dtype=jnp.int32)
    carry, unused = lax.scan(turn, carry, (numbers, pieces))
    return carry


def per_device(
    tokens,
    document_starts,
    attend_weight,
    attend_bias,
    project_weight,
    project_bias,
    expand_weight,
    expand_bias,
    contract_weight,
    contract_bias,
    gain_first,
    shift_first,
    gain_second,
    shift_second,
    cotangent,
):
    row_count = tokens.shape[0]
    stream_length = row_count * lax.axis_size(("ctx", "fsdp"))
    shard_params = (
        attend_weight,
        attend_bias,
        project_weight,
        project_bias,
        expand_weight,
        expand_bias,
        contract_weight,
        contract_bias,
        gain_first,
        shift_first,
        gain_second,
        shift_second,
    )
    gathered = (
        lax.all_gather(shard_params[0], "fsdp", axis=0, tiled=True),
        lax.all_gather(shard_params[1], "fsdp", axis=0, tiled=True),
        lax.all_gather(shard_params[2], "fsdp", axis=0, tiled=True),
        lax.all_gather(shard_params[3], "fsdp", axis=0, tiled=True),
        lax.all_gather(shard_params[4], "fsdp", axis=0, tiled=True),
        lax.all_gather(shard_params[5], "fsdp", axis=0, tiled=True),
        lax.all_gather(shard_params[6], "fsdp", axis=0, tiled=True),
        lax.all_gather(shard_params[7], "fsdp", axis=0, tiled=True),
        lax.all_gather(shard_params[8], "fsdp", axis=0, tiled=True),
        lax.all_gather(shard_params[9], "fsdp", axis=0, tiled=True),
        lax.all_gather(shard_params[10], "fsdp", axis=0, tiled=True),
        lax.all_gather(shard_params[11], "fsdp", axis=0, tiled=True),
    )
    (
        attend_w,
        attend_b,
        project_w,
        project_b,
        expand_w,
        expand_b,
        contract_w,
        contract_b,
        gain_one,
        shift_one,
        gain_two,
        shift_two,
    ) = gathered
    attend_b = attend_b.astype(jnp.float32)
    anchor = lax.axis_index(("ctx", "fsdp")) * row_count
    places = anchor + jnp.arange(row_count, dtype=jnp.int32)
    begins = first_position(places, document_starts)
    hidden_in = tokens.astype(jnp.float32)
    normed, unit_one, inverse_one = normalize(
        hidden_in, gain_one.astype(jnp.float32), shift_one.astype(jnp.float32)
    )
    normed_low = normed.astype(jnp.bfloat16)
    offsets = jnp.concatenate([attend_b[:D], jnp.zeros((D,), jnp.float32), attend_b[D:]])
    triple = (jnp.dot(normed_low, attend_w, preferred_element_type=jnp.float32) + offsets).astype(
        jnp.bfloat16
    )
    query_low = triple[:, :D]
    key_low = triple[:, D : 2 * D]
    value_low = triple[:, 2 * D :]
    query_heads = query_low.reshape(row_count, H, HD)
    key_heads = key_low.reshape(row_count, H, HD)
    value_heads = value_low.reshape(row_count, H, HD)

    def forward_step(carry, piece, start):
        peak, total, summed = carry
        keys_in, values_in = piece
        count = keys_in.shape[0]
        key_places = start + jnp.arange(count, dtype=jnp.int32)
        allowed = visible(places, begins, key_places)
        scores = (
            jnp.einsum(
                "qhd,khd->hqk",
                query_heads,
                keys_in.reshape(count, H, HD),
                preferred_element_type=jnp.float32,
            )
            * SCALE
        )
        scores = jnp.where(allowed, scores, NEG)
        new_peak = jnp.maximum(peak, jnp.max(scores, axis=2))
        weights = jnp.where(allowed, jnp.exp(scores - new_peak[:, :, None]), 0.0)
        factor = jnp.exp(peak - new_peak)
        total = total * factor + jnp.sum(weights, axis=2)
        update = jnp.einsum(
            "hqk,khd->qhd",
            weights.astype(jnp.bfloat16),
            values_in.reshape(count, H, HD),
            preferred_element_type=jnp.float32,
        )
        summed = summed * factor.T[:, :, None] + update
        return (new_peak, total, summed)

    start_state = (
        jnp.full((H, row_count), NEG, jnp.float32),
        jnp.zeros((H, row_count), jnp.float32),
        jnp.zeros((row_count, H, HD), jnp.float32),
    )
    peak, total, summed = in_blocks(
        forward_step,
        start_state,
        (
            lax.all_gather(key_low, ("ctx", "fsdp"), axis=0, tiled=True),
            lax.all_gather(value_low, ("ctx", "fsdp"), axis=0, tiled=True),
        ),
        jnp.int32(0),
    )
    log_total = peak + jnp.log(total)
    attended_exact = (summed / total.T[:, :, None]).reshape(row_count, D)
    attended = attended_exact.astype(jnp.bfloat16)
    middle = hidden_in + BRANCH * (
        jnp.dot(attended, project_w, preferred_element_type=jnp.float32)
        + project_b.astype(jnp.float32)
    )
    normed_two, unit_two, inverse_two = normalize(
        middle, gain_two.astype(jnp.float32), shift_two.astype(jnp.float32)
    )
    normed_two_low = normed_two.astype(jnp.bfloat16)
    expanded = jnp.dot(
        normed_two_low, expand_w, preferred_element_type=jnp.float32
    ) + expand_b.astype(jnp.float32)
    activation, gelu_pull = jax.vjp(
        lambda values_in: jax.nn.gelu(values_in, approximate=True), expanded
    )
    activated = activation.astype(jnp.bfloat16)
    block_output = middle + BRANCH * (
        jnp.dot(activated, contract_w, preferred_element_type=jnp.float32)
        + contract_b.astype(jnp.float32)
    )
    (
        attend_w,
        unused_one,
        project_w,
        unused_two,
        expand_w,
        unused_three,
        contract_w,
        unused_four,
        gain_one,
        unused_five,
        gain_two,
        unused_six,
    ) = gathered
    incoming = cotangent.astype(jnp.float32)
    grad_two = (BRANCH * incoming).astype(jnp.bfloat16)
    conbias_grad = jnp.sum(grad_two.astype(jnp.float32), axis=0)
    grad_activated = jnp.einsum(
        "tj,ij->ti", grad_two, contract_w, preferred_element_type=jnp.float32
    )
    grad_expanded = gelu_pull(grad_activated)[0].astype(jnp.bfloat16)
    expbias_grad = jnp.sum(grad_expanded.astype(jnp.float32), axis=0)
    grad_normed_two = jnp.einsum(
        "tj,ij->ti", grad_expanded, expand_w, preferred_element_type=jnp.float32
    )
    middle_part, gaintwo_grad, shifttwo_grad = normalize_back(
        grad_normed_two, unit_two, inverse_two, gain_two.astype(jnp.float32)
    )
    grad_middle = incoming + middle_part
    grad_one = (BRANCH * grad_middle).astype(jnp.bfloat16)
    projbias_grad = jnp.sum(grad_one.astype(jnp.float32), axis=0)
    grad_attended = jnp.einsum(
        "tj,ij->ti", grad_one, project_w, preferred_element_type=jnp.float32
    ).astype(jnp.bfloat16)
    grad_heads = grad_attended.reshape(row_count, H, HD)
    delta = jnp.sum(
        (grad_attended.astype(jnp.float32) * attended_exact).reshape(row_count, H, HD), axis=2
    )
    delta_heads = delta.T

    def query_step(grad_query, piece, start):
        keys_in, values_in = piece
        count = keys_in.shape[0]
        key_places = start + jnp.arange(count, dtype=jnp.int32)
        allowed = visible(places, begins, key_places)
        keys_split = keys_in.reshape(count, H, HD)
        scores = (
            jnp.einsum("qhd,khd->hqk", query_heads, keys_split, preferred_element_type=jnp.float32)
            * SCALE
        )
        probs = jnp.where(allowed, jnp.exp(scores - log_total[:, :, None]), 0.0)
        grad_probs = jnp.einsum(
            "qhd,khd->hqk",
            grad_heads,
            values_in.reshape(count, H, HD),
            preferred_element_type=jnp.float32,
        )
        grad_scores = (probs * (grad_probs - delta_heads[:, :, None])).astype(jnp.bfloat16)
        return (
            grad_query
            + jnp.einsum(
                "hqk,khd->qhd", grad_scores, keys_split, preferred_element_type=jnp.float32
            )
            * SCALE
        )

    def make_key_fold(lead):

        def key_step(carry, piece, start):
            grad_key, grad_value = carry
            queries_in, grads_in, totals_in, deltas_in = piece
            count = queries_in.shape[0]
            query_places = (start + lead + jnp.arange(count, dtype=jnp.int32)) % stream_length
            allowed = visible(query_places, first_position(query_places, document_starts), places)
            queries_split = queries_in.reshape(count, H, HD)
            grads_split = grads_in.reshape(count, H, HD)
            scores = (
                jnp.einsum(
                    "qhd,khd->hqk", queries_split, key_heads, preferred_element_type=jnp.float32
                )
                * SCALE
            )
            probs = jnp.where(allowed, jnp.exp(scores - totals_in.T[:, :, None]), 0.0)
            grad_value = grad_value + jnp.einsum(
                "hqk,qhd->khd",
                probs.astype(jnp.bfloat16),
                grads_split,
                preferred_element_type=jnp.float32,
            )
            grad_probs = jnp.einsum(
                "qhd,khd->hqk", grads_split, value_heads, preferred_element_type=jnp.float32
            )
            grad_scores = (probs * (grad_probs - deltas_in.T[:, :, None])).astype(jnp.bfloat16)
            grad_key = (
                grad_key
                + jnp.einsum(
                    "hqk,qhd->khd", grad_scores, queries_split, preferred_element_type=jnp.float32
                )
                * SCALE
            )
            return (grad_key, grad_value)

        def key_fold_step(carry, piece, start):
            return in_blocks(key_step, carry, piece, start)

        return key_fold_step

    zero_heads = jnp.zeros((row_count, H, HD), jnp.float32)
    query_side = (query_low, grad_attended, log_total.T, delta)
    grad_query = in_blocks(
        query_step,
        zero_heads,
        (
            lax.all_gather(key_low, ("ctx", "fsdp"), axis=0, tiled=True),
            lax.all_gather(value_low, ("ctx", "fsdp"), axis=0, tiled=True),
        ),
        jnp.int32(0),
    )
    next_side = (
        passed_along(query_side[0].astype(jnp.float32), ("ctx", "fsdp"), -1).astype(jnp.bfloat16),
        passed_along(query_side[1].astype(jnp.float32), ("ctx", "fsdp"), -1).astype(jnp.bfloat16),
        passed_along(query_side[2], ("ctx", "fsdp"), -1),
        passed_along(query_side[3], ("ctx", "fsdp"), -1),
    )
    grad_key, grad_value = make_key_fold(row_count)(
        (zero_heads, zero_heads),
        (
            lax.all_gather(
                next_side[0].astype(jnp.float32), ("ctx", "fsdp"), axis=0, tiled=True
            ).astype(jnp.bfloat16),
            lax.all_gather(
                next_side[1].astype(jnp.float32), ("ctx", "fsdp"), axis=0, tiled=True
            ).astype(jnp.bfloat16),
            lax.all_gather(next_side[2], ("ctx", "fsdp"), axis=0, tiled=True),
            lax.all_gather(next_side[3], ("ctx", "fsdp"), axis=0, tiled=True),
        ),
        jnp.int32(0),
    )
    grad_triple = jnp.concatenate(
        [
            grad_query.reshape(row_count, D),
            grad_key.reshape(row_count, D),
            grad_value.reshape(row_count, D),
        ],
        axis=1,
    ).astype(jnp.bfloat16)
    triple_sums = jnp.sum(grad_triple.astype(jnp.float32), axis=0)
    attbias_grad = jnp.concatenate([triple_sums[:D], triple_sums[2 * D :]])
    grad_normed = jnp.einsum("tj,ij->ti", grad_triple, attend_w, preferred_element_type=jnp.float32)
    first_part, gainone_grad, shiftone_grad = normalize_back(
        grad_normed, unit_one, inverse_one, gain_one.astype(jnp.float32)
    )
    tokens_grad = grad_middle + first_part
    vector_grads = (
        attbias_grad,
        projbias_grad,
        expbias_grad,
        conbias_grad,
        gainone_grad,
        shiftone_grad,
        gaintwo_grad,
        shifttwo_grad,
    )
    attend_grad = jnp.einsum(
        "ti,tj->ij", normed_low, grad_triple, preferred_element_type=jnp.float32
    )
    project_grad = jnp.einsum("ti,tj->ij", attended, grad_one, preferred_element_type=jnp.float32)
    expand_grad = jnp.einsum(
        "ti,tj->ij", normed_two_low, grad_expanded, preferred_element_type=jnp.float32
    )
    contract_grad = jnp.einsum("ti,tj->ij", activated, grad_two, preferred_element_type=jnp.float32)
    to_scatter = (attend_grad, project_grad, expand_grad, contract_grad) + vector_grads
    scattered = lax.psum_scatter(to_scatter, "fsdp", scatter_dimension=0, tiled=True)
    matrix_shards = tuple(scattered[:4])
    vector_shards = tuple(scattered[4:])
    ordered = (
        matrix_shards[0],
        vector_shards[0],
        matrix_shards[1],
        vector_shards[1],
        matrix_shards[2],
        vector_shards[2],
        matrix_shards[3],
        vector_shards[3],
        vector_shards[4],
        vector_shards[5],
        vector_shards[6],
        vector_shards[7],
    )
    total_grads = lax.psum(
        (
            ordered[0],
            ordered[1],
            ordered[2],
            ordered[3],
            ordered[4],
            ordered[5],
            ordered[6],
            ordered[7],
            ordered[8],
            ordered[9],
            ordered[10],
            ordered[11],
        ),
        "ctx",
    )
    return (block_output.astype(jnp.bfloat16), tokens_grad.astype(jnp.bfloat16)) + tuple(
        total_grads
    )


def solution(mesh):
    in_specs = (
        P(("ctx", "fsdp"), None),
        P(),
        P("fsdp", None),
        P("fsdp"),
        P("fsdp", None),
        P("fsdp"),
        P("fsdp", None),
        P("fsdp"),
        P("fsdp", None),
        P("fsdp"),
        P("fsdp"),
        P("fsdp"),
        P("fsdp"),
        P("fsdp"),
        P(("ctx", "fsdp"), None),
    )
    out_specs = (
        P(("ctx", "fsdp"), None),
        P(("ctx", "fsdp"), None),
        P("fsdp", None),
        P("fsdp"),
        P("fsdp", None),
        P("fsdp"),
        P("fsdp", None),
        P("fsdp"),
        P("fsdp", None),
        P("fsdp"),
        P("fsdp"),
        P("fsdp"),
        P("fsdp"),
        P("fsdp"),
    )
    return jax.shard_map(
        per_device, mesh=mesh, in_specs=in_specs, out_specs=out_specs, check_vma=False
    )
```

profile of v0, /device:TPU:3, one launch (start us, length us, event | category | flops | bytes accessed | tf_op | source)
XLA Modules:
  0.0 1116.9 jit_solution(6724650270096796833)
XLA Ops:
  15.0 10.7 all-reduce.17
  58.4 70.4 %all-gather.15.cloned.1.call-done = bf16[6144,768]{1,0:T(8,128)(2,1)} async-done(((bf16[192,768]{1,0:T(8,128)(2,1)}), bf16[6144,768]{1,0:T(8,128)(2,1)}) %all-gather.15.cloned.1.call-update) | async-done | bytes 9437200 | tf_op jit(solution)/shard_map/all_gather | solution.py:190
  128.8 12.7 %copy.73 = bf16[6,1024,768]{1,2,0:T(8,128)(2,1)} copy(bf16[6,1024,768]{2,1,0:T(8,128)(2,1)} %bitcast.207) | data formatting | bytes 18874368
  141.5 71.4 %all-gather.17.cloned.1.call-done = bf16[6144,768]{1,0:T(8,128)(2,1)} async-done(((bf16[192,768]{1,0:T(8,128)(2,1)}), bf16[6144,768]{1,0:T(8,128)(2,1)}) %all-gather.17.cloned.1.call-update) | async-done | bytes 9437200 | tf_op jit(solution)/shard_map/all_gather | solution.py:191
  212.9 12.7 %copy.74 = bf16[6,1024,768]{1,2,0:T(8,128)(2,1)} copy(bf16[6,1024,768]{2,1,0:T(8,128)(2,1)} %bitcast.208) | data formatting | bytes 18874368
  225.6 114.4 %while.41 = (s32[]{:T(128)}, f32[12,192]{1,0:T(8,128)S(1)}, f32[12,192]{1,0:T(8,128)S(1)}, f32[192,12,64]{0,2,1:T(8,128)S(1)}, s32[6]{0:T(128)S(1)}, /*index=5*/...) while((s32[]{:T(128)}, f32[12,192]{1,0:T(8,128)S(1)}, ...), condition=%wide.region_6.7_spmd.clone, body=%wide.region_3.6_spmd.clone.sunk | while | flops 635697856 | bytes 77916616 | solution.py:67
  361.3 13.7 %collective-permute-done.2 = bf16[192,768]{1,0:T(8,128)(2,1)} collective-permute-done((bf16[192,768]{1,0:T(8,128)(2,1)S(1)}, bf16[192,768]{1,0:T(8,128)(2,1)}, u32[]{:S(2)}, u32[]{:S(2)}) %collective-permute-start.2) | collective-permute-done | bytes 294944 | tf_op jit(solution)/shard_map/ppermute | solution.py:19
  388.8 111.9 %while.42 = (s32[]{:T(128)}, f32[192,12,64]{0,2,1:T(8,128)}, bf16[6,1024,768]{1,2,0:T(8,128)(2,1)}, s32[6]{0:T(128)S(1)}, s32[192]{0:T(256)S(1)}, /*index=5*/bf1...) while((s32[]{:T(128)}, f32[192,12,64]{0,2,1:T(8,128)}, ...), condition=%wide.region_13.14_spmd.clone, body=%wide.region_12.13_spmd.clone.sunk | while | flops 921158848 | bytes 32076208 | solution.py:67
  453.8 9.3 fusion.182
  472.4 9.5 fusion.182
  491.4 9.3 fusion.182
  509.7 43.2 %all-gather.3 = f32[32,192,12]{1,2,0:T(8,128)S(1)} all-gather(f32[1,192,12]{1,2,0:T(8,128)} %bitcast.17), channel_id=1, replica_groups=mesh['ctx'=8,'fsdp'=4] {'ctx','fsdp'}, dimensions={0}, use_global_device_ids=true | all-gather | bytes 304128 | tf_op jit(solution)/shard_map/all_gather | solution.py:351
  554.1 39.3 %all-gather.2 = f32[32,192,12]{1,2,0:T(8,128)S(1)} all-gather(f32[1,192,12]{1,2,0:T(8,128)S(1)} %bitcast.229), channel_id=1, replica_groups=mesh['ctx'=8,'fsdp'=4] {'ctx','fsdp'}, dimensions={0}, use_global_device_ids=true | all-gather | bytes 304128 | tf_op jit(solution)/shard_map/all_gather | solution.py:350
  594.7 197.1 %while.43 = (s32[]{:T(128)}, f32[192,12,64]{0,2,1:T(8,128)}, f32[192,12,64]{0,2,1:T(8,128)}, bf16[6,1024,768]{2,1,0:T(8,128)(2,1)}, s32[6]{0:T(128)S(1)}, /*inde...) while((s32[]{:T(128)}, f32[192,12,64]{0,2,1:T(8,128)}, ...), condition=%wide.region_16.17_spmd.clone, body=%wide.region_14.16_spmd.clone.sunk | while | flops 1232910592 | bytes 57775912 | solution.py:67
  619.2 9.9 fusion.191
  652.4 9.3 fusion.191
  685.0 9.3 fusion.191
  717.5 9.3 fusion.191
  750.1 9.3 fusion.191
  782.6 9.3 fusion.191
  799.8 60.8 %reduce-scatter.5.cloned.1.call-done = f32[192,2304]{1,0:T(8,128)} async-done(((f32[768,2304]{1,0:T(8,128)}), f32[192,2304]{1,0:T(8,128)}) %reduce-scatter.5.cloned.1.call-update) | async-done | bytes 1769488 | tf_op jit(solution)/shard_map/reduce_scatter | solution.py:389
  869.7 11.4 %all-reduce.16 = (f32[1536]{0:T(1024)S(1)}, f32[768]{0:T(1024)S(1)}, f32[3072]{0:T(1024)S(1)}, f32[768]{0:T(1024)S(1)}, f32[768]{0:T(1024)S(1)}, /*index=5*/f32[...) all-reduce(f32[1536]{0:T(1024)S(1)} %pad_maximum_fusion.2, ...), channel_id=3, replica_groups=mesh['ctx'=8,'fsdp'=4] {'fsdp'}, use_global_device_ids=true, to_apply=%region_22.23.clone | all-reduce | flops 9216 | bytes 73728
  881.7 32.7 %all-reduce.14 = (f32[384]{0:T(512)}, f32[192]{0:T(256)}, f32[768]{0:T(1024)}, f32[192]{0:T(256)}, f32[192]{0:T(256)}, /*index=5*/f32[192]{0:T(256)}, f32[192]{0:T(256)}, f32[192]{0:T(256)}) all-reduce(f32[384]{0:T(512)S(1)} %dynamic-slice.7, f32[192]{0:T(256)S(1)} %dynamic-slice.9, ...), channel_id=1, replica_groups=mesh['ctx'=8,'fsdp'=4] {'ctx'}, use_global_device_ids=true, to_apply=%region_23.24 | all-reduce | flops 2304 | bytes 18432 | tf_op jit(solution)/shard_map/psum | solution.py:406
  915.3 187.2 %all-reduce.20.cloned.1.call-done = (f32[192,2304]{1,0:T(8,128)}, f32[192,768]{1,0:T(8,128)}, f32[192,3072]{1,0:T(8,128)}, f32[768,768]{1,0:T(8,128)}) async-done(((f32[192,2304]{1,0:T(8,128)}, f32[192,768]{1,0:T(8,128)}, f32[192,3072]{1,0:T(8,128)}, f32[768,768]{1,0:T(8,128)}), (f32[192,2304]{1,0:T(8,128)}, f32[192,768]{1,0:T(8,128)}, f32[192,3072]{1,0:T(8,128)}, ...) | async-done | bytes 7077904 | tf_op jit(solution)/shard_map/psum | solution.py:406
  (450 shorter events, 436.0 us)
Async XLA Ops:
  7.2 33.9 %all-gather.13.cloned.1.call-start = ((), (), s32[]{:S(2)}) async-start(), calls=%async_computation.4 | async-start | bytes 4423680 | tf_op jit(solution)/shard_map/all_gather | solution.py:105
  7.9 120.9 %all-gather.15.cloned.1.call-start = ((), (), s32[]{:S(2)}) async-start(), calls=%async_computation.5 | async-start | bytes 9732096 | tf_op jit(solution)/shard_map/all_gather | solution.py:190
  25.7 15.3 %copy-start.30 = (f32[768]{0:T(1024)}, f32[768]{0:T(1024)S(1)}, u32[]{:S(2)}) copy-start(f32[768]{0:T(1024)S(1)} %convert_element_type.122) | copy-start | bytes 9220
  25.7 15.3 %copy-start.32 = (f32[768]{0:T(1024)}, f32[768]{0:T(1024)S(1)}, u32[]{:S(2)}) copy-start(f32[768]{0:T(1024)S(1)} %convert_element_type.123) | copy-start | bytes 9220
  45.1 167.9 %all-gather.17.cloned.1.call-start = ((), (), s32[]{:S(2)}) async-start(), calls=%async_computation.6 | async-start | bytes 9732096 | tf_op jit(solution)/shard_map/all_gather | solution.py:191
  45.8 297.4 %all-gather.19.cloned.1.call-start = ((), (), s32[]{:S(2)}) async-start(), calls=%async_computation.7 | async-start | bytes 1474560 | tf_op jit(solution)/shard_map/all_gather | solution.py:107
  46.4 299.0 %all-gather.21.cloned.1.call-start = ((), (), s32[]{:S(2)}) async-start(), calls=%async_computation.8 | async-start | bytes 5898240 | tf_op jit(solution)/shard_map/all_gather | solution.py:109
  47.0 303.4 %all-gather.23.cloned.1.call-start = ((), (), s32[]{:S(2)}) async-start(), calls=%async_computation.9 | async-start | bytes 5898240 | tf_op jit(solution)/shard_map/all_gather | solution.py:111
  47.5 547.2 %all-gather.25.cloned.1.call-start = ((), (), s32[]{:S(2)}) async-start(), calls=%async_computation.10 | async-start | bytes 9732096 | tf_op jit(solution)/shard_map/all_gather | solution.py:344
  47.6 9.9 collective-permute-start
  58.2 536.5 %all-gather.27.cloned.1.call-start = ((), (), s32[]{:S(2)}) async-start(), calls=%async_computation.11 | async-start | bytes 9732096 | tf_op jit(solution)/shard_map/all_gather | solution.py:347
  345.1 31.9 %copy-start.2 = (f32[192,768]{1,0:T(8,128)}, f32[192,768]{1,0:T(8,128)S(1)}, u32[]{:S(2)}) copy-start(f32[192,768]{1,0:T(8,128)S(1)} %get-tuple-element.657) | copy-start | bytes 1769476
  360.0 17.0 %copy-start.7 = (f32[192,768]{1,0:T(8,128)}, f32[192,768]{1,0:T(8,128)S(1)}, u32[]{:S(2)}) copy-start(f32[192,768]{1,0:T(8,128)S(1)} %get-tuple-element.636) | copy-start | bytes 1769476
  361.0 14.0 %collective-permute-start.2 = (bf16[192,768]{1,0:T(8,128)(2,1)S(1)}, bf16[192,768]{1,0:T(8,128)(2,1)}, u32[]{:S(2)}, u32[]{:S(2)}) collective-permute-start(bf16[192,768]{1,0:T(8,128)(2,1)S(1)} %get-tuple-element.660), channel_id=1, source_target_pairs={{0,31},{1,0},{2,1},{3,2},{4,3},{5,4},{6,5},{7,6},{8,7},{9,8},{10,9... | collective-permute-start | bytes 884744 | tf_op jit(solution)/shard_map/ppermute | solution.py:19
  375.0 424.7 %reduce-scatter.7.cloned.1.call-start = ((), (), s32[]{:S(2)}) async-start(), calls=%async_computation.13 | async-start | bytes 2949120 | tf_op jit(solution)/shard_map/reduce_scatter | solution.py:389
  377.0 422.8 %reduce-scatter.9.cloned.1.call-start = ((), (), s32[]{:S(2)}) async-start(), calls=%async_computation.14 | async-start | bytes 11796480 | tf_op jit(solution)/shard_map/reduce_scatter | solution.py:389
  383.5 416.3 %reduce-scatter.11.cloned.1.call-start = ((), (), s32[]{:S(2)}) async-start(), calls=%async_computation.15 | async-start | bytes 11796480 | tf_op jit(solution)/shard_map/reduce_scatter | solution.py:389
  388.2 121.5 %collective-permute-start.3 = (f32[192,12]{0,1:T(8,128)}, f32[192,12]{0,1:T(8,128)}, u32[]{:S(2)}, u32[]{:S(2)}) collective-permute-start(f32[192,12]{0,1:T(8,128)} %reduce_sum.168), channel_id=1, source_target_pairs={{0,31},{1,0},{2,1},{3,2},{4,3},{5,4},{6,5},{7,6},{8,7},{9,8},{10,9... | collective-permute-start | bytes 27656 | tf_op jit(solution)/shard_map/ppermute | solution.py:19
  508.9 45.2 %collective-permute-start.1 = (f32[192,12]{0,1:T(8,128)S(1)}, f32[192,12]{0,1:T(8,128)S(1)}, u32[]{:S(2)}, u32[]{:S(2)}) collective-permute-start(f32[192,12]{0,1:T(8,128)S(1)} %bitcast.228), channel_id=1, source_target_pairs={{0,31},{1,0},{2,1},{3,2},{4,3},{5,4},{6,5},{7,6},{8,7},{9,8},{10,9... | collective-permute-start | bytes 27656 | tf_op jit(solution)/shard_map/ppermute | solution.py:19
  509.6 85.1 %copy-start.4 = (bf16[192,768]{0,1:T(8,128)(2,1)S(1)}, bf16[192,768]{0,1:T(8,128)(2,1)}, u32[]{:S(2)}) copy-start(bf16[192,768]{0,1:T(8,128)(2,1)} %copy.80) | copy-start | bytes 884740
  509.6 85.1 %copy-start.37 = (s32[8]{0:T(128)S(1)}, s32[8]{0:T(128)}, u32[]{:S(2)}) copy-start(s32[8]{0:T(128)} %param.22) | copy-start | bytes 100
  509.6 351.0 %reduce-scatter.5.cloned.1.call-start = ((), (), s32[]{:S(2)}) async-start(), calls=%async_computation.12 | async-start | bytes 8847360 | tf_op jit(solution)/shard_map/reduce_scatter | solution.py:389
  799.5 303.0 %all-reduce.20.cloned.1.call-start = ((), (), s32[]{:S(2)}) async-start(), calls=%async_computation.16 | async-start | bytes 14155776 | tf_op jit(solution)/shard_map/psum | solution.py:406
  868.1 46.3 %copy-start.8 = (f32[192,768]{1,0:T(8,128)S(1)}, f32[192,768]{1,0:T(8,128)}, u32[]{:S(2)}) copy-start(f32[192,768]{1,0:T(8,128)} %copy-done.7) | copy-start | bytes 1769476
  (57 other events, 266.3 us)
Sparse Core Ops, SparseCore 0:
  9.6 31.4 all-gather.12
  45.2 83.5 all-gather.14
  132.3 80.6 all-gather.16
  214.4 14.9 all-gather.18
  230.7 37.5 all-gather.20
  269.7 37.4 all-gather.22
  310.0 86.4 all-gather.24
  399.5 80.7 all-gather.26
  483.4 30.2 reduce-scatter.6
  516.3 85.0 reduce-scatter.8
  604.2 78.0 reduce-scatter.10
  799.6 60.9 reduce-scatter.4
  865.0 237.4 all-reduce.19
where the time goes:
time: 1120 us
  waiting for transfers between devices  413 us (37%)
  matrix products  339 us (30%)
  blocking collectives  153 us (14%)
  local copies, waits for them, and re-layouts  138 us (12%)
  other arithmetic  41.7 us (4%)
  between operations  17.6 us (2%)
  loops' own time  12.6 us (1%)
    psum x1, waiting for transfers between devices, per_device(): lax.psum((ordered[0], ordered[1], ordered[2], ordered[3], ordered[4], ord...  187 us
    dynamic_slice x66, local copies, waits for them, and re-layouts, in_blocks(): carry, unused = lax.scan(turn, carry, (numbers, pieces))  82.6 us
    all_gather x1, waiting for transfers between devices, per_device(): lax.all_gather(value_low, ('ctx', 'fsdp'), axis=0, tiled=True)  71.4 us
    all_gather x1, waiting for transfers between devices, per_device(): lax.all_gather(key_low, ('ctx', 'fsdp'), axis=0, tiled=True)  70.4 us
    reduce_scatter x4, waiting for transfers between devices, per_device(): lax.psum_scatter(to_scatter, 'fsdp', scatter_dimension=0, tiled=True)  60.9 us
    dot_general x6, matrix products, key_step(): jnp.einsum('hqk,qhd->khd', grad_scores, queries_split, preferred_element_...  56.3 us
    dot_general x6, matrix products, query_step(): jnp.einsum('hqk,khd->qhd', grad_scores, keys_split, preferred_element_typ...  55.5 us
    unnamed x121, local copies, waits for them, and re-layouts  44.6 us
  transfers between devices with their start and end apart: 17, of which 6 were waited for; matrix products, arithmetic and copies ran while one was open for 45% of the time, Pallas kernels for 0%

commit v1 on v0

v1 whole, which is shorter than its diff:
```python
import functools
import jax
import jax.numpy as jnp
from jax import lax
from jax.experimental import pallas as pl
from jax.experimental.pallas import tpu as pltpu
from jax.sharding import PartitionSpec as P

D = 768
H = 12
HD = 64
EPS = 1e-05
SCALE = 0.125
BRANCH = 48.0 ** (-0.5)
NEG = -1e30
SUB = 256
BF = jnp.bfloat16
F32 = jnp.float32


def mm(a, b):
    return jnp.dot(a, b, preferred_element_type=F32)


def mm_nt(a, b):
    return lax.dot_general(a, b, (((1,), (1,)), ((), ())), preferred_element_type=F32)


def mm_tn(a, b):
    return lax.dot_general(a, b, (((0,), (0,)), ((), ())), preferred_element_type=F32)


def head_lanes(head):
    return slice(0, 128) if head < 2 else slice(128, 192)


def fill_masked_columns(target, flipped):
    zero = jnp.zeros((HD, flipped.shape[1]), BF)
    target[0, 0:HD, :] = flipped[0:HD]
    target[0, HD : 2 * HD, :] = zero
    target[1, 0:HD, :] = zero
    target[1, HD : 2 * HD, :] = flipped[HD : 2 * HD]
    target[2, 0:HD, :] = flipped[2 * HD : 3 * HD]


def masked_rows(array_in, head):
    if head == 2:
        return array_in[:, 128:192]
    pair = array_in[:, 0:128]
    lane = lax.broadcasted_iota(jnp.int32, pair.shape, 1)
    return jnp.where((lane < HD) if head == 0 else (lane >= HD), pair, jnp.zeros_like(pair))


def allowed_pairs(first_key, first_query, begins, shape):
    key_places = first_key + lax.broadcasted_iota(jnp.int32, shape, 0)
    query_places = first_query + lax.broadcasted_iota(jnp.int32, shape, 1)
    return (key_places <= query_places) & (key_places >= begins)


def attend_forward_kernel(
    where_ref, rows_ref, own_ref, wq_ref, wk_ref, wv_ref, bias_ref, begins_ref,
    q_out, k_out, v_out, o_out, lse_out,
    qm, vt, peak, total, acc,
):
    turn = pl.program_id(0)
    block = own_ref.shape[0]
    mine, begin_low, begin_high = where_ref[0], where_ref[1], where_ref[2]
    first_query = mine * block
    needed = (turn <= mine) & ((turn + 1) * block - 1 >= begin_low)

    @pl.when(turn == 0)
    def _():
        query = (mm(own_ref[...], wq_ref[...]) + bias_ref[0:1, :]).astype(BF)
        q_out[...] = query
        fill_masked_columns(qm, (query.astype(F32) * SCALE).T.astype(BF))
        peak[...] = jnp.full(peak.shape, NEG, F32)
        total[...] = jnp.zeros(total.shape, F32)
        acc[...] = jnp.zeros(acc.shape, F32)

    @pl.when(needed)
    def _():
        rows = rows_ref[...]
        k_out[...] = mm(rows, wk_ref[...]).astype(BF)
        value = (mm(rows, wv_ref[...]) + bias_ref[1:2, :]).astype(BF)
        v_out[...] = value
        vt[...] = value.astype(F32).T.astype(BF)

        def one(step, masked):
            at = pl.ds(pl.multiple_of(step * SUB, SUB), SUB)
            first_key = turn * block + step * SUB
            if masked:
                allowed = allowed_pairs(first_key, first_query, begins_ref[...], (SUB, block))
            for head in range(3):
                depth = 128 if head < 2 else HD
                scores = mm(k_out[at, head_lanes(head)], qm[head, 0:depth, :])
                if masked:
                    scores = jnp.where(allowed, scores, NEG)
                old = peak[head : head + 1, :]
                new = jnp.maximum(old, jnp.max(scores, axis=0, keepdims=True))
                weights = jnp.exp(scores - new)
                if masked:
                    weights = jnp.where(allowed, weights, 0.0)
                factor = jnp.exp(old - new)
                peak[head : head + 1, :] = new
                total[head : head + 1, :] = total[head : head + 1, :] * factor + jnp.sum(
                    weights, axis=0, keepdims=True
                )
                part = slice(head * HD, head * HD + HD)
                acc[part, :] = acc[part, :] * factor + mm(vt[part, at], weights.astype(BF))

        @pl.loop(0, block // SUB)
        def _(step):
            first_key = turn * block + step * SUB
            inner = (first_key + SUB - 1 <= first_query) & (first_key >= begin_high)
            touched = first_key + SUB - 1 >= begin_low

            @pl.when(inner)
            def _():
                one(step, False)

            @pl.when(jnp.logical_not(inner) & touched)
            def _():
                one(step, True)

    @pl.when(turn == mine)
    def _():
        for head in range(3):
            part = slice(head * HD, head * HD + HD)
            o_out[part, :] = acc[part, :] / total[head : head + 1, :]
        lse_out[...] = peak[...] + jnp.log(jnp.maximum(total[...], 1e-30))


def attend_forward(where, rows_all, own, wq, wk, wv, bias, begins):
    block = own.shape[0]
    count = rows_all.shape[0] // block

    def seen(turn, where_ref):
        return (jnp.minimum(turn, where_ref[0]), 0)

    def fixed(turn, where_ref):
        return (0, 0)

    return pl.pallas_call(
        attend_forward_kernel,
        grid_spec=pltpu.PrefetchScalarGridSpec(
            num_scalar_prefetch=1,
            grid=(count,),
            in_specs=[
                pl.BlockSpec((block, D), seen),
                pl.BlockSpec((block, D), fixed),
                pl.BlockSpec((D, 192), fixed),
                pl.BlockSpec((D, 192), fixed),
                pl.BlockSpec((D, 192), fixed),
                pl.BlockSpec((2, 192), fixed),
                pl.BlockSpec((1, block), fixed),
            ],
            out_specs=[
                pl.BlockSpec((block, 192), fixed),
                pl.BlockSpec((block, 192), seen),
                pl.BlockSpec((block, 192), seen),
                pl.BlockSpec((192, block), fixed),
                pl.BlockSpec((8, block), fixed),
            ],
            scratch_shapes=[
                pltpu.VMEM((3, 128, block), BF),
                pltpu.VMEM((192, block), BF),
                pltpu.VMEM((8, block), F32),
                pltpu.VMEM((8, block), F32),
                pltpu.VMEM((192, block), F32),
            ],
        ),
        out_shape=[
            jax.ShapeDtypeStruct((block, 192), BF),
            jax.ShapeDtypeStruct((block * count, 192), BF),
            jax.ShapeDtypeStruct((block * count, 192), BF),
            jax.ShapeDtypeStruct((192, block), F32),
            jax.ShapeDtypeStruct((8, block), F32),
        ],
        compiler_params=pltpu.CompilerParams(vmem_limit_bytes=48 << 20),
        name="attend_forward",
    )(where, rows_all, own, wq, wk, wv, bias, begins)


def attend_backward_kernel(
    where_ref, rows_ref, k_ref, v_ref, own_ref, q_ref, o_ref, lse_ref, g_ref, wp_ref,
    wq_ref, wk_ref, wv_ref, begins_ref,
    dn_out, grad_out, proj_out, sums_out,
    qm, dm, qn, dn, delta, dqt, kt, dk, dv,
):
    turn = pl.program_id(0)
    block = own_ref.shape[0]
    mine, begin_low, begin_high = where_ref[0], where_ref[1], where_ref[2]
    first_query = mine * block
    needed = (turn <= mine) & ((turn + 1) * block - 1 >= begin_low)

    @pl.when(turn == 0)
    def _():
        grads = g_ref[...]
        exact = o_ref[...]
        proj_out[...] = mm(exact.astype(BF), grads)
        outer = mm_nt(grads, wp_ref[...]).astype(BF)
        flipped = outer.astype(F32).T
        product = flipped * exact
        for head in range(3):
            delta[head : head + 1, :] = jnp.sum(
                product[head * HD : head * HD + HD], axis=0, keepdims=True
            )
        fill_masked_columns(dm, flipped.astype(BF))
        scaled = (q_ref[...].astype(F32) * SCALE)
        fill_masked_columns(qm, scaled.T.astype(BF))
        scaled = scaled.astype(BF)
        for head in range(3):
            depth = 128 if head < 2 else HD
            qn[head, :, 0:depth] = masked_rows(scaled, head)
            dn[head, :, 0:depth] = masked_rows(outer, head)
        dqt[...] = jnp.zeros(dqt.shape, F32)
        grad_out[...] = jnp.zeros(grad_out.shape, F32)
        sums_out[...] = jnp.zeros(sums_out.shape, F32)

    @pl.when(jnp.logical_not(needed))
    def _():
        dn_out[...] = jnp.zeros(dn_out.shape, BF)

    @pl.when(needed)
    def _():
        kt[...] = k_ref[...].astype(F32).T.astype(BF)
        dk[...] = jnp.zeros(dk.shape, F32)
        dv[...] = jnp.zeros(dv.shape, F32)

        def one(step, masked):
            at = pl.ds(pl.multiple_of(step * SUB, SUB), SUB)
            first_key = turn * block + step * SUB
            if masked:
                allowed = allowed_pairs(first_key, first_query, begins_ref[...], (SUB, block))
            for head in range(3):
                depth = 128 if head < 2 else HD
                lanes = head_lanes(head)
                scores = mm(k_ref[at, lanes], qm[head, 0:depth, :])
                probs = jnp.exp(scores - lse_ref[head : head + 1, :])
                if masked:
                    probs = jnp.where(allowed, probs, 0.0)
                outer = mm(v_ref[at, lanes], dm[head, 0:depth, :])
                inner = (probs * (outer - delta[head : head + 1, :])).astype(BF)
                dv[at, lanes] += mm(probs.astype(BF), dn[head, :, 0:depth])
                dk[at, lanes] += mm(inner, qn[head, :, 0:depth])
                part = slice(head * HD, head * HD + HD)
                dqt[part, :] += mm(kt[part, at], inner)

        @pl.loop(0, block // SUB)
        def _(step):
            first_key = turn * block + step * SUB
            inner = (first_key + SUB - 1 <= first_query) & (first_key >= begin_high)
            touched = first_key + SUB - 1 >= begin_low

            @pl.when(inner)
            def _():
                one(step, False)

            @pl.when(jnp.logical_not(inner) & touched)
            def _():
                one(step, True)

        rows = rows_ref[...]
        low_k = dk[...].astype(BF)
        low_v = dv[...].astype(BF)
        grad_out[192:384, :] += mm(low_k.astype(F32).T.astype(BF), rows)
        grad_out[384:576, :] += mm(low_v.astype(F32).T.astype(BF), rows)
        sums_out[1:2, :] += jnp.sum(low_v.astype(F32), axis=0, keepdims=True)
        through = mm_nt(low_k, wk_ref[...]) + mm_nt(low_v, wv_ref[...])

        @pl.when(turn < mine)
        def _():
            dn_out[...] = through.astype(BF)

        @pl.when(turn == mine)
        def _():
            flipped = dqt[...] * SCALE
            low_q = flipped.T.astype(BF)
            grad_out[0:192, :] += mm(flipped.astype(BF), own_ref[...])
            sums_out[0:1, :] += jnp.sum(low_q.astype(F32), axis=0, keepdims=True)
            dn_out[...] = (through + mm_nt(low_q, wq_ref[...])).astype(BF)


def attend_backward(where, rows_all, k, v, own, q, o, lse, g, wp, wq, wk, wv, begins):
    block = own.shape[0]
    count = rows_all.shape[0] // block

    def seen(turn, where_ref):
        return (jnp.minimum(turn, where_ref[0]), 0)

    def each(turn, where_ref):
        return (turn, 0)

    def fixed(turn, where_ref):
        return (0, 0)

    return pl.pallas_call(
        attend_backward_kernel,
        grid_spec=pltpu.PrefetchScalarGridSpec(
            num_scalar_prefetch=1,
            grid=(count,),
            in_specs=[
                pl.BlockSpec((block, D), seen),
                pl.BlockSpec((block, 192), seen),
                pl.BlockSpec((block, 192), seen),
                pl.BlockSpec((block, D), fixed),
                pl.BlockSpec((block, 192), fixed),
                pl.BlockSpec((192, block), fixed),
                pl.BlockSpec((8, block), fixed),
                pl.BlockSpec((block, D), fixed),
                pl.BlockSpec((192, D), fixed),
                pl.BlockSpec((D, 192), fixed),
                pl.BlockSpec((D, 192), fixed),
                pl.BlockSpec((D, 192), fixed),
                pl.BlockSpec((1, block), fixed),
            ],
            out_specs=[
                pl.BlockSpec((block, D), each),
                pl.BlockSpec((576, D), fixed),
                pl.BlockSpec((192, D), fixed),
                pl.BlockSpec((8, 192), fixed),
            ],
            scratch_shapes=[
                pltpu.VMEM((3, 128, block), BF),
                pltpu.VMEM((3, 128, block), BF),
                pltpu.VMEM((3, block, 128), BF),
                pltpu.VMEM((3, block, 128), BF),
                pltpu.VMEM((8, block), F32),
                pltpu.VMEM((192, block), F32),
                pltpu.VMEM((192, block), BF),
                pltpu.VMEM((block, 192), F32),
                pltpu.VMEM((block, 192), F32),
            ],
        ),
        out_shape=[
            jax.ShapeDtypeStruct((block * count, D), BF),
            jax.ShapeDtypeStruct((576, D), F32),
            jax.ShapeDtypeStruct((192, D), F32),
            jax.ShapeDtypeStruct((8, 192), F32),
        ],
        compiler_params=pltpu.CompilerParams(vmem_limit_bytes=48 << 20),
        name="attend_backward",
    )(where, rows_all, k, v, own, q, o, lse, g, wp, wq, wk, wv, begins)


MESH = pl.DeviceIdType.MESH


class Place:
    def __init__(self):
        ctx = lax.axis_index("ctx")
        part = lax.axis_index("fsdp")
        self.levels = lax.axis_size("ctx") // 2
        self.ctx, self.part = ctx, part
        self.level, self.side = ctx // 2, ctx % 2
        self.half, self.core = part // 2, part % 2

    def at(self, level=None, side=None, half=None, core=None):
        level = self.level if level is None else level
        side = self.side if side is None else side
        half = self.half if half is None else half
        core = self.core if core is None else core
        return (level * 2 + side, half * 2 + core)

    @property
    def twin(self):
        return self.at(core=1 - self.core)

    @property
    def across(self):
        return self.at(half=1 - self.half)

    @property
    def corner(self):
        return self.at(half=1 - self.half, core=1 - self.core)

    @property
    def beside(self):
        return self.at(side=1 - self.side)


def remote(source, target, send, recv, device):
    return pltpu.make_async_remote_copy(
        src_ref=source, dst_ref=target, send_sem=send, recv_sem=recv, device_id=device, device_id_type=MESH
    )


def signal(sem, device):
    pl.semaphore_signal(sem, inc=1, device_id=device, device_id_type=MESH)


def piece(ref, ctx, part):
    rows = 192
    return ref.at[pl.ds(pl.multiple_of((ctx * 4 + part) * rows, rows), rows)]


def rows_of(ref, part):
    return ref.at[pl.ds(pl.multiple_of(part * 192, 192), 192)]


def layer_norm(rows_in, gain, shift):
    mean = jnp.mean(rows_in, axis=1, keepdims=True)
    centered = rows_in - mean
    inverse = lax.rsqrt(jnp.mean(centered * centered, axis=1, keepdims=True) + EPS)
    unit = centered * inverse
    return unit * gain + shift, unit, inverse


def gather_kernel(
    levels, tok_ref, vec_ref, acol_ref, ecol_ref, cot_ref,
    all_ref, attend_ref, expand_ref, gtwo_ref, vec_out,
    normed, gtwo, vec_in,
    vec_send, vec_recv, att_send, att_recv, exp_send, exp_recv, two_send, two_recv,
    x_send, x_recv, z_send, z_recv, y_send, y_recv, core_send, core_recv, local_sem,
):
    me = Place()
    mine = me.part
    barrier = pltpu.get_barrier_semaphore()
    for device in (me.twin, me.across, me.corner, me.beside):
        signal(barrier, device)

    @pl.when(me.level > 0)
    def _():
        signal(barrier, me.at(level=me.level - 1))

    @pl.when(me.level < levels - 1)
    def _():
        signal(barrier, me.at(level=me.level + 1))

    ends = (me.level == 0).astype(jnp.int32) + (me.level == levels - 1).astype(jnp.int32)
    pl.semaphore_wait(barrier, 6 - ends)

    peers = (
        (me.twin, me.half * 2 + 1 - me.core),
        (me.across, (1 - me.half) * 2 + me.core),
        (me.corner, (1 - me.half) * 2 + 1 - me.core),
    )
    vecs = [remote(vec_ref, vec_in.at[i], vec_send.at[i], vec_recv.at[i], d) for i, (d, p) in enumerate(peers)]
    for copy in vecs:
        copy.start()
    atts = [
        remote(acol_ref.at[p], rows_of(attend_ref, mine), att_send.at[i], att_recv.at[i], d)
        for i, (d, p) in enumerate(peers)
    ]
    for copy in atts:
        copy.start()
    local = [
        pltpu.make_async_copy(acol_ref.at[mine], rows_of(attend_ref, mine), local_sem.at[0]),
        pltpu.make_async_copy(ecol_ref.at[:, pl.ds(pl.multiple_of(mine * D, D), D)], rows_of(expand_ref, mine), local_sem.at[1]),
    ]
    for copy in local:
        copy.start()
    gtwo[...] = (BRANCH * cot_ref[...].astype(F32)).astype(BF)
    for copy in vecs:
        copy.wait_recv()
    vec_out[...] = vec_ref[...] + vec_in[0] + vec_in[1] + vec_in[2]
    out, unit, inverse = layer_norm(tok_ref[...].astype(F32), vec_out[4:5, :], vec_out[5:6, :])
    normed[...] = out.astype(BF)

    def go(copy):
        copy.start()
        return copy

    ctx = me.ctx
    across = go(remote(normed, piece(all_ref, ctx, mine), x_send.at[0], x_recv.at[0], me.across))
    keep = go(pltpu.make_async_copy(normed, piece(all_ref, ctx, mine), local_sem.at[2]))
    keep_two = go(pltpu.make_async_copy(gtwo, rows_of(gtwo_ref, mine), local_sem.at[3]))
    local += [keep, keep_two]

    def spread_static(source, distance, slot):
        level = me.level - distance
        where = level * 2 + me.side
        half = me.half if slot == 0 else 1 - me.half
        part = half * 2 + me.core

        @pl.when(me.level < levels - 1)
        def _():
            remote(source, piece(all_ref, where, part), z_send.at[distance, slot], z_recv.at[distance + 1, slot], me.at(level=me.level + 1)).start()

        remote(source, piece(all_ref, where, part), y_send.at[distance, slot], y_recv.at[distance, slot], me.beside).start()
        remote(source, piece(all_ref, where, part), core_send.at[distance, 0, slot], core_recv.at[distance, 0, slot], me.twin).start()

    spread_static(normed, 0, 0)
    exps = [
        go(remote(ecol_ref.at[:, pl.ds(pl.multiple_of(p * D, D), D)], rows_of(expand_ref, mine), exp_send.at[i], exp_recv.at[i], d))
        for i, (d, p) in enumerate(peers)
    ]
    two_x = go(remote(gtwo, rows_of(gtwo_ref, mine), two_send.at[0], two_recv.at[0], me.across))
    two_c = go(remote(gtwo, rows_of(gtwo_ref, mine), two_send.at[1], two_recv.at[1], me.twin))

    other = (1 - me.half) * 2 + me.core

    def held(distance, slot, side):
        half = me.half if slot == 0 else 1 - me.half
        return piece(all_ref, (me.level - distance) * 2 + side, half * 2 + me.core)

    def take_y(distance):
        for slot in range(2):
            got = held(distance, slot, 1 - me.side)
            remote(got, got, y_send.at[distance, slot], y_recv.at[distance, slot], me.beside).wait_recv()
            remote(got, got, core_send.at[distance, 1, slot], core_recv.at[distance, 1, slot], me.twin).start()

    got = piece(all_ref, ctx, other)
    remote(normed, got, x_send.at[0], x_recv.at[0], me.across).wait_recv()
    spread_static(got, 0, 1)
    for distance in range(1, levels):

        @pl.when(me.level >= distance)
        def _():
            for slot in range(2):
                got = held(distance, slot, me.side)
                remote(got, got, z_send.at[distance, slot], z_recv.at[distance, slot], me.twin).wait_recv()
                spread_static(got, distance, slot)

        if distance == 1:
            take_y(0)
        else:

            @pl.when(me.level >= distance - 1)
            def _():
                take_y(distance - 1)

    @pl.when(me.level >= levels - 1)
    def _():
        take_y(levels - 1)

    got = rows_of(gtwo_ref, other)
    remote(gtwo, got, two_send.at[0], two_recv.at[0], me.across).wait_recv()
    two_f = go(remote(got, got, two_send.at[2], two_recv.at[2], me.twin))
    for copy in local:
        copy.wait()
    for copy in vecs:
        copy.wait_send()
    for copy in atts + exps + [two_c, two_f]:
        copy.wait()
    two_x.wait_send()
    across.wait_send()
    for distance in range(levels):

        @pl.when(me.level >= distance)
        def _():
            for slot in range(2):
                got = held(distance, slot, me.side)

                @pl.when(me.level < levels - 1)
                def _():
                    remote(got, got, z_send.at[distance, slot], z_recv.at[distance, slot], me.twin).wait_send()

                remote(got, got, y_send.at[distance, slot], y_recv.at[distance, slot], me.beside).wait_send()
                for side in range(2):
                    remote(got, got, core_send.at[distance, side, slot], core_recv.at[distance, side, slot], me.twin).wait()


def gather_inputs(tokens, vectors, attend_cols, expand_weight, cotangent):
    levels = lax.axis_size("ctx") // 2
    rows = tokens.shape[0]
    block = rows * 4
    vmem = pl.BlockSpec(memory_space=pltpu.VMEM)
    anywhere = pl.BlockSpec(memory_space=pl.ANY)
    dma = pltpu.SemaphoreType.DMA
    return pl.pallas_call(
        functools.partial(gather_kernel, levels),
        in_specs=[vmem, vmem, anywhere, anywhere, vmem],
        out_specs=[anywhere, anywhere, anywhere, anywhere, vmem],
        out_shape=[
            jax.ShapeDtypeStruct((block * levels * 2, D), BF),
            jax.ShapeDtypeStruct((D, 576), BF),
            jax.ShapeDtypeStruct((D, D), BF),
            jax.ShapeDtypeStruct((block, D), BF),
            jax.ShapeDtypeStruct((8, D), F32),
        ],
        scratch_shapes=[
            pltpu.VMEM((rows, D), BF),
            pltpu.VMEM((rows, D), BF),
            pltpu.VMEM((3, 8, D), F32),
            dma((3,)), dma((3,)), dma((3,)), dma((3,)), dma((3,)), dma((3,)), dma((3,)), dma((3,)),
            dma((1,)), dma((1,)),
            dma((levels, 2)), dma((levels + 1, 2)),
            dma((levels, 2)), dma((levels, 2)),
            dma((levels, 2, 2)), dma((levels, 2, 2)),
            dma((4,)),
        ],
        compiler_params=pltpu.CompilerParams(collective_id=1, has_side_effects=True, vmem_limit_bytes=16 << 20),
        name="gather_inputs",
    )(tokens, vectors, attend_cols, expand_weight, cotangent)


def gelu_pair(t):
    slope = 0.7978845608028654
    square = t * t
    bend = jnp.tanh(slope * t * (1.0 + 0.044715 * square))
    half = 0.5 * (1.0 + bend)
    return t * half, half + 0.5 * t * (1.0 - bend * bend) * (slope * (1.0 + 0.134145 * square))


def mlp_kernel(
    o_ref, wp_ref, expand_ref, contract_ref, ebias_ref, tok_ref, cot_ref, gtwo_ref, vec_ref,
    block_out, gmid_out, gone_out, cpart_out, epart_out, sums_out,
    o_rows, gact, n2, act, gexp, held, unit,
    c_send_buf, c_recv_buf, x_send_buf, x_recv_buf,
    c_send, c_recv, x_send, x_recv, ag_send, ag_recv,
):
    me = Place()
    mine = me.part
    barrier = pltpu.get_barrier_semaphore()
    signal(barrier, me.twin)
    signal(barrier, me.across)
    pl.semaphore_wait(barrier, 2)
    p_across = (1 - me.half) * 2 + me.core
    p_twin = me.half * 2 + 1 - me.core
    p_corner = (1 - me.half) * 2 + 1 - me.core

    def part(ref, p):
        return ref[pl.ds(pl.multiple_of(p * 192, 192), 192), :]

    def to_twin(i, slot, value):
        c_send_buf[i, slot] = value.astype(BF)
        remote(c_send_buf.at[i, slot], c_recv_buf.at[i, slot], c_send.at[i, slot], c_recv.at[i, slot], me.twin).start()

    def from_twin(i, slot):
        remote(c_send_buf.at[i, slot], c_recv_buf.at[i, slot], c_send.at[i, slot], c_recv.at[i, slot], me.twin).wait_recv()
        return c_recv_buf[i, slot].astype(F32)

    def to_across(i, value):
        x_send_buf[i] = value.astype(BF)
        remote(x_send_buf.at[i], x_recv_buf.at[i], x_send.at[i], x_recv.at[i], me.across).start()

    def from_across(i):
        remote(x_send_buf.at[i], x_recv_buf.at[i], x_send.at[i], x_recv.at[i], me.across).wait_recv()
        return x_recv_buf[i].astype(F32)

    def share(i, ref):
        own = rows_of(ref, mine)
        remote(own, own, ag_send.at[i, 0], ag_recv.at[i, 0], me.across).start()
        remote(own, own, ag_send.at[i, 1], ag_recv.at[i, 1], me.twin).start()

    def share_across(i, ref):
        got = rows_of(ref, p_across)
        remote(got, got, ag_send.at[i, 0], ag_recv.at[i, 0], me.across).wait_recv()
        remote(got, got, ag_send.at[i, 2], ag_recv.at[i, 2], me.twin).start()

    def share_twin(i, ref):
        got = rows_of(ref, p_twin)
        remote(got, got, ag_send.at[i, 1], ag_recv.at[i, 1], me.twin).wait_recv()

    def share_corner(i, ref):
        got = rows_of(ref, p_corner)
        remote(got, got, ag_send.at[i, 2], ag_recv.at[i, 2], me.twin).wait_recv()

    o_rows[...] = o_ref[...].T.astype(BF)
    to_twin(0, 0, mm(part(o_rows, p_corner), wp_ref[...]))
    to_twin(0, 1, mm(part(o_rows, p_twin), wp_ref[...]))
    value = mm(part(o_rows, p_across), wp_ref[...])
    to_across(0, value + from_twin(0, 0))
    for p in range(4):
        gact[p * 192 : p * 192 + 192, :] = mm_nt(gtwo_ref[p * 192 : p * 192 + 192, :], contract_ref[...])
    value = mm(part(o_rows, mine), wp_ref[...]) + from_twin(0, 1)
    value = value + from_across(0)
    middle = tok_ref[...].astype(F32) + BRANCH * (value + vec_ref[2:3, :])
    out, unit_two, inverse = layer_norm(middle, vec_ref[6:7, :], vec_ref[7:8, :])
    n2[pl.ds(pl.multiple_of(mine * 192, 192), 192), :] = out.astype(BF)
    share(0, n2)
    unit[...] = unit_two
    held[...] = middle

    def through(p):
        at = pl.ds(pl.multiple_of(p * 192, 192), 192)
        expanded = mm(n2[at, :], expand_ref[...]) + ebias_ref[...]
        activation, slope = gelu_pair(expanded)
        act[at, :] = activation.astype(BF)
        low = (gact[at, :] * slope).astype(BF)
        gexp[at, :] = low
        return mm_nt(low, expand_ref[...])

    own_value = through(mine)
    share_twin(0, n2)
    to_twin(1, 1, through(p_twin))
    share_across(0, n2)
    across_value = through(p_across)
    share_corner(0, n2)
    to_twin(1, 0, through(p_corner))
    to_across(1, across_value + from_twin(1, 0))
    own_value = own_value + from_twin(1, 1)
    to_twin(2, 0, mm(part(act, p_corner), contract_ref[...]))
    to_twin(2, 1, mm(part(act, p_twin), contract_ref[...]))
    to_across(2, mm(part(act, p_across), contract_ref[...]) + from_twin(2, 0))
    cpart_out[...] = mm_tn(act[...], gtwo_ref[...]).astype(BF)
    grad = own_value + from_across(1)
    unit_two = unit[...]
    scaled = grad * vec_ref[6:7, :]
    spread = (
        scaled
        - jnp.mean(scaled, axis=1, keepdims=True)
        - unit_two * jnp.mean(scaled * unit_two, axis=1, keepdims=True)
    )
    grad_middle = cot_ref[...].astype(F32) + inverse * spread
    gmid_out[...] = grad_middle
    low = (BRANCH * grad_middle).astype(BF)
    gone_out[pl.ds(pl.multiple_of(mine * 192, 192), 192), :] = low
    share(1, gone_out)
    sums_out[0:1, :] = jnp.sum(low.astype(F32), axis=0, keepdims=True)
    sums_out[1:2, :] = jnp.sum(part(gtwo_ref, mine).astype(F32), axis=0, keepdims=True)
    sums_out[2:3, :] = jnp.sum(grad * unit_two, axis=0, keepdims=True)
    sums_out[3:4, :] = jnp.sum(grad, axis=0, keepdims=True)
    sums_out[4:5, :] = jnp.sum(gexp[...].astype(F32), axis=0, keepdims=True)
    sums_out[5:8, :] = jnp.zeros((3, D), F32)
    epart_out[...] = mm_tn(n2[...], gexp[...]).astype(BF)
    value = mm(part(act, mine), contract_ref[...]) + from_twin(2, 1)
    value = value + from_across(2)
    block_out[...] = (held[...] + BRANCH * (value + vec_ref[3:4, :])).astype(BF)
    share_across(1, gone_out)
    share_twin(1, gone_out)
    share_corner(1, gone_out)
    for i in range(3):
        for slot in range(2):
            remote(c_send_buf.at[i, slot], c_recv_buf.at[i, slot], c_send.at[i, slot], c_recv.at[i, slot], me.twin).wait_send()
        remote(x_send_buf.at[i], x_recv_buf.at[i], x_send.at[i], x_recv.at[i], me.across).wait_send()
    for i, ref in ((0, n2), (1, gone_out)):
        own = rows_of(ref, mine)
        for j in range(3):
            remote(own, own, ag_send.at[i, j], ag_recv.at[i, j], me.twin).wait_send()


def feed_forward(o, wp, expand, contract, ebias, tokens, cotangent, gtwo, vectors):
    rows = tokens.shape[0]
    block = rows * 4
    vmem = pl.BlockSpec(memory_space=pltpu.VMEM)
    dma = pltpu.SemaphoreType.DMA
    return pl.pallas_call(
        mlp_kernel,
        in_specs=[vmem] * 9,
        out_specs=[vmem] * 6,
        out_shape=[
            jax.ShapeDtypeStruct((rows, D), BF),
            jax.ShapeDtypeStruct((rows, D), F32),
            jax.ShapeDtypeStruct((block, D), BF),
            jax.ShapeDtypeStruct((D, D), BF),
            jax.ShapeDtypeStruct((D, D), BF),
            jax.ShapeDtypeStruct((8, D), F32),
        ],
        scratch_shapes=[
            pltpu.VMEM((block, 192), BF),
            pltpu.VMEM((block, D), F32),
            pltpu.VMEM((block, D), BF),
            pltpu.VMEM((block, D), BF),
            pltpu.VMEM((block, D), BF),
            pltpu.VMEM((rows, D), F32),
            pltpu.VMEM((rows, D), F32),
            pltpu.VMEM((3, 2, rows, D), BF),
            pltpu.VMEM((3, 2, rows, D), BF),
            pltpu.VMEM((3, rows, D), BF),
            pltpu.VMEM((3, rows, D), BF),
            dma((3, 2)), dma((3, 2)), dma((3,)), dma((3,)), dma((2, 3)), dma((2, 3)),
        ],
        compiler_params=pltpu.CompilerParams(collective_id=2, has_side_effects=True, vmem_limit_bytes=48 << 20),
        name="feed_forward",
    )(o, wp, expand, contract, ebias, tokens, cotangent, gtwo, vectors)


def normalize(rows_in, gain, shift):
    mean = jnp.mean(rows_in, axis=1, keepdims=True)
    centered = rows_in - mean
    inverse = lax.rsqrt(jnp.mean(centered * centered, axis=1, keepdims=True) + EPS)
    unit = centered * inverse
    return (unit * gain + shift, unit, inverse)


def normalize_back(incoming, unit, inverse, gain):
    scaled = incoming * gain
    spread = (
        scaled
        - jnp.mean(scaled, axis=1, keepdims=True)
        - unit * jnp.mean(scaled * unit, axis=1, keepdims=True)
    )
    return (inverse * spread, jnp.sum(incoming * unit, axis=0), jnp.sum(incoming, axis=0))


def first_position(places, starts):
    below = starts[None, :] <= places[:, None]
    return jnp.max(jnp.where(below, starts[None, :], 0), axis=1)


def per_device(
    tokens, document_starts, attend_weight, attend_bias, project_weight, project_bias,
    expand_weight, expand_bias, contract_weight, contract_bias,
    gain_first, shift_first, gain_second, shift_second, cotangent,
):
    both = ("ctx", "fsdp")
    rows = tokens.shape[0]
    ways = lax.axis_size("fsdp")
    block = rows * ways
    ctx = lax.axis_index("ctx")
    part = lax.axis_index("fsdp")

    def whole(array_in):
        return lax.all_gather(array_in, "fsdp", axis=0, tiled=True)

    own_vectors = jnp.stack([project_bias, contract_bias, gain_first, shift_first, gain_second, shift_second])
    vectors = lax.dynamic_update_slice(jnp.zeros((6, D), F32), own_vectors.astype(F32), (0, part * rows))
    biases = lax.dynamic_update_slice(jnp.zeros((2 * D,), F32), attend_bias.astype(F32), (part * 2 * rows,))
    vectors = jnp.concatenate([biases.reshape(2, D), vectors])
    attend_cols = attend_weight.reshape(rows, 3, ways, 192).transpose(2, 0, 1, 3).reshape(ways, rows, 576)
    normed_all, attend_cols, expand_cols, g2, vectors = gather_inputs(
        tokens, vectors, attend_cols, expand_weight, cotangent
    )
    project_b, contract_b, gain_one, shift_one, gain_two, shift_two = [vectors[i] for i in range(2, 8)]
    wq, wk, wv = attend_cols[:, :192], attend_cols[:, 192:384], attend_cols[:, 384:]
    bias = lax.dynamic_slice(vectors, (0, part * 192), (2, 192))

    hidden_in = tokens.astype(F32)
    normed, unit_one, inverse_one = normalize(hidden_in, gain_one, shift_one)
    own = lax.dynamic_slice(normed_all, (ctx * block, 0), (block, D))
    places = ctx * block + jnp.arange(block, dtype=jnp.int32)
    begins = first_position(places, document_starts)
    where = jnp.stack([ctx, begins[0], begins[-1]]).astype(jnp.int32)
    begins_row = begins.reshape(1, block)
    q, k, v, o, lse = attend_forward(where, normed_all, own, wq, wk, wv, bias, begins_row)
    block_output, grad_middle, g1, contract_part, expand_part, mlp_sums = feed_forward(
        o, project_weight, expand_cols, contract_weight, expand_bias.astype(F32).reshape(1, D), tokens, cotangent, g2, vectors
    )
    dn, attend_t, project_part, sums = attend_backward(
        where, normed_all, k, v, own, q, o, lse, g1, project_weight, wq, wk, wv, begins_row
    )
    grad_normed = lax.psum_scatter(dn.astype(F32), both, scatter_dimension=0, tiled=True)
    first_part, gainone_grad, shiftone_grad = normalize_back(grad_normed, unit_one, inverse_one, gain_one)
    tokens_grad = grad_middle + first_part

    def summed(array_in):
        return lax.psum(array_in.astype(BF), "ctx").astype(F32)

    contract_grad = summed(contract_part)
    project_grad = summed(project_part)
    expand_grad = lax.all_to_all(summed(expand_part).reshape(ways, rows, D), "fsdp", 0, 0)
    expand_grad = expand_grad.transpose(1, 0, 2).reshape(rows, ways * D)
    attend_grad = lax.all_to_all(summed(attend_t.T).reshape(ways, rows, 576), "fsdp", 0, 0)
    attend_grad = attend_grad.reshape(ways, rows, 3, 192).transpose(1, 2, 0, 3).reshape(rows, 3 * D)
    expbias_grad = lax.psum(mlp_sums[4], "ctx")
    spread = jnp.zeros((2, D), F32)
    spread = lax.dynamic_update_slice(spread, sums[:2], (0, part * 192))
    vectors = jnp.concatenate([
        spread.reshape(-1),
        mlp_sums[0], mlp_sums[1], gainone_grad, shiftone_grad, mlp_sums[2], mlp_sums[3],
    ])
    vectors = lax.psum(vectors, both)

    def mine_of(start, length):
        return lax.dynamic_slice(vectors, (start + part * (length // ways),), (length // ways,))

    return (
        block_output.astype(BF), tokens_grad.astype(BF),
        attend_grad, mine_of(0, 2 * D), project_grad, mine_of(2 * D, D), expand_grad, expbias_grad,
        contract_grad, mine_of(3 * D, D), mine_of(4 * D, D), mine_of(5 * D, D), mine_of(6 * D, D), mine_of(7 * D, D),
    )


def solution(mesh):
    tok, row, vec = P(("ctx", "fsdp"), None), P("fsdp", None), P("fsdp")
    in_specs = (tok, P(), row, vec, row, vec, row, vec, row, vec, vec, vec, vec, vec, tok)
    out_specs = (tok, tok, row, vec, row, vec, row, vec, row, vec, vec, vec, vec, vec)
    return jax.shard_map(per_device, mesh=mesh, in_specs=in_specs, out_specs=out_specs, check_vma=False)
```

time: 1120 us -> 552 us (0.49)
  matrix products: 339 us -> 0 us
  waiting for transfers between devices: 413 us -> 277 us
  Pallas kernels: 0 us -> 119 us
  local copies, waits for them, and re-layouts: 138 us -> 38.9 us
  blocking collectives: 153 us -> 58.5 us
  other arithmetic: 41.7 us -> 27.5 us
  loops' own time: 12.6 us -> 0 us
    dot_general x54 -> x0, matrix products: 339 us -> none  [the longest x6 56.3 us: key_step(): jnp.einsum('hqk,qhd->khd', grad_scores, queries_split, preferred_element_...]
    all_gather x8 -> x0, waiting for transfers between devices: 148 us -> none  [the longest x1 71.4 us: per_device(): lax.all_gather(value_low, ('ctx', 'fsdp'), axis=0, tiled=True)]
    pallas_call x0 -> x4, Pallas kernels: none -> 119 us  [the longest x1 49.6 us: feed_forward(): pl.pallas_call(mlp_kernel, in_specs=[vmem] * 9, out_specs=[vmem] * 6, out...]
    all_gather x4 -> x0, blocking collectives: 97.8 us -> none  [the longest x1 43.2 us: per_device(): lax.all_gather(next_side[3], ('ctx', 'fsdp'), axis=0, tiled=True)]
    dynamic_slice x66 -> x4, local copies, waits for them, and re-layouts: 82.6 us -> 2.73 us  [the longest x1 1.35 us: per_device(): own = lax.dynamic_slice(normed_all, (ctx * block, 0), (block, D))]
    psum x1, waiting for transfers between devices: 187 us -> 250 us  [summed(): return lax.psum(array_in.astype(BF), 'ctx').astype(F32)]
    reduce_scatter x4 -> x1, waiting for transfers between devices: 60.9 us -> 0.01 us  [per_device(): lax.psum_scatter(dn.astype(F32), both, scatter_dimension=0, tiled=True)]
    unnamed x121 -> x29, local copies, waits for them, and re-layouts: 44.6 us -> 8.1 us
  transfers between devices with their start and end apart: 17 -> 4, of which waited for: 6 -> 2; matrix products, arithmetic and copies ran while one was open for 45% -> 6% of each run, Pallas kernels for 0% -> 0%
where the time goes in v1:
time: 552 us; the launch traced here: 548 us
  waiting for transfers between devices  277 us (50%)
  Pallas kernels  119 us (22%)
  blocking collectives  58.5 us (11%)
  local copies, waits for them, and re-layouts  38.9 us (7%)
  other arithmetic  27.5 us (5%)
  between operations  15.7 us (3%)
  starting transfers between devices  11.9 us (2%)
    psum x1, waiting for transfers between devices, summed(): return lax.psum(array_in.astype(BF), 'ctx').astype(F32)  250 us
    pallas_call x1, Pallas kernels, feed_forward(): pl.pallas_call(mlp_kernel, in_specs=[vmem] * 9, out_specs=[vmem] * 6, out...  49.6 us
    pallas_call x1, Pallas kernels, gather_inputs(): pl.pallas_call(functools.partial(gather_kernel, levels), in_specs=[vmem,...  42.5 us
    psum x1, blocking collectives, per_device(): vectors = lax.psum(vectors, both)  40.3 us
    all_to_all x1, waiting for transfers between devices, per_device(): lax.all_to_all(summed(attend_t.T).reshape(ways, rows, 576), 'fsdp', 0, 0)  27.4 us
    psum x1, blocking collectives, per_device(): expbias_grad = lax.psum(mlp_sums[4], 'ctx')  18.2 us
    pallas_call x1, Pallas kernels, attend_backward(): pl.pallas_call(attend_backward_kernel, grid_spec=pltpu.PrefetchScalarGrid...  16.3 us
    convert_element_type x1, other arithmetic, per_device(): dn.astype(F32)  11.7 us
  transfers between devices with their start and end apart: 4, of which 2 were waited for; matrix products, arithmetic and copies ran while one was open for 6% of the time, Pallas kernels for 0%

profile of v1, /device:TPU:3, one launch (start us, length us, event | category | flops | bytes accessed | tf_op | source)
XLA Modules:
  0.0 548.4 jit_solution(3049176375530227257)
XLA Ops:
  14.2 3.7 reshape.95
  17.9 2.6 copy.48
  22.8 42.5 %gather_inputs.1 = (bf16[6144,768]{1,0:T(8,128)(2,1)S(1)}, bf16[768,576]{1,0:T(8,128)(2,1)S(1)}, bf16[768,768]{1,0:T(8,128)(2,1)S(1)}, bf16[768,768]{1,0:T(8,128)(2,1)S(1)}, f32[8,768]{1,0:T(8,128)S(1)}) custom-call(bf16[192,768]{1,0:T(8,128)(2,1)S(1)} %copy-done.1, f32[8,768]{1,0:T(8,128)S(1)} %pad_maximum_fusion.vec_ref, ...), custom_call_target="tpu_custom_call" | custom-call | tf_op jit(solution)/shard_map/gather_inputs/pallas_call | solution.py:561
  65.3 3.6 copy-done
  74.4 10.4 %attend_forward.1 = (bf16[768,192]{1,0:T(8,128)(2,1)S(1)}, bf16[6144,192]{1,0:T(8,128)(2,1)}, bf16[6144,192]{1,0:T(8,128)(2,1)}, f32[192,768]{1,0:T(8,128)S(1)}, f32[8,768]{1,0:T(8,128)S(1)}) custom-call(s32[3]{0:T(128)S(1)} %pad_add_fusion.where_ref, bf16[6144,768]{1,0:T(8,128)(2,1)} %copy-done, bf16[768,768]{1,0:T(8,128)(2,1)S(1)} %constant_dynamic-slice_fusion.1.own_ref, ...), custom_call_target="tpu_custom_call" | custom-call | tf_op jit(solution)/shard_map/attend_forward/pallas_call | solution.py:143
  84.7 49.6 %feed_forward.1 = (bf16[192,768]{1,0:T(8,128)(2,1)S(1)}, f32[192,768]{1,0:T(8,128)S(1)}, bf16[768,768]{1,0:T(8,128)(2,1)S(1)}, bf16[768,768]{1,0:T(8,128)(2,1)},...) custom-call(f32[192,768]{1,0:T(8,128)S(1)} %get-tuple-element.37.o_ref, bf16[192,768]{1,0:T(8,128)(2,1)S(1)} %copy-done.6, ...), custom_call_target="tpu_custom_call" | custom-call | tf_op jit(solution)/shard_map/feed_forward/pallas_call | solution.py:729
  134.4 16.3 %attend_backward.1 = (bf16[6144,768]{1,0:T(8,128)(2,1)}, f32[576,768]{1,0:T(8,128)}, f32[192,768]{1,0:T(8,128)S(1)}, f32[8,192]{1,0:T(8,128)S(1)}) custom-call(s32[3]{0:T(128)S(1)} %pad_add_fusion.where_ref, bf16[6144,768]{1,0:T(8,128)(2,1)} %copy-done, bf16[6144,192]{1,0:T(8,128)(2,1)} %get-tuple-element.42.k_ref, ...), custom_call_target="tpu_custom_call" | custom-call | tf_op jit(solution)/shard_map/attend_backward/pallas_call | solution.py:297
  150.7 1.6 convert_bitcast_fusion
  154.4 11.7 %convert_element_type.36 = f32[6144,768]{1,0:T(8,128)} convert(bf16[6144,768]{1,0:T(8,128)(2,1)} %get-tuple-element.47) | non-fusion elementwise | flops 4718592 | bytes 28311552 | tf_op jit(solution)/shard_map/convert_element_type | solution.py:824
  166.1 249.5 %all-reduce.3.cloned.1.call-done = (bf16[4,192,576]{2,1,0:T(8,128)(2,1)}, bf16[192,768]{1,0:T(8,128)(2,1)}, bf16[4,192,768]{2,1,0:T(8,128)(2,1)}, bf16[768,768]{1,0:T(8,128)(2,1)}) async-done(((bf16[4,192,576]{2,1,0:T(8,128)(2,1)}, bf16[192,768]{1,0:T(8,128)(2,1)}, bf16[4,192,768]{2,1,0:T(8,128)(2,1)}, bf16[768,768]{1,0:T(8,128)(2,1)}), (bf16[4,192,576]{2,1,0:T(8,128)(2,1)}, bf16[192,768]{1,0:T(8,128)(2,1)}, ...) | async-done | bytes 3538960 | tf_op jit(solution)/shard_map/psum | solution.py:829
  415.6 2.6 reshape.101
  418.2 5.6 %all-to-all-start = ((f32[4,192,576]{2,1,0:T(8,128)}), f32[4,192,576]{2,1,0:T(8,128)}, u32[]{:S(2)}, u32[]{:S(2)}) async-start(f32[4,192,576]{2,1,0:T(8,128)} %reshape.101), calls=%async_computation.1 | async-start | bytes 3932160 | tf_op jit(solution)/shard_map/all_to_all | solution.py:835
  423.8 1.6 reshape.106
  425.4 27.4 %all-to-all-done = f32[4,192,576]{2,1,0:T(8,128)} async-done(((f32[4,192,576]{2,1,0:T(8,128)}), f32[4,192,576]{2,1,0:T(8,128)}, u32[]{:S(2)}, u32[]{:S(2)}) %all-to-all-start) | async-done | bytes 1769504 | tf_op jit(solution)/shard_map/all_to_all | solution.py:835
  452.9 6.3 %all-to-all-start.1 = ((f32[4,192,768]{2,1,0:T(8,128)}), f32[4,192,768]{2,1,0:T(8,128)}, u32[]{:S(2)}, u32[]{:S(2)}) async-start(f32[4,192,768]{2,1,0:T(8,128)} %reshape.106), calls=%async_computation.2 | async-start | bytes 4718592 | tf_op jit(solution)/shard_map/all_to_all | solution.py:833
  459.4 18.2 %psum.46 = f32[768]{0:T(1024)} all-reduce(f32[768]{0:T(1024)S(1)} %get-tuple-element.58), channel_id=1, replica_groups=mesh['ctx'=8,'fsdp'=4] {'ctx'}, use_global_device_ids=true, to_apply=%region_12.13 | all-reduce | flops 768 | bytes 6144 | tf_op jit(solution)/shard_map/psum | solution.py:837
  478.1 1.6 convert_element_type.42
  480.5 3.0 copy.51
  483.5 4.5 copy.52
  488.0 3.7 reshape.103
  491.6 3.4 copy.54
  495.0 1.4 fusion.10
  496.5 40.3 %psum.43 = f32[6144]{0:T(1024)S(1)} all-reduce(f32[6144]{0:T(1024)S(1)} %constant_dynamic-update-slice_fusion), channel_id=1, replica_groups=mesh['ctx'=8,'fsdp'=4] {'ctx','fsdp'}, use_global_device_ids=true, to_apply=%region_9.10 | all-reduce | flops 6144 | bytes 49152 | tf_op jit(solution)/shard_map/psum | solution.py:844
  538.2 2.0 fusion.9
  (76 shorter events, 19.6 us)
Async XLA Ops:
  8.0 407.6 %all-reduce.3.cloned.1.call-start = ((), (), s32[]{:S(2)}) async-start(), calls=%async_computation.4 | async-start | bytes 7274496 | tf_op jit(solution)/shard_map/psum | solution.py:829
  17.9 3.6 copy-start.1
  17.9 3.6 copy-start.4
  21.5 1.3 copy-start.5
  65.3 3.6 copy-start
  68.9 1.0 copy-start.2
  69.9 1.0 copy-start.3
  70.9 0.7 copy-start.10
  74.4 10.4 %copy-start.6 = (bf16[192,768]{1,0:T(8,128)(2,1)S(1)}, bf16[192,768]{1,0:T(8,128)(2,1)}, u32[]{:S(2)}) copy-start(bf16[192,768]{1,0:T(8,128)(2,1)} %wp_ref.3) | copy-start | bytes 884740
  154.3 340.7 %reduce-scatter.2.cloned.1.call-start = ((), (), s32[]{:S(2)}) async-start(), calls=%async_computation.3 | async-start | bytes 19464192 | tf_op jit(solution)/shard_map/reduce_scatter | solution.py:824
  418.2 5.6 %copy-start.8 = (bf16[4,192,768]{2,1,0:T(8,128)(2,1)S(1)}, bf16[4,192,768]{2,1,0:T(8,128)(2,1)}, u32[]{:S(2)}) copy-start(bf16[4,192,768]{2,1,0:T(8,128)(2,1)} %get-tuple-element.65) | copy-start | bytes 3538948
  418.2 34.6 %all-to-all-start = ((f32[4,192,576]{2,1,0:T(8,128)}), f32[4,192,576]{2,1,0:T(8,128)}, u32[]{:S(2)}, u32[]{:S(2)}) async-start(f32[4,192,576]{2,1,0:T(8,128)} %reshape.101), calls=%async_computation.1 | async-start | bytes 3932160 | tf_op jit(solution)/shard_map/all_to_all | solution.py:835
  425.4 52.6 %copy-start.7 = (bf16[768,768]{1,0:T(8,128)(2,1)S(1)}, bf16[768,768]{1,0:T(8,128)(2,1)}, u32[]{:S(2)}) copy-start(bf16[768,768]{1,0:T(8,128)(2,1)} %get-tuple-element.66) | copy-start | bytes 3538948
  452.9 38.8 %all-to-all-start.1 = ((f32[4,192,768]{2,1,0:T(8,128)}), f32[4,192,768]{2,1,0:T(8,128)}, u32[]{:S(2)}, u32[]{:S(2)}) async-start(f32[4,192,768]{2,1,0:T(8,128)} %reshape.106), calls=%async_computation.2 | async-start | bytes 4718592 | tf_op jit(solution)/shard_map/all_to_all | solution.py:833
  478.1 1.6 copy-start.9
Sparse Core Ops, SparseCore 0:
  154.4 261.1 all-reduce.2
Sparse Core Ops, SparseCore 1:
  166.2 323.6 reduce-scatter.1

commit v2 on v1

--- a/solution.py
+++ b/solution.py
@@ -757,6 +757,501 @@
     )(o, wp, expand, contract, ebias, tokens, cotangent, gtwo, vectors)
 
 
+def reduce_kernel(
+    levels, dn_ref, c_ref, e_ref, a_ref, p_ref, tok_ref, gmid_ref, vec_ref, sums_ref,
+    tg_out, cg_out, eg_out, ag_out, pg_out, vec_out,
+    far, near, keep, x_out, x_in, y_out, y_in, d_out, d_in,
+    yc, ye, ya, yp, zc_out, ze_out, za_out, zp_out, zc_in, ze_in, za_in, zp_in, v_out, v_in, e_move, a_move,
+    far_send, far_recv, near_sem, x_send, x_recv, y_send, y_recv, d_send, d_recv,
+    gy_send, gy_recv, gz_send, gz_recv, m_send, m_recv, u_send, u_recv, w_send, w_recv, b_send, b_recv, t_send, t_recv,
+    v_send, v_recv,
+):
+    me = Place()
+    z, side, mine = me.level, me.side, me.part
+    top = levels - 1
+    barrier = pltpu.get_barrier_semaphore()
+    for device in (me.twin, me.across, me.corner, me.beside):
+        signal(barrier, device)
+    for step in range(1, levels):
+        signal(barrier, me.at(level=(z + step) % levels))
+    pl.semaphore_wait(barrier, levels + 3)
+    below, above = me.at(level=z - 1), me.at(level=z + 1)
+
+    def corner_of(ref, level, across):
+        return ref.at[pl.ds(pl.multiple_of(level * 48, 48), 48), pl.ds(pl.multiple_of(across * 384, 128), 384)]
+
+    grads_y = ((c_ref, yc), (e_ref, ye), (a_ref, ya))
+
+    def grad_y(level, act):
+        for i, (own, got) in enumerate(grads_y):
+            act(remote(own.at[level * 2 + 1 - side], got.at[level], gy_send.at[level, i], gy_recv.at[level, i], me.beside))
+        act(remote(corner_of(p_ref, level, 1 - side), yp.at[level], gy_send.at[level, 3], gy_recv.at[level, 3], me.beside))
+
+    start = lambda copy: copy.start()
+    wait_recv = lambda copy: copy.wait_recv()
+    wait_send = lambda copy: copy.wait_send()
+
+    def each_step(step, act):
+        down = step - (top - z)
+        up = top - (step - z)
+
+        @pl.when((down >= 0) & (down < z))
+        def _():
+            act(down, 0)
+
+        @pl.when((up <= top) & (up > z))
+        def _():
+            act(up, 1)
+
+    for step in range(levels - 1):
+        each_step(step, lambda level, way: grad_y(level, start))
+    grad_y(z, start)
+
+    def dn_piece(level, across, half, core):
+        return dn_ref.at[(level * 2 + across) * 4 + half * 2 + core]
+
+    for level in range(levels):
+
+        @pl.when(level <= z)
+        def _():
+            for across in range(2):
+                for half in range(2):
+                    remote(
+                        dn_piece(level, across, half, 1 - me.core), far.at[level, across, half],
+                        far_send.at[level, across, half], far_recv.at[level, across, half], me.twin,
+                    ).start()
+                    pltpu.make_async_copy(
+                        dn_piece(level, across, half, me.core), near.at[level, across, half], near_sem.at[level, across, half]
+                    ).start()
+
+    for level in range(levels):
+
+        @pl.when(level <= z)
+        def _():
+            for across in range(2):
+                for half in range(2):
+                    remote(
+                        dn_piece(level, across, half, me.core), far.at[level, across, half],
+                        far_send.at[level, across, half], far_recv.at[level, across, half], me.twin,
+                    ).wait_recv()
+                    pltpu.make_async_copy(
+                        dn_piece(level, across, half, me.core), near.at[level, across, half], near_sem.at[level, across, half]
+                    ).wait()
+                other = 1 - me.half
+                x_out[level, across] = (
+                    near[level, across, other].astype(F32) + far[level, across, other].astype(F32)
+                ).astype(BF)
+                remote(
+                    x_out.at[level, across], x_in.at[level, across], x_send.at[level, across], x_recv.at[level, across], me.across
+                ).start()
+                keep[level, across] = near[level, across, me.half].astype(F32) + far[level, across, me.half].astype(F32)
+
+    def dn_across(level):
+        def take(across):
+            remote(
+                x_out.at[level, across], x_in.at[level, across], x_send.at[level, across], x_recv.at[level, across], me.across
+            ).wait_recv()
+            return keep[level, across] + x_in[level, across].astype(F32)
+
+        y_out[level] = take(1 - side).astype(BF)
+        remote(y_out.at[level], y_in.at[level], y_send.at[level], y_recv.at[level], me.beside).start()
+        keep[level, side] = take(side)
+
+    def dn_sum(level):
+        remote(y_out.at[level], y_in.at[level], y_send.at[level], y_recv.at[level], me.beside).wait_recv()
+        return keep[level, side] + y_in[level].astype(F32)
+
+    def dn_down(level):
+        return remote(d_out.at[level], d_in.at[level], d_send.at[level], d_recv.at[level], below)
+
+    def dn_step(step):
+        level = step - (top - z)
+
+        @pl.when((level >= 0) & (level < z))
+        def _():
+            keep[level, side] = dn_sum(level)
+
+            @pl.when(z < top)
+            def _():
+                dn_down(level).wait_recv()
+                keep[level, side] += d_in[level].astype(F32)
+
+            d_out[level] = keep[level, side].astype(BF)
+            dn_down(level).start()
+
+    grads_z = ((c_ref, yc, zc_out, zc_in), (e_ref, ye, ze_out, ze_in), (a_ref, ya, za_out, za_in))
+
+    def grad_z(level, way, act):
+        device = below if way == 0 else above
+        for i, (own, got, out, come) in enumerate(grads_z):
+            act(remote(out.at[level], come.at[way, level], gz_send.at[level, i], gz_recv.at[way, level, i], device))
+        act(remote(zp_out.at[level], zp_in.at[way, level], gz_send.at[level, 3], gz_recv.at[way, level, 3], device))
+
+    def own_corner(level):
+        return p_ref[pl.ds(pl.multiple_of(level * 48, 48), 48), pl.ds(pl.multiple_of(side * 384, 128), 384)]
+
+    def grad_step(step):
+        def act(level, way):
+            grad_y(level, wait_recv)
+            inner = (z < top) if way == 0 else (z > 0)
+
+            @pl.when(inner)
+            def _():
+                grad_z(level, way, wait_recv)
+                for own, got, out, come in grads_z:
+                    out[level] = (
+                        own[level * 2 + side].astype(F32) + got[level].astype(F32) + come[way, level].astype(F32)
+                    ).astype(BF)
+                zp_out[level] = (own_corner(level).astype(F32) + yp[level].astype(F32) + zp_in[way, level].astype(F32)).astype(BF)
+
+            @pl.when(jnp.logical_not(inner))
+            def _():
+                for own, got, out, come in grads_z:
+                    out[level] = (own[level * 2 + side].astype(F32) + got[level].astype(F32)).astype(BF)
+                zp_out[level] = (own_corner(level).astype(F32) + yp[level].astype(F32)).astype(BF)
+
+            grad_z(level, way, start)
+
+        each_step(step, act)
+
+    def done_c(level, across):
+        return cg_out.at[level * 2 + across]
+
+    def done_p(level, across):
+        return corner_of(pg_out, level, across)
+
+    def up_copies(distance):
+        level = z - distance
+        return (
+            remote(done_c(level, side), done_c(level, side), u_send.at[0, distance, 0], u_recv.at[0, distance, 0], above),
+            remote(done_p(level, side), done_p(level, side), u_send.at[0, distance, 1], u_recv.at[0, distance, 1], above),
+        )
+
+    def down_copies(distance):
+        level = z + distance
+        return (
+            remote(done_c(level, side), done_c(level, side), u_send.at[1, distance, 0], u_recv.at[1, distance, 0], below),
+            remote(done_p(level, side), done_p(level, side), u_send.at[1, distance, 1], u_recv.at[1, distance, 1], below),
+        )
+
+    def side_copies(level):
+        return (
+            remote(done_c(level, side), done_c(level, side), w_send.at[level, 0], w_recv.at[level, 0], me.beside),
+            remote(done_p(level, side), done_p(level, side), w_send.at[level, 1], w_recv.at[level, 1], me.beside),
+        )
+
+    def side_takes(level):
+        other = 1 - side
+        return (
+            remote(done_c(level, other), done_c(level, other), w_send.at[level, 0], w_recv.at[level, 0], me.beside),
+            remote(done_p(level, other), done_p(level, other), w_send.at[level, 1], w_recv.at[level, 1], me.beside),
+        )
+
+    keeper = (z // 2, z % 2)
+
+    def move_copies():
+        device = me.at(half=z // 2, core=z % 2)
+        return (
+            remote(e_move, eg_out.at[side, mine], m_send.at[0], m_recv.at[mine, 0], device),
+            remote(a_move, ag_out.at[side, mine], m_send.at[1], m_recv.at[mine, 1], device),
+        )
+
+    def move_takes(origin):
+        return (
+            remote(eg_out.at[side, origin], eg_out.at[side, origin], m_send.at[0], m_recv.at[origin, 0], me.twin),
+            remote(ag_out.at[side, origin], ag_out.at[side, origin], m_send.at[1], m_recv.at[origin, 1], me.twin),
+        )
+
+    def row_copies(way):
+        device = below if way == 0 else above
+        return (
+            remote(eg_out.at[side], eg_out.at[side], b_send.at[way, 0], b_recv.at[way, 0], device),
+            remote(ag_out.at[side], ag_out.at[side], b_send.at[way, 1], b_recv.at[way, 1], device),
+        )
+
+    def row_side(across):
+        return (
+            remote(eg_out.at[across], eg_out.at[across], t_send.at[0], t_recv.at[0], me.beside),
+            remote(ag_out.at[across], ag_out.at[across], t_send.at[1], t_recv.at[1], me.beside),
+        )
+
+    def all_of(copies, act):
+        for copy in copies:
+            act(copy)
+
+    def grad_final():
+        grad_y(z, wait_recv)
+        kept = (cg_out.at[z * 2 + side], e_move, a_move)
+
+        def add(ways):
+            for (own, got, out, come), target in zip(grads_z, kept):
+                total = own[z * 2 + side].astype(F32) + got[z].astype(F32)
+                for way in ways:
+                    total = total + come[way, z].astype(F32)
+                target[...] = total.astype(BF)
+            total = own_corner(z).astype(F32) + yp[z].astype(F32)
+            for way in ways:
+                total = total + zp_in[way, z].astype(F32)
+            done_p(z, side)[...] = total.astype(BF)
+
+        @pl.when(z < top)
+        def _():
+            grad_z(z, 0, wait_recv)
+
+        @pl.when(z > 0)
+        def _():
+            grad_z(z, 1, wait_recv)
+
+        @pl.when(z == 0)
+        def _():
+            add((0,))
+
+        @pl.when(z == top)
+        def _():
+            add((1,))
+
+        @pl.when((z > 0) & (z < top))
+        def _():
+            add((0, 1))
+
+        @pl.when(mine != z)
+        def _():
+            all_of(move_copies(), start)
+
+        @pl.when(mine == z)
+        def _():
+            eg_out[side, mine] = e_move[...]
+            ag_out[side, mine] = a_move[...]
+
+        pass_on(0, 0)
+
+    def pass_on(distance, way):
+        if way in (0, 1):
+
+            @pl.when(z < top)
+            def _():
+                all_of(up_copies(distance), start)
+
+        if way in (0, 2):
+
+            @pl.when(z > 0)
+            def _():
+                all_of(down_copies(distance), start)
+
+        all_of(side_copies(z if way == 0 else z - distance if way == 1 else z + distance), start)
+
+    def spread_rows():
+        @pl.when(mine == z)
+        def _():
+            for origin in range(4):
+
+                @pl.when(origin != mine)
+                def _():
+                    all_of(move_takes(origin), wait_recv)
+
+        @pl.when(mine > z)
+        def _():
+            all_of(row_copies(0), wait_recv)
+
+        @pl.when(mine < z)
+        def _():
+            all_of(row_copies(1), wait_recv)
+
+        @pl.when((mine >= z) & (z > 0))
+        def _():
+            all_of(row_copies(0), start)
+
+        @pl.when((mine <= z) & (z < top))
+        def _():
+            all_of(row_copies(1), start)
+
+        all_of(row_side(side), start)
+
+    for step in range(levels + 1):
+        if step < levels - 1:
+            grad_step(step)
+        elif step == levels - 1:
+            grad_final()
+        if step < levels:
+
+            @pl.when(step <= z)
+            def _():
+                dn_across(step)
+
+        if step >= 1:
+            dn_step(step - 1)
+
+    spread_rows()
+
+    def arrivals(distance):
+        @pl.when(z - distance >= 0)
+        def _():
+            level = z - distance
+            all_of(
+                (
+                    remote(done_c(level, side), done_c(level, side), u_send.at[0, distance - 1, 0], u_recv.at[0, distance - 1, 0], me.twin),
+                    remote(done_p(level, side), done_p(level, side), u_send.at[0, distance - 1, 1], u_recv.at[0, distance - 1, 1], me.twin),
+                ),
+                wait_recv,
+            )
+            pass_on(distance, 1)
+
+        @pl.when(z + distance <= top)
+        def _():
+            level = z + distance
+            all_of(
+                (
+                    remote(done_c(level, side), done_c(level, side), u_send.at[1, distance - 1, 0], u_recv.at[1, distance - 1, 0], me.twin),
+                    remote(done_p(level, side), done_p(level, side), u_send.at[1, distance - 1, 1], u_recv.at[1, distance - 1, 1], me.twin),
+                ),
+                wait_recv,
+            )
+            pass_on(distance, 2)
+
+    arrivals(1)
+
+    grad = dn_sum(z)
+
+    @pl.when(z < top)
+    def _():
+        dn_down(z).wait_recv()
+
+    keep[0, 0] = grad
+
+    @pl.when(z < top)
+    def _():
+        keep[0, 0] += d_in[z].astype(F32)
+
+    grad = keep[0, 0]
+    gain = vec_ref[4:5, :]
+    out, unit, inverse = layer_norm(tok_ref[...].astype(F32), gain, vec_ref[5:6, :])
+    scaled = grad * gain
+    spread = (
+        scaled - jnp.mean(scaled, axis=1, keepdims=True) - unit * jnp.mean(scaled * unit, axis=1, keepdims=True)
+    )
+    tg_out[...] = (gmid_ref[...] + inverse * spread).astype(BF)
+    v_out[0] = sums_ref[...]
+    v_out[0, 4:5, :] = jnp.sum(grad * unit, axis=0, keepdims=True)
+    v_out[0, 5:6, :] = jnp.sum(grad, axis=0, keepdims=True)
+
+    for i, device in enumerate((me.twin, me.across, me.beside)):
+        copy = remote(v_out.at[i], v_in.at[i], v_send.at[i], v_recv.at[i], device)
+        copy.start()
+        copy.wait_recv()
+        v_out[i + 1] = v_out[i] + v_in[i]
+    v_in[3 + z] = v_out[3]
+    for step in range(1, levels):
+        remote(v_out.at[3], v_in.at[3 + z], v_send.at[2 + step], v_recv.at[3 + z], me.at(level=(z + step) % levels)).start()
+
+    for distance in range(2, levels):
+        arrivals(distance)
+    for step in range(1, levels):
+        level = (z + step) % levels
+        remote(v_out.at[3], v_in.at[3 + level], v_send.at[2 + step], v_recv.at[3 + level], me.twin).wait_recv()
+    total = v_in[3]
+    for level in range(1, levels):
+        total = total + v_in[3 + level]
+    vec_out[...] = total
+
+    for level in range(levels):
+        all_of(side_takes(level), wait_recv)
+    all_of(row_side(1 - side), wait_recv)
+    for level in range(levels):
+        grad_y(level, wait_send)
+
+        @pl.when(level != z)
+        def _():
+            for i, (own, got, out, come) in enumerate(grads_z):
+                remote(out.at[level], come.at[0, level], gz_send.at[level, i], gz_recv.at[0, level, i], me.twin).wait_send()
+            remote(zp_out.at[level], zp_in.at[0, level], gz_send.at[level, 3], gz_recv.at[0, level, 3], me.twin).wait_send()
+
+        all_of(side_copies(level), wait_send)
+
+        @pl.when(level <= z)
+        def _():
+            for across in range(2):
+                for half in range(2):
+                    remote(
+                        dn_piece(level, across, half, me.core), far.at[level, across, half],
+                        far_send.at[level, across, half], far_recv.at[level, across, half], me.twin,
+                    ).wait_send()
+                remote(
+                    x_out.at[level, across], x_in.at[level, across], x_send.at[level, across], x_recv.at[level, across], me.across
+                ).wait_send()
+            remote(y_out.at[level], y_in.at[level], y_send.at[level], y_recv.at[level], me.beside).wait_send()
+
+        @pl.when(level < z)
+        def _():
+            dn_down(level).wait_send()
+
+    for distance in range(levels):
+
+        @pl.when((z - distance >= 0) & (z < top))
+        def _():
+            all_of(up_copies(distance), wait_send)
+
+        @pl.when((z + distance <= top) & (z > 0))
+        def _():
+            all_of(down_copies(distance), wait_send)
+
+    @pl.when(mine != z)
+    def _():
+        all_of(move_copies(), wait_send)
+
+    @pl.when((mine >= z) & (z > 0))
+    def _():
+        all_of(row_copies(0), wait_send)
+
+    @pl.when((mine <= z) & (z < top))
+    def _():
+        all_of(row_copies(1), wait_send)
+
+    all_of(row_side(side), wait_send)
+    for i in range(2 + levels):
+        remote(v_out.at[0], v_in.at[0], v_send.at[i], v_recv.at[0], me.twin).wait_send()
+
+
+def reduce_all(dn, contract, expand, attend, project, tokens, grad_middle, vectors, sums):
+    levels = lax.axis_size("ctx") // 2
+    rows = tokens.shape[0]
+    vmem = pl.BlockSpec(memory_space=pltpu.VMEM)
+    anywhere = pl.BlockSpec(memory_space=pl.ANY)
+    dma = pltpu.SemaphoreType.DMA
+    n = levels
+
+    def buf(*shape):
+        return pltpu.VMEM(shape, BF)
+
+    return pl.pallas_call(
+        functools.partial(reduce_kernel, levels),
+        in_specs=[anywhere] + [vmem] * 8,
+        out_specs=[vmem] * 6,
+        out_shape=[
+            jax.ShapeDtypeStruct((rows, D), BF),
+            jax.ShapeDtypeStruct((2 * n, 96, D), BF),
+            jax.ShapeDtypeStruct((2, 4, 96, D), BF),
+            jax.ShapeDtypeStruct((2, 4, 96, 576), BF),
+            jax.ShapeDtypeStruct((192, D), BF),
+            jax.ShapeDtypeStruct((16, D), F32),
+        ],
+        scratch_shapes=[
+            buf(n, 2, 2, rows, D), buf(n, 2, 2, rows, D), pltpu.VMEM((n, 2, rows, D), F32),
+            buf(n, 2, rows, D), buf(n, 2, rows, D), buf(n, rows, D), buf(n, rows, D), buf(n, rows, D), buf(n, rows, D),
+            buf(n, 96, D), buf(n, 96, D), buf(n, 96, 576), buf(n, 48, 384),
+            buf(n, 96, D), buf(n, 96, D), buf(n, 96, 576), buf(n, 48, 384),
+            buf(2, n, 96, D), buf(2, n, 96, D), buf(2, n, 96, 576), buf(2, n, 48, 384),
+            pltpu.VMEM((4, 16, D), F32), pltpu.VMEM((3 + n, 16, D), F32), buf(96, D), buf(96, 576),
+            dma((n, 2, 2)), dma((n, 2, 2)), dma((n, 2, 2)), dma((n, 2)), dma((n, 2)), dma((n,)), dma((n,)), dma((n,)), dma((n,)),
+            dma((n, 4)), dma((n, 4)), dma((n, 4)), dma((2, n, 4)),
+            dma((2,)), dma((4, 2)), dma((2, n, 2)), dma((2, n, 2)), dma((n, 2)), dma((n, 2)),
+            dma((2, 2)), dma((2, 2)), dma((2,)), dma((2,)),
+            dma((2 + n,)), dma((3 + n,)),
+        ],
+        compiler_params=pltpu.CompilerParams(collective_id=3, has_side_effects=True, vmem_limit_bytes=56 << 20),
+        name="reduce_all",
+    )(dn, contract, expand, attend, project, tokens, grad_middle, vectors, sums)
+
+
 def normalize(rows_in, gain, shift):
     mean = jnp.mean(rows_in, axis=1, keepdims=True)
     centered = rows_in - mean
@@ -778,6 +1273,54 @@
 def first_position(places, starts):
     below = starts[None, :] <= places[:, None]
     return jnp.max(jnp.where(below, starts[None, :], 0), axis=1)
+
+
+def combine_plain(dn, contract_part, expand_part, attend_part, project_part, tokens, grad_middle, gain_one, mlp_sums, sums):
+    both = ("ctx", "fsdp")
+    rows = tokens.shape[0]
+    ways = lax.axis_size("fsdp")
+    part = lax.axis_index("fsdp")
+    grad_normed = lax.psum_scatter(dn.astype(F32), both, scatter_dimension=0, tiled=True)
+    shift = jnp.zeros_like(gain_one)
+    normed, unit_one, inverse_one = normalize(tokens.astype(F32), gain_one, shift)
+    first_part, gainone_grad, shiftone_grad = normalize_back(grad_normed, unit_one, inverse_one, gain_one)
+    tokens_grad = (grad_middle + first_part).astype(BF)
+
+    def summed(array_in):
+        return lax.psum(array_in.astype(BF), "ctx").astype(F32)
+
+    contract_grad = summed(contract_part)
+    project_grad = summed(project_part)
+    expand_grad = lax.all_to_all(summed(expand_part).reshape(ways, rows, D), "fsdp", 0, 0)
+    expand_grad = expand_grad.transpose(1, 0, 2).reshape(rows, ways * D)
+    attend_grad = lax.all_to_all(summed(attend_part).reshape(ways, rows, 576), "fsdp", 0, 0)
+    attend_grad = attend_grad.reshape(ways, rows, 3, 192).transpose(1, 2, 0, 3).reshape(rows, 3 * D)
+    spread = lax.dynamic_update_slice(jnp.zeros((2, D), F32), sums[:2], (0, part * 192))
+    hidden = lax.dynamic_update_slice(jnp.zeros((4, D), F32), mlp_sums[4:5], (part, 0))
+    vectors = jnp.concatenate([
+        spread, mlp_sums[0:2], gainone_grad[None], shiftone_grad[None], mlp_sums[2:4], hidden, jnp.zeros((4, D), F32)
+    ])
+    return tokens_grad, contract_grad, expand_grad, attend_grad, project_grad, lax.psum(vectors, both)
+
+
+def combine(dn, contract_part, expand_part, attend_part, project_part, tokens, grad_middle, vectors, mlp_sums, sums):
+    rows = tokens.shape[0]
+    ways = lax.axis_size("fsdp")
+    part = lax.axis_index("fsdp")
+    if lax.axis_size("ctx") != 8:
+        return combine_plain(
+            dn, contract_part, expand_part, attend_part, project_part, tokens, grad_middle, vectors[4], mlp_sums, sums
+        )
+    spread = lax.dynamic_update_slice(jnp.zeros((2, D), F32), sums[:2], (0, part * 192))
+    hidden = lax.dynamic_update_slice(jnp.zeros((4, D), F32), mlp_sums[4:5], (part, 0))
+    local = jnp.concatenate([spread, mlp_sums[0:2], jnp.zeros((2, D), F32), mlp_sums[2:4], hidden, jnp.zeros((4, D), F32)])
+    tokens_grad, c, e, a, p, totals = reduce_all(
+        dn.reshape(-1, rows, D), contract_part.reshape(8, 96, D), expand_part.reshape(8, 96, D),
+        attend_part.astype(BF).reshape(8, 96, 576), project_part.astype(BF), tokens, grad_middle, vectors, local,
+    )
+    expand_grad = e.transpose(0, 2, 1, 3).reshape(rows, ways * D).astype(F32)
+    attend_grad = a.reshape(2, ways, 96, 3, 192).transpose(0, 2, 3, 1, 4).reshape(rows, 3 * D).astype(F32)
+    return tokens_grad, c.reshape(D, D).astype(F32), expand_grad, attend_grad, p.astype(F32), totals
 
 
 def per_device(
@@ -807,8 +1350,6 @@
     wq, wk, wv = attend_cols[:, :192], attend_cols[:, 192:384], attend_cols[:, 384:]
     bias = lax.dynamic_slice(vectors, (0, part * 192), (2, 192))
 
-    hidden_in = tokens.astype(F32)
-    normed, unit_one, inverse_one = normalize(hidden_in, gain_one, shift_one)
     own = lax.dynamic_slice(normed_all, (ctx * block, 0), (block, D))
     places = ctx * block + jnp.arange(block, dtype=jnp.int32)
     begins = first_position(places, document_starts)
@@ -821,35 +1362,15 @@
     dn, attend_t, project_part, sums = attend_backward(
         where, normed_all, k, v, own, q, o, lse, g1, project_weight, wq, wk, wv, begins_row
     )
-    grad_normed = lax.psum_scatter(dn.astype(F32), both, scatter_dimension=0, tiled=True)
-    first_part, gainone_grad, shiftone_grad = normalize_back(grad_normed, unit_one, inverse_one, gain_one)
-    tokens_grad = grad_middle + first_part
-
-    def summed(array_in):
-        return lax.psum(array_in.astype(BF), "ctx").astype(F32)
-
-    contract_grad = summed(contract_part)
-    project_grad = summed(project_part)
-    expand_grad = lax.all_to_all(summed(expand_part).reshape(ways, rows, D), "fsdp", 0, 0)
-    expand_grad = expand_grad.transpose(1, 0, 2).reshape(rows, ways * D)
-    attend_grad = lax.all_to_all(summed(attend_t.T).reshape(ways, rows, 576), "fsdp", 0, 0)
-    attend_grad = attend_grad.reshape(ways, rows, 3, 192).transpose(1, 2, 0, 3).reshape(rows, 3 * D)
-    expbias_grad = lax.psum(mlp_sums[4], "ctx")
-    spread = jnp.zeros((2, D), F32)
-    spread = lax.dynamic_update_slice(spread, sums[:2], (0, part * 192))
-    vectors = jnp.concatenate([
-        spread.reshape(-1),
-        mlp_sums[0], mlp_sums[1], gainone_grad, shiftone_grad, mlp_sums[2], mlp_sums[3],
-    ])
-    vectors = lax.psum(vectors, both)
-
-    def mine_of(start, length):
-        return lax.dynamic_slice(vectors, (start + part * (length // ways),), (length // ways,))
-
+    tokens_grad, contract_grad, expand_grad, attend_grad, project_grad, totals = combine(
+        dn, contract_part, expand_part, attend_t.T, project_part, tokens, grad_middle, vectors, mlp_sums, sums
+    )
+    attbias = lax.dynamic_slice(totals[:2].reshape(-1), (part * 2 * rows,), (2 * rows,))
+    mine = lax.dynamic_slice(totals, (2, part * rows), (6, rows))
+    expbias = lax.dynamic_slice(totals, (8 + part, 0), (1, D)).reshape(D)
     return (
-        block_output.astype(BF), tokens_grad.astype(BF),
-        attend_grad, mine_of(0, 2 * D), project_grad, mine_of(2 * D, D), expand_grad, expbias_grad,
-        contract_grad, mine_of(3 * D, D), mine_of(4 * D, D), mine_of(5 * D, D), mine_of(6 * D, D), mine_of(7 * D, D),
+        block_output, tokens_grad, attend_grad, attbias, project_grad, mine[0], expand_grad, expbias,
+        contract_grad, mine[1], mine[2], mine[3], mine[4], mine[5],
     )
 
 

time: 552 us -> 422 us (0.76)
  waiting for transfers between devices: 277 us -> 0 us
  Pallas kernels: 119 us -> 363 us
  blocking collectives: 58.5 us -> 0 us
  other arithmetic: 27.5 us -> 8.55 us
  between operations: 15.7 us -> 1.38 us
  starting transfers between devices: 11.9 us -> 0 us
    psum x1 -> x0, waiting for transfers between devices: 250 us -> none  [summed(): return lax.psum(array_in.astype(BF), 'ctx').astype(F32)]
    pallas_call x0 -> x1, Pallas kernels: none -> 245 us  [reduce_all(): pl.pallas_call(functools.partial(reduce_kernel, levels), in_specs=[anywhe...]
    psum x2 -> x0, blocking collectives: 58.5 us -> none  [the longest x1 40.3 us: per_device(): vectors = lax.psum(vectors, both)]
    all_to_all x2 -> x0, waiting for transfers between devices: 27.4 us -> none  [the longest x1 27.4 us: per_device(): lax.all_to_all(summed(attend_t.T).reshape(ways, rows, 576), 'fsdp', 0, 0)]
    convert_element_type x6 -> x5, other arithmetic: 18.5 us -> 6.29 us  [the longest x1 1.65 us: combine(): c.reshape(D, D).astype(F32)]
    all_to_all x2 -> x0, starting transfers between devices: 11.8 us -> none  [the longest x1 6.27 us: per_device(): lax.all_to_all(summed(expand_part).reshape(ways, rows, D), 'fsdp', 0, 0)]
    convert_element_type x1 -> x5, local copies, waits for them, and re-layouts: 1.32 us -> 10.7 us  [the longest x3 7.84 us: combine(): a.reshape(2, ways, 96, 3, 192).transpose(0, 2, 3, 1, 4).reshape(rows, 3 * D)]
    reshape x3 -> x1, local copies, waits for them, and re-layouts: 7.06 us -> 0.01 us  [per_device(): totals[:2].reshape(-1)]
  transfers between devices with their start and end apart: 4 -> 0, of which waited for: 2 -> 0; matrix products, arithmetic and copies ran while one was open for 6% -> 0% of each run, Pallas kernels for 0% -> 0%
where the time goes in v2:
time: 422 us; the launch traced here: 415 us
  Pallas kernels  363 us (86%)
  local copies, waits for them, and re-layouts  42.6 us (10%)
  other arithmetic  8.55 us (2%)
    pallas_call x1, Pallas kernels, reduce_all(): pl.pallas_call(functools.partial(reduce_kernel, levels), in_specs=[anywhe...  245 us
    pallas_call x1, Pallas kernels, feed_forward(): pl.pallas_call(mlp_kernel, in_specs=[vmem] * 9, out_specs=[vmem] * 6, out...  48.1 us
    pallas_call x1, Pallas kernels, gather_inputs(): pl.pallas_call(functools.partial(gather_kernel, levels), in_specs=[vmem,...  42.5 us
    pallas_call x1, Pallas kernels, attend_backward(): pl.pallas_call(attend_backward_kernel, grid_spec=pltpu.PrefetchScalarGrid...  16.2 us
    unnamed x35, local copies, waits for them, and re-layouts  12.7 us
    pallas_call x1, Pallas kernels, attend_forward(): pl.pallas_call(attend_forward_kernel, grid_spec=pltpu.PrefetchScalarGridS...  10.5 us

profile of v2, /device:TPU:3, one launch (start us, length us, event | category | flops | bytes accessed | tf_op | source)
XLA Modules:
  0.0 415.2 jit_solution(5692189451037247162)
XLA Ops:
  5.8 2.9 reshape.81
  8.7 2.2 copy.43
  10.8 1.6 copy.44.acol_ref
  12.5 1.3 copy-done.7
  13.8 42.5 %gather_inputs.1 = (bf16[6144,768]{1,0:T(8,128)(2,1)S(1)}, bf16[768,576]{1,0:T(8,128)(2,1)S(1)}, bf16[768,768]{1,0:T(8,128)(2,1)S(1)}, bf16[768,768]{1,0:T(8,128)(2,1)S(1)}, f32[8,768]{1,0:T(8,128)S(1)}) custom-call(bf16[192,768]{1,0:T(8,128)(2,1)S(1)} %copy-done.1, f32[8,768]{1,0:T(8,128)S(1)} %pad_maximum_fusion.vec_ref, ...), custom_call_target="tpu_custom_call" | custom-call | tf_op jit(solution)/shard_map/gather_inputs/pallas_call | solution.py:561
  56.3 3.7 copy-done
  62.1 1.3 constant_dynamic-slice_fusion.1.own_ref
  64.8 1.4 pad_add_fusion.where_ref
  66.1 10.5 %attend_forward.1 = (bf16[768,192]{1,0:T(8,128)(2,1)S(1)}, bf16[6144,192]{1,0:T(8,128)(2,1)}, bf16[6144,192]{1,0:T(8,128)(2,1)}, f32[192,768]{1,0:T(8,128)S(1)}, f32[8,768]{1,0:T(8,128)S(1)}) custom-call(s32[3]{0:T(128)S(1)} %pad_add_fusion.where_ref, bf16[6144,768]{1,0:T(8,128)(2,1)} %copy-done, bf16[768,768]{1,0:T(8,128)(2,1)S(1)} %constant_dynamic-slice_fusion.1.own_ref, ...), custom_call_target="tpu_custom_call" | custom-call | tf_op jit(solution)/shard_map/attend_forward/pallas_call | solution.py:143
  76.7 48.1 %feed_forward.1 = (bf16[192,768]{1,0:T(8,128)(2,1)S(1)}, f32[192,768]{1,0:T(8,128)S(1)}, bf16[768,768]{1,0:T(8,128)(2,1)S(1)}, bf16[768,768]{1,0:T(8,128)(2,1)S(...) custom-call(f32[192,768]{1,0:T(8,128)S(1)} %get-tuple-element.43.o_ref, bf16[192,768]{1,0:T(8,128)(2,1)S(1)} %copy-done.8, ...), custom_call_target="tpu_custom_call" | custom-call | tf_op jit(solution)/shard_map/feed_forward/pallas_call | solution.py:729
  126.9 16.2 %attend_backward.1 = (bf16[6144,768]{1,0:T(8,128)(2,1)}, f32[576,768]{1,0:T(8,128)}, f32[192,768]{1,0:T(8,128)S(1)}, f32[8,192]{1,0:T(8,128)S(1)}) custom-call(s32[3]{0:T(128)S(1)} %pad_add_fusion.where_ref, bf16[6144,768]{1,0:T(8,128)(2,1)} %copy-done, bf16[6144,192]{1,0:T(8,128)(2,1)} %get-tuple-element.47.k_ref, ...), custom_call_target="tpu_custom_call" | custom-call | tf_op jit(solution)/shard_map/attend_backward/pallas_call | solution.py:297
  143.5 1.3 concatenate.7.sums_ref
  144.7 1.6 convert_bitcast_fusion.1
  146.3 1.3 copy.45
  148.4 245.3 %reduce_all.1 = (bf16[192,768]{1,0:T(8,128)(2,1)}, bf16[8,96,768]{2,1,0:T(8,128)(2,1)}, bf16[2,4,96,768]{3,2,1,0:T(8,128)(2,1)}, bf16[2,4,96,576]{3,2,1,0:T(8,12...) custom-call(bf16[32,192,768]{2,1,0:T(8,128)(2,1)} %bitcast.29, bf16[8,96,768]{2,1,0:T(8,128)(2,1)} %bitcast.27, ...), custom_call_target="tpu_custom_call" | custom-call | tf_op jit(solution)/shard_map/reduce_all/pallas_call | solution.py:1225
  393.7 1.5 convert_bitcast_fusion
  395.2 1.5 copy.48
  396.7 1.8 copy.49
  398.5 1.5 copy.46
  400.1 2.5 copy.47
  402.6 3.8 reshape.94
  406.4 1.7 bitcast_convert_fusion
  410.3 1.7 fusion.1
  412.0 1.3 dynamic-slice_reduce_fusion
  (67 shorter events, 15.4 us)
Async XLA Ops:
  8.7 3.8 copy-start.1
  8.7 3.8 copy-start.6
  12.5 1.3 copy-start.7
  56.3 3.7 copy-start
  60.0 1.0 copy-start.4
  61.0 1.0 copy-start.5
  62.0 14.7 %copy-start.10 = (f32[8,768]{1,0:T(8,128)}, f32[8,768]{1,0:T(8,128)S(1)}, u32[]{:S(2)}) copy-start(f32[8,768]{1,0:T(8,128)S(1)} %get-tuple-element.42.vec_ref) | copy-start | bytes 73732
  63.4 0.7 copy-start.15
  66.1 10.5 %copy-start.14 = (bf16[768]{0:T(1024)(128)(2,1)S(1)}, bf16[768]{0:T(1024)(128)(2,1)}, u32[]{:S(2)}) copy-start(bf16[768]{0:T(1024)(128)(2,1)} %param.22) | copy-start | bytes 4612
  66.1 10.6 %copy-start.8 = (bf16[192,768]{1,0:T(8,128)(2,1)S(1)}, bf16[192,768]{1,0:T(8,128)(2,1)}, u32[]{:S(2)}) copy-start(bf16[192,768]{1,0:T(8,128)(2,1)} %wp_ref.3) | copy-start | bytes 884740
  124.8 1.0 copy-start.2
  125.9 1.0 copy-start.3
  126.9 16.2 %copy-start.9 = (f32[192,768]{1,0:T(8,128)}, f32[192,768]{1,0:T(8,128)S(1)}, u32[]{:S(2)}) copy-start(f32[192,768]{1,0:T(8,128)S(1)} %get-tuple-element.57.gmid_ref) | copy-start | bytes 1769476
  402.6 3.8 copy-start.11
  406.4 1.7 copy-start.12
  406.4 7.7 %copy-start.13 = (bf16[192,768]{1,0:T(8,128)(2,1)S(1)}, bf16[192,768]{1,0:T(8,128)(2,1)}, u32[]{:S(2)}) copy-start(bf16[192,768]{1,0:T(8,128)(2,1)} %get-tuple-element.94) | copy-start | bytes 884740

commit v3 on v1

--- a/solution.py
+++ b/solution.py
@@ -13,7 +13,11 @@
 SCALE = 0.125
 BRANCH = 48.0 ** (-0.5)
 NEG = -1e30
-SUB = 256
+SUB = 768
+STRIP = 256
+QS = STRIP
+LEAD = 4
+BACK_LEAD = 2
 BF = jnp.bfloat16
 F32 = jnp.float32
 
@@ -90,23 +94,32 @@
             first_key = turn * block + step * SUB
             if masked:
                 allowed = allowed_pairs(first_key, first_query, begins_ref[...], (SUB, block))
-            for head in range(3):
+            strips = [(head, strip) for head in range(3) for strip in range(block // QS)]
+
+            def scored(head, strip):
                 depth = 128 if head < 2 else HD
-                scores = mm(k_out[at, head_lanes(head)], qm[head, 0:depth, :])
+                return mm(k_out[at, head_lanes(head)], qm[head, 0:depth, strip * QS : strip * QS + QS])
+
+            ahead = [scored(*strips[i]) for i in range(LEAD)]
+            for i, (head, strip) in enumerate(strips):
+                scores = ahead.pop(0)
+                if i + LEAD < len(strips):
+                    ahead.append(scored(*strips[i + LEAD]))
+                lanes = slice(strip * QS, strip * QS + QS)
                 if masked:
-                    scores = jnp.where(allowed, scores, NEG)
-                old = peak[head : head + 1, :]
+                    scores = jnp.where(allowed[:, lanes], scores, NEG)
+                old = peak[head : head + 1, lanes]
                 new = jnp.maximum(old, jnp.max(scores, axis=0, keepdims=True))
                 weights = jnp.exp(scores - new)
                 if masked:
-                    weights = jnp.where(allowed, weights, 0.0)
+                    weights = jnp.where(allowed[:, lanes], weights, 0.0)
                 factor = jnp.exp(old - new)
-                peak[head : head + 1, :] = new
-                total[head : head + 1, :] = total[head : head + 1, :] * factor + jnp.sum(
+                peak[head : head + 1, lanes] = new
+                total[head : head + 1, lanes] = total[head : head + 1, lanes] * factor + jnp.sum(
                     weights, axis=0, keepdims=True
                 )
                 part = slice(head * HD, head * HD + HD)
-                acc[part, :] = acc[part, :] * factor + mm(vt[part, at], weights.astype(BF))
+                acc[part, lanes] = acc[part, lanes] * factor + mm(vt[part, at], weights.astype(BF))
 
         @pl.loop(0, block // SUB)
         def _(step):
@@ -585,6 +598,274 @@
     )(tokens, vectors, attend_cols, expand_weight, cotangent)
 
 
+def begins_of(starts_ref, first, count):
+    places = first + lax.broadcasted_iota(jnp.int32, (1, count), 1)
+    begins = jnp.zeros((1, count), jnp.int32)
+    for document in range(8):
+        start = starts_ref[document]
+        begins = jnp.where(places >= start, jnp.maximum(begins, start), begins)
+    return begins
+
+
+def gather_attend_kernel(
+    levels, starts_ref, tok_ref, vec_ref, aw_ref, ew_ref, cot_ref,
+    all_ref, attend_ref, expand_ref, gtwo_ref, vec_out, q_out, k_out, v_out, o_out, lse_out,
+    staged, vec_in, begins, qm, vt, acc, peak, total,
+    vec_send, vec_recv, att_send, att_recv, exp_send, exp_recv, two_send, two_recv,
+    x_send, x_recv, z_send, z_recv, y_send, y_recv, core_send, core_recv, local_sem,
+):
+    me = Place()
+    mine, z, side = me.part, me.level, me.side
+    top = levels - 1
+    block = gtwo_ref.shape[0]
+    barrier = pltpu.get_barrier_semaphore()
+    for device in (me.twin, me.across, me.corner, me.beside):
+        signal(barrier, device)
+
+    @pl.when(z > 0)
+    def _():
+        signal(barrier, me.at(level=z - 1))
+
+    @pl.when(z < top)
+    def _():
+        signal(barrier, me.at(level=z + 1))
+
+    for part in range(4):
+        for kind in range(3):
+            staged[part, :, kind * 192 : kind * 192 + 192] = aw_ref[:, kind * D + part * 192 : kind * D + part * 192 + 192]
+    ends = (z == 0).astype(jnp.int32) + (z == top).astype(jnp.int32)
+    pl.semaphore_wait(barrier, 6 - ends)
+
+    peers = (
+        (me.twin, me.half * 2 + 1 - me.core),
+        (me.across, (1 - me.half) * 2 + me.core),
+        (me.corner, (1 - me.half) * 2 + 1 - me.core),
+    )
+
+    def go(copy):
+        copy.start()
+        return copy
+
+    vecs = [go(remote(vec_ref, vec_in.at[mine], vec_send.at[i], vec_recv.at[i], d)) for i, (d, p) in enumerate(peers)]
+    atts = [
+        go(remote(staged.at[p], rows_of(attend_ref, mine), att_send.at[i], att_recv.at[i], d))
+        for i, (d, p) in enumerate(peers)
+    ]
+    vec_in[mine] = vec_ref[...]
+    rows_of(attend_ref, mine)[...] = staged[mine]
+    local = [
+        go(pltpu.make_async_copy(
+            ew_ref.at[:, pl.ds(pl.multiple_of(mine * D, D), D)], rows_of(expand_ref, mine), local_sem.at[0]
+        ))
+    ]
+    own_two = rows_of(gtwo_ref, mine)
+    own_two[...] = (BRANCH * cot_ref[...].astype(F32)).astype(BF)
+    for i, (d, p) in enumerate(peers):
+        remote(vec_ref, vec_in.at[p], vec_send.at[i], vec_recv.at[i], d).wait_recv()
+    for part in range(4):
+        vec_out[:, part * 192 : part * 192 + 192] = vec_in[part]
+    out, unit, inverse = layer_norm(tok_ref[...].astype(F32), vec_out[4:5, :], vec_out[5:6, :])
+    own_rows = piece(all_ref, me.ctx, mine)
+    own_rows[...] = out.astype(BF)
+    across = go(remote(own_rows, own_rows, x_send.at[0], x_recv.at[0], me.across))
+
+    def spread(distance, slot):
+        half = me.half if slot == 0 else 1 - me.half
+        got = piece(all_ref, (z - distance) * 2 + side, half * 2 + me.core)
+
+        @pl.when(z < top)
+        def _():
+            remote(got, got, z_send.at[distance, slot], z_recv.at[distance + 1, slot], me.at(level=z + 1)).start()
+
+        remote(got, got, y_send.at[distance, slot], y_recv.at[distance, slot], me.beside).start()
+        remote(got, got, core_send.at[distance, 0, slot], core_recv.at[distance, 0, slot], me.twin).start()
+
+    def held(distance, slot, where):
+        half = me.half if slot == 0 else 1 - me.half
+        return piece(all_ref, (z - distance) * 2 + where, half * 2 + me.core)
+
+    def from_twin(distance, which, where):
+        for slot in range(2):
+            half = me.half if slot == 0 else 1 - me.half
+            got = piece(all_ref, (z - distance) * 2 + where, half * 2 + 1 - me.core)
+            remote(got, got, core_send.at[distance, which, slot], core_recv.at[distance, which, slot], me.twin).wait_recv()
+
+    spread(0, 0)
+    two_x = go(remote(own_two, own_two, two_send.at[0], two_recv.at[0], me.across))
+    two_c = go(remote(own_two, own_two, two_send.at[1], two_recv.at[1], me.twin))
+    exps = [
+        go(remote(ew_ref.at[:, pl.ds(pl.multiple_of(p * D, D), D)], rows_of(expand_ref, mine), exp_send.at[i], exp_recv.at[i], d))
+        for i, (d, p) in enumerate(peers)
+    ]
+    begins[...] = begins_of(starts_ref, me.ctx * block, block)
+    got = held(0, 1, side)
+    remote(got, got, x_send.at[0], x_recv.at[0], me.across).wait_recv()
+    spread(0, 1)
+    for copy in atts:
+        copy.wait_recv()
+    from_twin(0, 0, side)
+
+    first_query = me.ctx * block
+    bias_q = vec_in[mine // 2, pl.ds(mine % 2, 1), :]
+    query = (mm(all_ref[pl.ds(pl.multiple_of(first_query, block), block), :], attend_ref[:, 0:192]) + bias_q).astype(BF)
+    q_out[...] = query
+    fill_masked_columns(qm, (query.astype(F32) * SCALE).T.astype(BF))
+    peak[...] = jnp.full(peak.shape, NEG, F32)
+    total[...] = jnp.zeros(total.shape, F32)
+    acc[...] = jnp.zeros(acc.shape, F32)
+
+    def attend(ctx, diagonal):
+        first_key = ctx * block
+        at = pl.ds(pl.multiple_of(first_key, block), block)
+        rows = all_ref[at, :]
+        key = mm(rows, attend_ref[:, 192:384]).astype(BF)
+        k_out[at, :] = key
+        value = (mm(rows, attend_ref[:, 384:576]) + vec_in[2 + mine // 2, pl.ds(mine % 2, 1), :]).astype(BF)
+        v_out[at, :] = value
+        vt[...] = value.astype(F32).T.astype(BF)
+        strips = [(head, strip) for head in range(3) for strip in range(block // STRIP)]
+
+        def keys_of(strip):
+            return strip * STRIP + STRIP if diagonal else block
+
+        def scored(head, strip):
+            depth = 128 if head < 2 else HD
+            return mm(key[0 : keys_of(strip), head_lanes(head)], qm[head, 0:depth, strip * STRIP : strip * STRIP + STRIP])
+
+        ahead = [scored(*strips[i]) for i in range(LEAD)]
+        for i, (head, strip) in enumerate(strips):
+            scores = ahead.pop(0)
+            if i + LEAD < len(strips):
+                ahead.append(scored(*strips[i + LEAD]))
+            lanes = slice(strip * STRIP, strip * STRIP + STRIP)
+            count = keys_of(strip)
+            places = first_key + lax.broadcasted_iota(jnp.int32, (count, STRIP), 0)
+            allowed = places >= begins[:, lanes]
+            if diagonal:
+                queries = first_query + strip * STRIP + lax.broadcasted_iota(jnp.int32, (count, STRIP), 1)
+                allowed = allowed & (places <= queries)
+            scores = jnp.where(allowed, scores, NEG)
+            old = peak[head : head + 1, lanes]
+            new = jnp.maximum(old, jnp.max(scores, axis=0, keepdims=True))
+            weights = jnp.exp(scores - new)
+            factor = jnp.exp(old - new)
+            peak[head : head + 1, lanes] = new
+            total[head : head + 1, lanes] = total[head : head + 1, lanes] * factor + jnp.sum(
+                weights, axis=0, keepdims=True
+            )
+            part = slice(head * HD, head * HD + HD)
+            acc[part, lanes] = acc[part, lanes] * factor + mm(vt[part, 0:count], weights.astype(BF))
+
+    attend(me.ctx, True)
+
+    @pl.loop(0, levels)
+    def _(step):
+        @pl.when(step + 1 <= z)
+        def _():
+            for slot in range(2):
+                got = held(step + 1, slot, side)
+                remote(got, got, z_send.at[step, slot], z_recv.at[step + 1, slot], me.twin).wait_recv()
+                spread(step + 1, slot)
+
+        @pl.when(step <= z)
+        def _():
+            for slot in range(2):
+                got = held(step, slot, 1 - side)
+                remote(got, got, y_send.at[step, slot], y_recv.at[step, slot], me.beside).wait_recv()
+                remote(got, got, core_send.at[step, 1, slot], core_recv.at[step, 1, slot], me.twin).start()
+
+        @pl.loop(0, 2)
+        def _(turn):
+            ctx = me.ctx - 2 * step + (1 - turn) * (1 - 2 * side) - 2 * turn
+
+            @pl.when((turn == 0) & (step <= z))
+            def _():
+                from_twin(step, 1, 1 - side)
+
+            @pl.when((turn == 1) & (step + 1 <= z))
+            def _():
+                from_twin(step + 1, 0, side)
+
+            @pl.when((ctx >= 0) & (ctx < me.ctx))
+            def _():
+                attend(ctx, False)
+
+    for head in range(3):
+        part = slice(head * HD, head * HD + HD)
+        o_out[part, :] = acc[part, :] / total[head : head + 1, :]
+    lse_out[...] = peak[...] + jnp.log(jnp.maximum(total[...], 1e-30))
+
+    other = (1 - me.half) * 2 + me.core
+    got = rows_of(gtwo_ref, other)
+    remote(got, got, two_send.at[0], two_recv.at[0], me.across).wait_recv()
+    two_f = go(remote(got, got, two_send.at[2], two_recv.at[2], me.twin))
+    for copy in local:
+        copy.wait()
+    for copy in vecs + atts + [two_x, across]:
+        copy.wait_send()
+    for copy in exps + [two_c, two_f]:
+        copy.wait()
+
+    @pl.loop(0, levels)
+    def _(step):
+        @pl.when(step <= z)
+        def _():
+            for slot in range(2):
+                got = held(step, slot, side)
+
+                @pl.when(z < top)
+                def _():
+                    remote(got, got, z_send.at[step, slot], z_recv.at[step, slot], me.twin).wait_send()
+
+                remote(got, got, y_send.at[step, slot], y_recv.at[step, slot], me.beside).wait_send()
+                for which in range(2):
+                    remote(got, got, core_send.at[step, which, slot], core_recv.at[step, which, slot], me.twin).wait_send()
+
+
+def gather_attend(starts, tokens, vectors, attend_weight, expand_weight, cotangent):
+    levels = lax.axis_size("ctx") // 2
+    rows = tokens.shape[0]
+    block = rows * 4
+    length = block * levels * 2
+    vmem = pl.BlockSpec(memory_space=pltpu.VMEM)
+    dma = pltpu.SemaphoreType.DMA
+    return pl.pallas_call(
+        functools.partial(gather_attend_kernel, levels),
+        in_specs=[pl.BlockSpec(memory_space=pltpu.SMEM), vmem, vmem, vmem, pl.BlockSpec(memory_space=pl.ANY), vmem],
+        out_specs=[vmem] * 10,
+        out_shape=[
+            jax.ShapeDtypeStruct((length, D), BF),
+            jax.ShapeDtypeStruct((D, 576), BF),
+            jax.ShapeDtypeStruct((D, D), BF),
+            jax.ShapeDtypeStruct((block, D), BF),
+            jax.ShapeDtypeStruct((8, D), F32),
+            jax.ShapeDtypeStruct((block, 192), BF),
+            jax.ShapeDtypeStruct((length, 192), BF),
+            jax.ShapeDtypeStruct((length, 192), BF),
+            jax.ShapeDtypeStruct((192, block), F32),
+            jax.ShapeDtypeStruct((8, block), F32),
+        ],
+        scratch_shapes=[
+            pltpu.VMEM((4, rows, 576), BF),
+            pltpu.VMEM((4, 8, 192), F32),
+            pltpu.VMEM((1, block), jnp.int32),
+            pltpu.VMEM((3, 128, block), BF),
+            pltpu.VMEM((192, block), BF),
+            pltpu.VMEM((192, block), F32),
+            pltpu.VMEM((8, block), F32),
+            pltpu.VMEM((8, block), F32),
+            dma((3,)), dma((3,)), dma((3,)), dma((3,)), dma((3,)), dma((3,)), dma((3,)), dma((3,)),
+            dma((1,)), dma((1,)),
+            dma((levels, 2)), dma((levels + 1, 2)),
+            dma((levels, 2)), dma((levels, 2)),
+            dma((levels, 2, 2)), dma((levels, 2, 2)),
+            dma((1,)),
+        ],
+        compiler_params=pltpu.CompilerParams(collective_id=4, has_side_effects=True, vmem_limit_bytes=48 << 20),
+        name="gather_attend",
+    )(starts, tokens, vectors, attend_weight, expand_weight, cotangent)
+
+
 def gelu_pair(t):
     slope = 0.7978845608028654
     square = t * t
@@ -757,6 +1038,640 @@
     )(o, wp, expand, contract, ebias, tokens, cotangent, gtwo, vectors)
 
 
+class Exchange:
+    def __init__(self, me, levels, items, y_send, y_recv, z_send, z_recv):
+        self.me, self.top, self.items = me, levels - 1, items
+        self.y_send, self.y_recv, self.z_send, self.z_recv = y_send, y_recv, z_send, z_recv
+
+    def beside(self, level, act, only=None):
+        for i, (chunk, y_in, z_out, z_in) in enumerate(self.items):
+            if only is None or i in only:
+                act(remote(chunk(level, 1 - self.me.side), y_in.at[level], self.y_send.at[level, i], self.y_recv.at[level, i], self.me.beside))
+
+    def steps(self, step, act):
+        z, top = self.me.level, self.top
+        down = step - (top - z)
+        up = top - (step - z)
+
+        @pl.when((down >= 0) & (down < z))
+        def _():
+            act(down, 0)
+
+        @pl.when((up <= top) & (up > z))
+        def _():
+            act(up, 1)
+
+    def along(self, level, way, act):
+        device = self.me.at(level=self.me.level - 1) if way == 0 else self.me.at(level=self.me.level + 1)
+        last = level == (self.me.level - 1 if way == 0 else self.me.level + 1)
+        spot = level if way == 0 else jnp.where(last, self.top + 1, level)
+        for i, (chunk, y_in, z_out, z_in) in enumerate(self.items):
+            act(remote(z_out.at[level], z_in.at[spot], self.z_send.at[level, i], self.z_recv.at[spot, i], device))
+
+    def arrived(self, level, way):
+        spot = level if way == 0 else jnp.where(level == self.me.level, self.top + 1, level)
+        for i, (chunk, y_in, z_out, z_in) in enumerate(self.items):
+            remote(z_out.at[level], z_in.at[spot], self.z_send.at[level, i], self.z_recv.at[spot, i], self.me.twin).wait_recv()
+        return spot
+
+    def step(self, step):
+        z, top, side = self.me.level, self.top, self.me.side
+
+        def act(level, way):
+            self.beside(level, lambda copy: copy.wait_recv())
+            inner = (z < top) if way == 0 else (z > 0)
+
+            @pl.when(inner)
+            def _():
+                spot = self.arrived(level, way)
+                for chunk, y_in, z_out, z_in in self.items:
+                    z_out[level] = (
+                        chunk(level, side)[...].astype(F32) + y_in[level].astype(F32) + z_in[spot].astype(F32)
+                    ).astype(BF)
+
+            @pl.when(jnp.logical_not(inner))
+            def _():
+                for chunk, y_in, z_out, z_in in self.items:
+                    z_out[level] = (chunk(level, side)[...].astype(F32) + y_in[level].astype(F32)).astype(BF)
+
+            self.along(level, way, lambda copy: copy.start())
+
+        self.steps(step, act)
+
+    def final(self, targets):
+        z, top, side = self.me.level, self.top, self.me.side
+        self.beside(z, lambda copy: copy.wait_recv())
+
+        def add(spots):
+            for (chunk, y_in, z_out, z_in), target in zip(self.items, targets):
+                sum_of = chunk(z, side)[...].astype(F32) + y_in[z].astype(F32)
+                for spot in spots:
+                    sum_of = sum_of + z_in[spot].astype(F32)
+                target[...] = sum_of.astype(BF)
+
+        @pl.when(z < top)
+        def _():
+            self.arrived(z, 0)
+
+        @pl.when(z > 0)
+        def _():
+            self.arrived(z, 1)
+
+        @pl.when(z == 0)
+        def _():
+            add((z,))
+
+        @pl.when(z == top)
+        def _():
+            add((top + 1,))
+
+        @pl.when((z > 0) & (z < top))
+        def _():
+            add((z, top + 1))
+
+    def drain(self):
+        for level in range(self.top + 1):
+            self.beside(level, lambda copy: copy.wait_send())
+
+            @pl.when(level != self.me.level)
+            def _():
+                for i, (chunk, y_in, z_out, z_in) in enumerate(self.items):
+                    remote(z_out.at[level], z_in.at[level], self.z_send.at[level, i], self.z_recv.at[level, i], self.me.twin).wait_send()
+
+
+def attend_reduce_kernel(
+    levels, starts_ref, all_ref, k_ref, v_ref, q_ref, o_ref, lse_ref, g_ref, wp_ref, aw_ref,
+    c_ref, e_ref, tok_ref, gmid_ref, vec_ref, sums_ref,
+    tg_out, cg_out, eg_out, ag_out, pg_out, vec_out, hid_out,
+    rows_in, keys_in, values_in, begins, qm, dm, qn, dn, delta, dqt, kt, dk, dv, gt, a_part, p_part,
+    dnb, far, keep, x_out, x_in, y_out, y_in, d_out, d_in,
+    yc, ye, ya, yp, zc_out, ze_out, za_out, zp_out, zc_in, ze_in, za_in, zp_in, v_out, v_in, e_move, a_move, a_rows,
+    pre_sem, far_send, far_recv, x_send, x_recv, y_send, y_recv, d_send, d_recv,
+    gy_send, gy_recv, gz_send, gz_recv, ay_send, ay_recv, az_send, az_recv,
+    me_send, me_recv, ma_send, ma_recv, u_send, u_recv, w_send, w_recv,
+    be_send, be_recv, ba_send, ba_recv, te_send, te_recv, ta_send, ta_recv, v_send, v_recv,
+):
+    me = Place()
+    z, side, mine, ctx = me.level, me.side, me.part, me.ctx
+    top = levels - 1
+    block = g_ref.shape[0]
+    barrier = pltpu.get_barrier_semaphore()
+    for device in (me.twin, me.across, me.corner, me.beside):
+        signal(barrier, device)
+    for step in range(1, levels):
+        signal(barrier, me.at(level=(z + step) % levels))
+    below, above = me.at(level=z - 1), me.at(level=z + 1)
+    start = lambda copy: copy.start()
+    wait_recv = lambda copy: copy.wait_recv()
+    wait_send = lambda copy: copy.wait_send()
+
+    def prefetch(index):
+        slot = index % 2
+        at = pl.ds(pl.multiple_of(index * block, block), block)
+        return (
+            pltpu.make_async_copy(all_ref.at[at], rows_in.at[slot], pre_sem.at[slot, 0]),
+            pltpu.make_async_copy(k_ref.at[at], keys_in.at[slot], pre_sem.at[slot, 1]),
+            pltpu.make_async_copy(v_ref.at[at], values_in.at[slot], pre_sem.at[slot, 2]),
+        )
+
+    def all_of(copies, act):
+        for copy in copies:
+            act(copy)
+
+    all_of(prefetch(0), start)
+
+    def corner_of(ref, level, where):
+        return ref.at[pl.ds(pl.multiple_of(level * 48, 48), 48), pl.ds(pl.multiple_of(where * 384, 128), 384)]
+
+    grads = Exchange(
+        me, levels,
+        (
+            (lambda level, where: c_ref.at[level * 2 + where], yc, zc_out, zc_in),
+            (lambda level, where: e_ref.at[level * 2 + where], ye, ze_out, ze_in),
+            (lambda level, where: corner_of(p_part, level, where), yp, zp_out, zp_in),
+        ),
+        gy_send, gy_recv, gz_send, gz_recv,
+    )
+    attends = Exchange(
+        me, levels, ((lambda level, where: a_part.at[level * 2 + where], ya, za_out, za_in),), ay_send, ay_recv, az_send, az_recv
+    )
+    grads_in = g_ref[...]
+    exact = o_ref[...]
+    p_part[...] = mm(exact.astype(BF), grads_in).astype(BF)
+    outer = mm_nt(grads_in, wp_ref[...]).astype(BF)
+    pl.semaphore_wait(barrier, levels + 3)
+    for step in range(levels - 1):
+        grads.steps(step, lambda level, way: grads.beside(level, start))
+    grads.beside(z, start)
+    flipped = outer.astype(F32).T
+    product = flipped * exact
+    for head in range(3):
+        delta[head : head + 1, :] = jnp.sum(product[head * HD : head * HD + HD], axis=0, keepdims=True)
+    fill_masked_columns(dm, flipped.astype(BF))
+    scaled = q_ref[...].astype(F32) * SCALE
+    fill_masked_columns(qm, scaled.T.astype(BF))
+    scaled = scaled.astype(BF)
+    for head in range(3):
+        depth = 128 if head < 2 else HD
+        qn[head, :, 0:depth] = masked_rows(scaled, head)
+        dn[head, :, 0:depth] = masked_rows(outer, head)
+    dqt[...] = jnp.zeros(dqt.shape, F32)
+    gt[...] = jnp.zeros(gt.shape, F32)
+    first_query = ctx * block
+    begins[...] = begins_of(starts_ref, first_query, block)
+    v_out[0] = jnp.zeros(v_out.shape[1:], F32)
+
+    def attend(index, diagonal):
+        slot = index % 2
+        first_key = index * block
+        kt[...] = keys_in[slot].astype(F32).T.astype(BF)
+        dk[...] = jnp.zeros(dk.shape, F32)
+        dv[...] = jnp.zeros(dv.shape, F32)
+        strips = [(head, strip) for head in range(3) for strip in range(block // STRIP)]
+
+        def keys_of(strip):
+            return strip * STRIP + STRIP if diagonal else block
+
+        def scored(head, strip):
+            depth = 128 if head < 2 else HD
+            lanes = head_lanes(head)
+            cols = slice(strip * STRIP, strip * STRIP + STRIP)
+            count = keys_of(strip)
+            return (
+                mm(keys_in[slot, 0:count, lanes], qm[head, 0:depth, cols]),
+                mm(values_in[slot, 0:count, lanes], dm[head, 0:depth, cols]),
+            )
+
+        ahead = [scored(*strips[i]) for i in range(BACK_LEAD)]
+        for i, (head, strip) in enumerate(strips):
+            scores, outer = ahead.pop(0)
+            if i + BACK_LEAD < len(strips):
+                ahead.append(scored(*strips[i + BACK_LEAD]))
+            depth = 128 if head < 2 else HD
+            lanes = head_lanes(head)
+            cols = slice(strip * STRIP, strip * STRIP + STRIP)
+            count = keys_of(strip)
+            places = first_key + lax.broadcasted_iota(jnp.int32, (count, STRIP), 0)
+            allowed = places >= begins[:, cols]
+            if diagonal:
+                queries = first_query + strip * STRIP + lax.broadcasted_iota(jnp.int32, (count, STRIP), 1)
+                allowed = allowed & (places <= queries)
+            probs = jnp.where(allowed, jnp.exp(scores - lse_ref[head : head + 1, cols]), 0.0)
+            inner = (probs * (outer - delta[head : head + 1, cols])).astype(BF)
+            dv[0:count, lanes] += mm(probs.astype(BF), dn[head, cols, 0:depth])
+            dk[0:count, lanes] += mm(inner, qn[head, cols, 0:depth])
+            part = slice(head * HD, head * HD + HD)
+            dqt[part, cols] += mm(kt[part, 0:count], inner)
+        rows = rows_in[slot]
+        low_k = dk[...].astype(BF)
+        low_v = dv[...].astype(BF)
+        gt[192:384, :] += mm(low_k.astype(F32).T.astype(BF), rows)
+        gt[384:576, :] += mm(low_v.astype(F32).T.astype(BF), rows)
+        v_out[0, 12:13, 0:192] += jnp.sum(low_v.astype(F32), axis=0, keepdims=True)
+        through = mm_nt(low_k, aw_ref[:, 192:384]) + mm_nt(low_v, aw_ref[:, 384:576])
+        if diagonal:
+            flipped = dqt[...] * SCALE
+            low_q = flipped.T.astype(BF)
+            gt[0:192, :] = mm(flipped.astype(BF), rows)
+            v_out[0, 13:14, 0:192] = jnp.sum(low_q.astype(F32), axis=0, keepdims=True)
+            through = through + mm_nt(low_q, aw_ref[:, 0:192])
+        dnb[index % 3] = through.astype(BF)
+
+    def to_twin(index):
+        slot = index % 3
+        return tuple(
+            remote(
+                rows_of(dnb.at[slot], half * 2 + 1 - me.core), far.at[index, half],
+                far_send.at[index, half], far_recv.at[index, half], me.twin,
+            )
+            for half in range(2)
+        )
+
+    def x_copy(index):
+        return remote(x_out.at[index], x_in.at[index], x_send.at[index], x_recv.at[index], me.across)
+
+    def y_copy(level):
+        return remote(y_out.at[level], y_in.at[level], y_send.at[level], y_recv.at[level], me.beside)
+
+    def down_copy(level):
+        return remote(d_out.at[level], d_in.at[level], d_send.at[level], d_recv.at[level], below)
+
+    def with_twin(index):
+        slot = index % 3
+        all_of(to_twin(index), lambda copy: copy.wait())
+
+        def rows(half):
+            own = dnb[slot, pl.ds(pl.multiple_of((half * 2 + me.core) * 192, 192), 192), :]
+            return own.astype(F32) + far[index, half].astype(F32)
+
+        x_out[index] = rows(1 - me.half).astype(BF)
+        x_copy(index).start()
+        keep[index] = rows(me.half)
+
+    def with_across(index):
+        x_copy(index).wait_recv()
+        keep[index] += x_in[index].astype(F32)
+        level = index // 2
+
+        @pl.when((index % 2 != side))
+        def _():
+            y_out[level] = keep[index].astype(BF)
+            y_copy(level).start()
+
+    def with_beside(level):
+        y_copy(level).wait_recv()
+        keep[level * 2 + side] += y_in[level].astype(F32)
+
+    def dn_step(step):
+        level = step - (top - z)
+
+        @pl.when((level >= 0) & (level < z))
+        def _():
+            with_beside(level)
+            index = level * 2 + side
+
+            @pl.when(z < top)
+            def _():
+                down_copy(level).wait_recv()
+                keep[index] += d_in[level].astype(F32)
+
+            d_out[level] = keep[index].astype(BF)
+            down_copy(level).start()
+
+    def done(level, where):
+        return (cg_out.at[level * 2 + where], corner_of(pg_out, level, where))
+
+    def along_copies(way, distance):
+        level = z - distance if way == 0 else z + distance
+        device = above if way == 0 else below
+        return tuple(
+            remote(ref, ref, u_send.at[way, distance, i], u_recv.at[way, distance, i], device)
+            for i, ref in enumerate(done(level, side))
+        )
+
+    def side_copies(level, where):
+        return tuple(
+            remote(ref, ref, w_send.at[level, i], w_recv.at[level, i], me.beside) for i, ref in enumerate(done(level, where))
+        )
+
+    def pass_on(distance, way):
+        if way != 1:
+
+            @pl.when(z < top)
+            def _():
+                all_of(along_copies(0, distance), start)
+
+        if way != 0:
+
+            @pl.when(z > 0)
+            def _():
+                all_of(along_copies(1, distance), start)
+
+        all_of(side_copies(z - distance if way == 0 else z + distance, side), start)
+
+    def arrivals(distance):
+        for way in range(2):
+            level = z - distance if way == 0 else z + distance
+
+            @pl.when((level >= 0) & (level <= top))
+            def _():
+                for i, ref in enumerate(done(level, side)):
+                    remote(ref, ref, u_send.at[way, distance - 1, i], u_recv.at[way, distance - 1, i], me.twin).wait_recv()
+                pass_on(distance, way)
+
+    def e_chunk(where, origin):
+        return eg_out.at[pl.ds(pl.multiple_of(where * 96, 96), 96), pl.ds(pl.multiple_of(origin * D, D), D)]
+
+    def a_chunk(where, origin):
+        return a_rows.at[where, origin]
+
+    class Rows:
+        def __init__(self, moved, chunk, m_send, m_recv, b_send, b_recv, t_send, t_recv):
+            self.moved, self.chunk = moved, chunk
+            self.m_send, self.m_recv, self.b_send, self.b_recv = m_send, m_recv, b_send, b_recv
+            self.t_send, self.t_recv = t_send, t_recv
+
+        def move(self):
+            return remote(self.moved, self.chunk(side, mine), self.m_send.at[0], self.m_recv.at[mine], me.at(half=z // 2, core=z % 2))
+
+        def begin(self):
+            @pl.when(mine != z)
+            def _():
+                self.move().start()
+
+            @pl.when(mine == z)
+            def _():
+                self.chunk(side, mine)[...] = self.moved[...]
+
+        def line(self, way, origin):
+            ref = self.chunk(side, origin)
+            return remote(ref, ref, self.b_send.at[way, origin], self.b_recv.at[way, origin], below if way == 0 else above)
+
+        def turn(self, origin, where):
+            ref = self.chunk(where, origin)
+            return remote(ref, ref, self.t_send.at[origin], self.t_recv.at[origin], me.beside)
+
+        def spread(self, origin):
+            @pl.when((mine == z) & (mine != origin))
+            def _():
+                remote(self.moved, self.chunk(side, origin), self.m_send.at[0], self.m_recv.at[origin], me.twin).wait_recv()
+
+            @pl.when(mine > z)
+            def _():
+                self.line(0, origin).wait_recv()
+
+            @pl.when(mine < z)
+            def _():
+                self.line(1, origin).wait_recv()
+
+            @pl.when((mine >= z) & (z > 0))
+            def _():
+                self.line(0, origin).start()
+
+            @pl.when((mine <= z) & (z < top))
+            def _():
+                self.line(1, origin).start()
+
+            self.turn(origin, side).start()
+
+        def drain(self):
+            @pl.when(mine != z)
+            def _():
+                self.move().wait_send()
+
+            for origin in range(4):
+
+                @pl.when((mine >= z) & (z > 0))
+                def _():
+                    self.line(0, origin).wait_send()
+
+                @pl.when((mine <= z) & (z < top))
+                def _():
+                    self.line(1, origin).wait_send()
+
+                self.turn(origin, side).wait_send()
+
+    e_flow = Rows(e_move, e_chunk, me_send, me_recv, be_send, be_recv, te_send, te_recv)
+    a_flow = Rows(a_move, a_chunk, ma_send, ma_recv, ba_send, ba_recv, ta_send, ta_recv)
+
+    @pl.loop(0, 2 * levels + 3)
+    def _(turn):
+        @pl.when(turn <= ctx)
+        def _():
+            all_of(prefetch(turn), lambda copy: copy.wait())
+
+        @pl.when(turn + 1 <= ctx)
+        def _():
+            all_of(prefetch(turn + 1), start)
+
+        @pl.when(turn < ctx)
+        def _():
+            attend(turn, False)
+
+        @pl.when(turn == ctx)
+        def _():
+            attend(turn, True)
+            flipped = gt[...].T.astype(BF)
+            for chunk in range(8):
+                a_part[chunk] = flipped[chunk * 96 : chunk * 96 + 96]
+            for step in range(levels - 1):
+                attends.steps(step, lambda level, way: attends.beside(level, start))
+            attends.beside(z, start)
+
+        @pl.when(turn <= ctx)
+        def _():
+            all_of(to_twin(turn), start)
+
+        @pl.when((turn >= 1) & (turn - 1 <= ctx))
+        def _():
+            with_twin(turn - 1)
+
+        @pl.when((turn % 2 == 1) & (turn < 2 * levels - 1))
+        def _():
+            grads.step(turn // 2)
+
+        @pl.when(turn == 2 * levels - 1)
+        def _():
+            grads.final((cg_out.at[ctx], e_move, corner_of(pg_out, z, side)))
+            e_flow.begin()
+            pass_on(0, 2)
+
+        @pl.when((turn >= 3) & (turn - 3 <= ctx))
+        def _():
+            with_across(turn - 3)
+
+        @pl.when((turn >= 6) & (turn % 2 == 0))
+        def _():
+            dn_step((turn - 6) // 2)
+
+    attends.step(0)
+    arrivals(1)
+    attends.step(1)
+    for origin in range(4):
+        e_flow.spread(origin)
+    attends.step(2)
+    arrivals(2)
+    attends.final((a_move,))
+    a_flow.begin()
+
+    @pl.when(side == 0)
+    def _():
+        with_beside(z)
+
+    @pl.when(z < top)
+    def _():
+        down_copy(z).wait_recv()
+        keep[ctx] += d_in[z].astype(F32)
+
+    grad = keep[ctx]
+    gain = vec_ref[4:5, :]
+    normed, unit, inverse = layer_norm(tok_ref[...].astype(F32), gain, vec_ref[5:6, :])
+    scaled = grad * gain
+    spread = (
+        scaled - jnp.mean(scaled, axis=1, keepdims=True) - unit * jnp.mean(scaled * unit, axis=1, keepdims=True)
+    )
+    tg_out[...] = (gmid_ref[...] + inverse * spread).astype(BF)
+    for part in range(4):
+
+        @pl.when(mine == part)
+        def _():
+            v_out[0, 0:1, part * 192 : part * 192 + 192] = v_out[0, 13:14, 0:192]
+            v_out[0, 1:2, part * 192 : part * 192 + 192] = v_out[0, 12:13, 0:192]
+            v_out[0, 8 + part : 9 + part, :] = sums_ref[4:5, :]
+
+    v_out[0, 12:16, :] = jnp.zeros((4, D), F32)
+    v_out[0, 2:4, :] = sums_ref[0:2, :]
+    v_out[0, 4:5, :] = jnp.sum(grad * unit, axis=0, keepdims=True)
+    v_out[0, 5:6, :] = jnp.sum(grad, axis=0, keepdims=True)
+    v_out[0, 6:8, :] = sums_ref[2:4, :]
+    for origin in range(4):
+        a_flow.spread(origin)
+    for i, device in enumerate((me.twin, me.across, me.beside)):
+        copy = remote(v_out.at[i], v_in.at[i], v_send.at[i], v_recv.at[i], device)
+        copy.start()
+        copy.wait_recv()
+        v_out[i + 1] = v_out[i] + v_in[i]
+    v_in[3 + z] = v_out[3]
+    for step in range(1, levels):
+        remote(v_out.at[3], v_in.at[3 + z], v_send.at[2 + step], v_recv.at[3 + z], me.at(level=(z + step) % levels)).start()
+    arrivals(3)
+    for step in range(1, levels):
+        level = (z + step) % levels
+        remote(v_out.at[3], v_in.at[3 + level], v_send.at[2 + step], v_recv.at[3 + level], me.twin).wait_recv()
+    total = v_in[3]
+    for level in range(1, levels):
+        total = total + v_in[3 + level]
+    v_out[4] = total
+    hid_out[...] = v_out[4, pl.ds(8 + mine, 1), :]
+    for part in range(4):
+
+        @pl.when(mine == part)
+        def _():
+            source, lane = part // 2, (part % 2) * 384
+            vec_out[0:1, :] = total[source : source + 1, lane : lane + 192]
+            vec_out[1:2, :] = total[source : source + 1, lane + 192 : lane + 384]
+            vec_out[2:8, :] = total[2:8, part * 192 : part * 192 + 192]
+
+    for level in range(levels):
+        all_of(side_copies(level, 1 - side), wait_recv)
+    for flow in (e_flow, a_flow):
+        for origin in range(4):
+            flow.turn(origin, 1 - side).wait_recv()
+    for where in range(2):
+        for part in range(4):
+            for kind in range(3):
+                lane = kind * D + part * 192
+                ag_out[where * 96 : where * 96 + 96, lane : lane + 192] = a_rows[
+                    where, part, :, kind * 192 : kind * 192 + 192
+                ].astype(F32)
+    grads.drain()
+    attends.drain()
+    e_flow.drain()
+    a_flow.drain()
+    for level in range(levels):
+        all_of(side_copies(level, side), wait_send)
+
+        @pl.when((level < z) | ((level == z) & (side == 1)))
+        def _():
+            y_copy(level).wait_send()
+
+        @pl.when(level < z)
+        def _():
+            down_copy(level).wait_send()
+
+    @pl.loop(0, 2 * levels)
+    def _(index):
+        @pl.when(index <= ctx)
+        def _():
+            x_copy(index).wait_send()
+
+    for distance in range(levels):
+
+        @pl.when((z - distance >= 0) & (z < top))
+        def _():
+            all_of(along_copies(0, distance), wait_send)
+
+        @pl.when((z + distance <= top) & (z > 0))
+        def _():
+            all_of(along_copies(1, distance), wait_send)
+
+    for i in range(2 + levels):
+        remote(v_out.at[0], v_in.at[0], v_send.at[i], v_recv.at[0], me.twin).wait_send()
+
+
+def attend_reduce(starts, rows_all, k, v, q, o, lse, g, wp, aw, contract, expand, tokens, grad_middle, vectors, sums):
+    levels = lax.axis_size("ctx") // 2
+    rows = tokens.shape[0]
+    block = rows * 4
+    vmem = pl.BlockSpec(memory_space=pltpu.VMEM)
+    anywhere = pl.BlockSpec(memory_space=pl.ANY)
+    dma = pltpu.SemaphoreType.DMA
+    n = levels
+
+    def buf(*shape):
+        return pltpu.VMEM(shape, BF)
+
+    def wide(*shape):
+        return pltpu.VMEM(shape, F32)
+
+    return pl.pallas_call(
+        functools.partial(attend_reduce_kernel, levels),
+        in_specs=[pl.BlockSpec(memory_space=pltpu.SMEM)] + [anywhere] * 3 + [vmem] * 12,
+        out_specs=[vmem] * 7,
+        out_shape=[
+            jax.ShapeDtypeStruct((rows, D), BF),
+            jax.ShapeDtypeStruct((2 * n, 96, D), BF),
+            jax.ShapeDtypeStruct((192, 4 * D), BF),
+            jax.ShapeDtypeStruct((192, 3 * D), F32),
+            jax.ShapeDtypeStruct((192, D), BF),
+            jax.ShapeDtypeStruct((8, 192), F32),
+            jax.ShapeDtypeStruct((1, D), F32),
+        ],
+        scratch_shapes=[
+            buf(2, block, D), buf(2, block, 192), buf(2, block, 192), pltpu.VMEM((1, block), jnp.int32),
+            buf(3, 128, block), buf(3, 128, block), buf(3, block, 128), buf(3, block, 128),
+            wide(8, block), wide(192, block), buf(192, block), wide(block, 192), wide(block, 192), wide(576, D),
+            buf(2 * n, 96, 576), buf(192, D),
+            buf(3, block, D), buf(2 * n, 2, rows, D), wide(2 * n, rows, D), buf(2 * n, rows, D), buf(2 * n, rows, D),
+            buf(n, rows, D), buf(n, rows, D), buf(n, rows, D), buf(n, rows, D),
+            buf(n, 96, D), buf(n, 96, D), buf(n, 96, 576), buf(n, 48, 384),
+            buf(n, 96, D), buf(n, 96, D), buf(n, 96, 576), buf(n, 48, 384),
+            buf(n + 1, 96, D), buf(n + 1, 96, D), buf(n + 1, 96, 576), buf(n + 1, 48, 384),
+            wide(5, 16, D), wide(3 + n, 16, D), buf(96, D), buf(96, 576), buf(2, 4, 96, 576),
+            dma((2, 3)), dma((2 * n, 2)), dma((2 * n, 2)), dma((2 * n,)), dma((2 * n,)),
+            dma((n,)), dma((n,)), dma((n,)), dma((n,)),
+            dma((n, 3)), dma((n, 3)), dma((n, 3)), dma((n + 1, 3)),
+            dma((n, 1)), dma((n, 1)), dma((n, 1)), dma((n + 1, 1)),
+            dma((1,)), dma((4,)), dma((1,)), dma((4,)),
+            dma((2, n, 2)), dma((2, n, 2)), dma((n, 2)), dma((n, 2)),
+            dma((2, 4)), dma((2, 4)), dma((2, 4)), dma((2, 4)), dma((4,)), dma((4,)), dma((4,)), dma((4,)),
+            dma((2 + n,)), dma((3 + n,)),
+        ],
+        compiler_params=pltpu.CompilerParams(collective_id=5, has_side_effects=True, vmem_limit_bytes=60 << 20),
+        name="attend_reduce",
+    )(starts, rows_all, k, v, q, o, lse, g, wp, aw, contract, expand, tokens, grad_middle, vectors, sums)
+
+
 def normalize(rows_in, gain, shift):
     mean = jnp.mean(rows_in, axis=1, keepdims=True)
     centered = rows_in - mean
@@ -778,6 +1693,97 @@
 def first_position(places, starts):
     below = starts[None, :] <= places[:, None]
     return jnp.max(jnp.where(below, starts[None, :], 0), axis=1)
+
+
+def forward_plain(
+    tokens, document_starts, attend_weight, attend_bias, expand_weight, cotangent, own_vectors
+):
+    rows = tokens.shape[0]
+    ways = lax.axis_size("fsdp")
+    block = rows * ways
+    ctx = lax.axis_index("ctx")
+    part = lax.axis_index("fsdp")
+    vectors = lax.dynamic_update_slice(jnp.zeros((6, D), F32), jnp.stack(own_vectors).astype(F32), (0, part * rows))
+    biases = lax.dynamic_update_slice(jnp.zeros((2 * D,), F32), attend_bias.astype(F32), (part * 2 * rows,))
+    vectors = jnp.concatenate([biases.reshape(2, D), vectors])
+    attend_cols = attend_weight.reshape(rows, 3, ways, 192).transpose(2, 0, 1, 3).reshape(ways, rows, 576)
+    normed_all, attend_cols, expand_cols, g2, vectors = gather_inputs(
+        tokens, vectors, attend_cols, expand_weight, cotangent
+    )
+    wq, wk, wv = attend_cols[:, :192], attend_cols[:, 192:384], attend_cols[:, 384:]
+    bias = lax.dynamic_slice(vectors, (0, part * 192), (2, 192))
+    own = lax.dynamic_slice(normed_all, (ctx * block, 0), (block, D))
+    where, begins_row = places_of(document_starts, block)
+    q, k, v, o, lse = attend_forward(where, normed_all, own, wq, wk, wv, bias, begins_row)
+    return normed_all, attend_cols, expand_cols, g2, vectors, q, k, v, o, lse
+
+
+def places_of(document_starts, block):
+    ctx = lax.axis_index("ctx")
+    places = ctx * block + jnp.arange(block, dtype=jnp.int32)
+    begins = first_position(places, document_starts)
+    where = jnp.stack([ctx, begins[0], begins[-1]]).astype(jnp.int32)
+    return where, begins.reshape(1, block)
+
+
+def forward(tokens, document_starts, attend_weight, attend_bias, expand_weight, cotangent, own_vectors):
+    rows = tokens.shape[0]
+    if lax.axis_size("ctx") != 8:
+        return forward_plain(
+            tokens, document_starts, attend_weight, attend_bias, expand_weight, cotangent, own_vectors
+        )
+    listed = [attend_bias[:rows], attend_bias[rows:]] + list(own_vectors)
+    line = lax.broadcasted_iota(jnp.int32, (8, rows), 0)
+    vectors = jnp.zeros((8, rows), F32)
+    for i, vector in enumerate(listed):
+        vectors = jnp.where(line == i, vector.astype(F32)[None, :], vectors)
+    return gather_attend(document_starts, tokens, vectors, attend_weight, expand_weight, cotangent)
+
+
+def backward_plain(
+    document_starts, normed_all, k, v, q, o, lse, g1, project_weight, attend_cols,
+    contract_part, expand_part, tokens, grad_middle, vectors, mlp_sums,
+):
+    both = ("ctx", "fsdp")
+    rows = tokens.shape[0]
+    ways = lax.axis_size("fsdp")
+    block = rows * ways
+    ctx = lax.axis_index("ctx")
+    part = lax.axis_index("fsdp")
+    gain_one = vectors[4]
+    wq, wk, wv = attend_cols[:, :192], attend_cols[:, 192:384], attend_cols[:, 384:]
+    where, begins_row = places_of(document_starts, block)
+    own = lax.dynamic_slice(normed_all, (ctx * block, 0), (block, D))
+    dn, attend_t, project_part, sums = attend_backward(
+        where, normed_all, k, v, own, q, o, lse, g1, project_weight, wq, wk, wv, begins_row
+    )
+    grad_normed = lax.psum_scatter(dn.astype(F32), both, scatter_dimension=0, tiled=True)
+    normed, unit_one, inverse_one = normalize(tokens.astype(F32), gain_one, jnp.zeros_like(gain_one))
+    first_part, gainone_grad, shiftone_grad = normalize_back(grad_normed, unit_one, inverse_one, gain_one)
+    tokens_grad = (grad_middle + first_part).astype(BF)
+
+    def summed(array_in):
+        return lax.psum(array_in.astype(BF), "ctx").astype(F32)
+
+    contract_grad = summed(contract_part)
+    project_grad = summed(project_part)
+    expand_grad = lax.all_to_all(summed(expand_part).reshape(ways, rows, D), "fsdp", 0, 0)
+    expand_grad = expand_grad.transpose(1, 0, 2).reshape(rows, ways * D)
+    attend_grad = lax.all_to_all(summed(attend_t.T).reshape(ways, rows, 576), "fsdp", 0, 0)
+    attend_grad = attend_grad.reshape(ways, rows, 3, 192).transpose(1, 2, 0, 3).reshape(rows, 3 * D)
+    spread = lax.dynamic_update_slice(jnp.zeros((2, D), F32), sums[:2], (0, part * 192))
+    hidden = lax.dynamic_update_slice(jnp.zeros((4, D), F32), mlp_sums[4:5], (part, 0))
+    totals = jnp.concatenate([
+        spread, mlp_sums[0:2], gainone_grad[None], shiftone_grad[None], mlp_sums[2:4], hidden
+    ])
+    totals = lax.psum(totals, both)
+    attbias = lax.dynamic_slice(totals[:2].reshape(-1), (part * 2 * rows,), (2 * rows,))
+    mine = lax.dynamic_slice(totals, (2, part * rows), (6, rows))
+    expbias = lax.dynamic_slice(totals, (8 + part, 0), (1, D)).reshape(D)
+    return (
+        tokens_grad, attend_grad, attbias, project_grad, mine[0], expand_grad, expbias,
+        contract_grad, mine[1], mine[2], mine[3], mine[4], mine[5],
+    )
 
 
 def per_device(
@@ -795,61 +1801,26 @@
     def whole(array_in):
         return lax.all_gather(array_in, "fsdp", axis=0, tiled=True)
 
-    own_vectors = jnp.stack([project_bias, contract_bias, gain_first, shift_first, gain_second, shift_second])
-    vectors = lax.dynamic_update_slice(jnp.zeros((6, D), F32), own_vectors.astype(F32), (0, part * rows))
-    biases = lax.dynamic_update_slice(jnp.zeros((2 * D,), F32), attend_bias.astype(F32), (part * 2 * rows,))
-    vectors = jnp.concatenate([biases.reshape(2, D), vectors])
-    attend_cols = attend_weight.reshape(rows, 3, ways, 192).transpose(2, 0, 1, 3).reshape(ways, rows, 576)
-    normed_all, attend_cols, expand_cols, g2, vectors = gather_inputs(
-        tokens, vectors, attend_cols, expand_weight, cotangent
+    normed_all, attend_cols, expand_cols, g2, vectors, q, k, v, o, lse = forward(
+        tokens, document_starts, attend_weight, attend_bias, expand_weight, cotangent,
+        (project_bias, contract_bias, gain_first, shift_first, gain_second, shift_second),
     )
-    project_b, contract_b, gain_one, shift_one, gain_two, shift_two = [vectors[i] for i in range(2, 8)]
-    wq, wk, wv = attend_cols[:, :192], attend_cols[:, 192:384], attend_cols[:, 384:]
-    bias = lax.dynamic_slice(vectors, (0, part * 192), (2, 192))
-
-    hidden_in = tokens.astype(F32)
-    normed, unit_one, inverse_one = normalize(hidden_in, gain_one, shift_one)
-    own = lax.dynamic_slice(normed_all, (ctx * block, 0), (block, D))
-    places = ctx * block + jnp.arange(block, dtype=jnp.int32)
-    begins = first_position(places, document_starts)
-    where = jnp.stack([ctx, begins[0], begins[-1]]).astype(jnp.int32)
-    begins_row = begins.reshape(1, block)
-    q, k, v, o, lse = attend_forward(where, normed_all, own, wq, wk, wv, bias, begins_row)
     block_output, grad_middle, g1, contract_part, expand_part, mlp_sums = feed_forward(
         o, project_weight, expand_cols, contract_weight, expand_bias.astype(F32).reshape(1, D), tokens, cotangent, g2, vectors
     )
-    dn, attend_t, project_part, sums = attend_backward(
-        where, normed_all, k, v, own, q, o, lse, g1, project_weight, wq, wk, wv, begins_row
+    if lax.axis_size("ctx") != 8:
+        return (block_output,) + backward_plain(
+            document_starts, normed_all, k, v, q, o, lse, g1, project_weight, attend_cols,
+            contract_part, expand_part, tokens, grad_middle, vectors, mlp_sums,
+        )
+    tokens_grad, contract_grad, expand_grad, attend_grad, project_grad, small, hidden = attend_reduce(
+        document_starts, normed_all, k, v, q, o, lse, g1, project_weight, attend_cols,
+        contract_part.reshape(8, 96, D), expand_part.reshape(8, 96, D), tokens, grad_middle, vectors, mlp_sums,
     )
-    grad_normed = lax.psum_scatter(dn.astype(F32), both, scatter_dimension=0, tiled=True)
-    first_part, gainone_grad, shiftone_grad = normalize_back(grad_normed, unit_one, inverse_one, gain_one)
-    tokens_grad = grad_middle + first_part
-
-    def summed(array_in):
-        return lax.psum(array_in.astype(BF), "ctx").astype(F32)
-
-    contract_grad = summed(contract_part)
-    project_grad = summed(project_part)
-    expand_grad = lax.all_to_all(summed(expand_part).reshape(ways, rows, D), "fsdp", 0, 0)
-    expand_grad = expand_grad.transpose(1, 0, 2).reshape(rows, ways * D)
-    attend_grad = lax.all_to_all(summed(attend_t.T).reshape(ways, rows, 576), "fsdp", 0, 0)
-    attend_grad = attend_grad.reshape(ways, rows, 3, 192).transpose(1, 2, 0, 3).reshape(rows, 3 * D)
-    expbias_grad = lax.psum(mlp_sums[4], "ctx")
-    spread = jnp.zeros((2, D), F32)
-    spread = lax.dynamic_update_slice(spread, sums[:2], (0, part * 192))
-    vectors = jnp.concatenate([
-        spread.reshape(-1),
-        mlp_sums[0], mlp_sums[1], gainone_grad, shiftone_grad, mlp_sums[2], mlp_sums[3],
-    ])
-    vectors = lax.psum(vectors, both)
-
-    def mine_of(start, length):
-        return lax.dynamic_slice(vectors, (start + part * (length // ways),), (length // ways,))
-
     return (
-        block_output.astype(BF), tokens_grad.astype(BF),
-        attend_grad, mine_of(0, 2 * D), project_grad, mine_of(2 * D, D), expand_grad, expbias_grad,
-        contract_grad, mine_of(3 * D, D), mine_of(4 * D, D), mine_of(5 * D, D), mine_of(6 * D, D), mine_of(7 * D, D),
+        block_output, tokens_grad, attend_grad, small[:2].reshape(-1), project_grad.astype(F32), small[2],
+        expand_grad.astype(F32), hidden.reshape(-1), contract_grad.reshape(D, D).astype(F32),
+        small[3], small[4], small[5], small[6], small[7],
     )
 
 

time: 552 us -> 311 us (0.56)
  waiting for transfers between devices: 277 us -> 0 us
  Pallas kernels: 119 us -> 276 us
  blocking collectives: 58.5 us -> 0 us
  local copies, waits for them, and re-layouts: 38.9 us -> 18.1 us
  other arithmetic: 27.5 us -> 12 us
  between operations: 15.7 us -> 0.78 us
  starting transfers between devices: 11.9 us -> 0 us
    psum x1 -> x0, waiting for transfers between devices: 250 us -> none  [summed(): return lax.psum(array_in.astype(BF), 'ctx').astype(F32)]
    pallas_call x3 -> x2, Pallas kernels: 69.2 us -> 228 us  [the longest x1 182 us: attend_reduce(): pl.pallas_call(functools.partial(attend_reduce_kernel, levels), in_specs=...]
    psum x2 -> x0, blocking collectives: 58.5 us -> none  [the longest x1 40.3 us: per_device(): vectors = lax.psum(vectors, both)]
    all_to_all x2 -> x0, waiting for transfers between devices: 27.4 us -> none  [the longest x1 27.4 us: per_device(): lax.all_to_all(summed(attend_t.T).reshape(ways, rows, 576), 'fsdp', 0, 0)]
    reshape x8 -> x1, local copies, waits for them, and re-layouts: 14 us -> 0.66 us  [per_device(): small[:2].reshape(-1)]
    all_to_all x2 -> x0, starting transfers between devices: 11.8 us -> none  [the longest x1 6.27 us: per_device(): lax.all_to_all(summed(expand_part).reshape(ways, rows, D), 'fsdp', 0, 0)]
    convert_element_type x7 -> x10, other arithmetic: 18.5 us -> 11.3 us  [the longest x7 4.77 us: forward(): vectors = jnp.where(line == i, vector.astype(F32)[None, :], vectors)]
    unnamed x29 -> x51, local copies, waits for them, and re-layouts: 8.1 us -> 15.2 us
  transfers between devices with their start and end apart: 4 -> 0, of which waited for: 2 -> 0; matrix products, arithmetic and copies ran while one was open for 6% -> 0% of each run, Pallas kernels for 0% -> 0%
where the time goes in v3:
time: 311 us; the launch traced here: 307 us
  Pallas kernels  276 us (89%)
  local copies, waits for them, and re-layouts  18.1 us (6%)
  other arithmetic  12 us (4%)
    pallas_call x1, Pallas kernels, attend_reduce(): pl.pallas_call(functools.partial(attend_reduce_kernel, levels), in_specs=...  182 us
    pallas_call x1, Pallas kernels, feed_forward(): pl.pallas_call(mlp_kernel, in_specs=[vmem] * 9, out_specs=[vmem] * 6, out...  48.2 us
    pallas_call x1, Pallas kernels, gather_attend(): pl.pallas_call(functools.partial(gather_attend_kernel, levels), in_specs=...  46.3 us
    unnamed x51, local copies, waits for them, and re-layouts  15.2 us

profile of v3, /device:TPU:3, one launch (start us, length us, event | category | flops | bytes accessed | tf_op | source)
XLA Modules:
  0.0 307.2 jit_solution(10453455946221785243)
XLA Ops:
  0.6 0.8 slice_convert_fusion.1
  5.5 1.0 copy-done
  6.5 1.0 copy-done.6
  7.5 1.2 copy-done.12
  9.3 46.3 %gather_attend.1 = (bf16[6144,768]{1,0:T(8,128)(2,1)}, bf16[768,576]{1,0:T(8,128)(2,1)S(1)}, bf16[768,768]{1,0:T(8,128)(2,1)S(1)}, bf16[768,768]{1,0:T(8,128)(2,...) custom-call(s32[8]{0:T(128)S(1)} %copy-done.18, ...), custom_call_target="tpu_custom_call" | custom-call | tf_op jit(solution)/shard_map/gather_attend/pallas_call | solution.py:832
  55.6 1.0 copy-done.8
  56.6 1.0 copy-done.9
  57.6 0.9 copy-done.11
  58.6 0.8 copy-done.14
  60.0 48.2 %feed_forward.1 = (bf16[192,768]{1,0:T(8,128)(2,1)S(1)}, f32[192,768]{1,0:T(8,128)S(1)}, bf16[768,768]{1,0:T(8,128)(2,1)S(1)}, bf16[768,768]{1,0:T(8,128)(2,1)S(...) custom-call(f32[192,768]{1,0:T(8,128)S(1)} %get-tuple-element.37.o_ref, bf16[192,768]{1,0:T(8,128)(2,1)S(1)} %copy-done.10, ...), custom_call_target="tpu_custom_call" | custom-call | tf_op jit(solution)/shard_map/feed_forward/pallas_call | solution.py:1010
  108.2 1.0 copy-done.3
  109.2 1.0 copy-done.4
  110.2 1.0 copy-done.5
  111.2 0.8 copy-done.13
  112.6 182.0 %attend_reduce.1 = (bf16[192,768]{1,0:T(8,128)(2,1)}, bf16[8,96,768]{2,1,0:T(8,128)(2,1)}, bf16[192,3072]{1,0:T(8,128)(2,1)}, f32[192,2304]{1,0:T(8,128)}, bf16[...) custom-call(s32[8]{0:T(128)} %starts_ref.3, bf16[6144,768]{1,0:T(8,128)(2,1)} %get-tuple-element.42.all_ref, ...), custom_call_target="tpu_custom_call" | custom-call | tf_op jit(solution)/shard_map/attend_reduce/pallas_call | solution.py:1637
  294.6 0.7 slice.29
  295.3 0.7 reshape.60
  296.0 1.8 convert_element_type.45
  297.8 1.5 fusion
  299.3 3.0 convert_element_type.46
  302.9 1.7 bitcast_convert_fusion
  304.6 0.7 copy.32
  305.3 0.7 copy.33
  306.0 1.2 copy.34
  (50 shorter events, 6.6 us)
Async XLA Ops:
  5.5 1.0 copy-start
  6.5 1.0 copy-start.6
  7.5 1.2 copy-start.12
  8.6 0.7 copy-start.18
  9.3 50.6 %copy-start.23 = (bf16[768]{0:T(1024)(128)(2,1)S(1)}, bf16[768]{0:T(1024)(128)(2,1)}, u32[]{:S(2)}) copy-start(bf16[768]{0:T(1024)(128)(2,1)} %param.22) | copy-start | bytes 4612
  9.3 50.6 %copy-start.1 = (bf16[192,768]{1,0:T(8,128)(2,1)S(1)}, bf16[192,768]{1,0:T(8,128)(2,1)}, u32[]{:S(2)}) copy-start(bf16[192,768]{1,0:T(8,128)(2,1)} %tok_ref.5) | copy-start | bytes 884740
  9.3 50.6 %copy-start.7 = (bf16[192,768]{1,0:T(8,128)(2,1)S(1)}, bf16[192,768]{1,0:T(8,128)(2,1)}, u32[]{:S(2)}) copy-start(bf16[192,768]{1,0:T(8,128)(2,1)} %cot_ref.3) | copy-start | bytes 884740
  9.3 50.7 %copy-start.10 = (bf16[192,768]{1,0:T(8,128)(2,1)S(1)}, bf16[192,768]{1,0:T(8,128)(2,1)}, u32[]{:S(2)}) copy-start(bf16[192,768]{1,0:T(8,128)(2,1)} %wp_ref.3) | copy-start | bytes 884740
  55.6 1.0 copy-start.8
  56.6 1.0 copy-start.9
  57.6 0.9 copy-start.11
  58.5 0.8 copy-start.14
  59.3 0.6 copy-start.16
  59.9 48.2 %copy-start.2 = (f32[192,768]{1,0:T(8,128)}, f32[192,768]{1,0:T(8,128)S(1)}, u32[]{:S(2)}) copy-start(f32[192,768]{1,0:T(8,128)S(1)} %get-tuple-element.37.o_ref) | copy-start | bytes 1769476
  59.9 48.2 %copy-start.15 = (f32[8,768]{1,0:T(8,128)}, f32[8,768]{1,0:T(8,128)S(1)}, u32[]{:S(2)}) copy-start(f32[8,768]{1,0:T(8,128)S(1)} %get-tuple-element.40.vec_ref) | copy-start | bytes 73732
  108.2 1.0 copy-start.3
  109.2 1.0 copy-start.4
  110.2 1.0 copy-start.5
  111.2 0.8 copy-start.13
  112.0 0.6 copy-start.17
  299.3 3.0 copy-start.22
  299.3 3.6 %copy-start.20 = (bf16[8,96,768]{2,1,0:T(8,128)(2,1)S(1)}, bf16[8,96,768]{2,1,0:T(8,128)(2,1)}, u32[]{:S(2)}) copy-start(bf16[8,96,768]{2,1,0:T(8,128)(2,1)} %get-tuple-element.59) | copy-start | bytes 3538948
  302.9 2.4 copy-start.21
  302.9 3.1 %copy-start.19 = (f32[192,2304]{1,0:T(8,128)S(1)}, f32[192,2304]{1,0:T(8,128)}, u32[]{:S(2)}) copy-start(f32[192,2304]{1,0:T(8,128)} %get-tuple-element.92) | copy-start | bytes 5308420

commit v4 on v3

--- a/solution.py
+++ b/solution.py
@@ -598,6 +598,9 @@
     )(tokens, vectors, attend_cols, expand_weight, cotangent)
 
 
+SHARE = 160
+
+
 def begins_of(starts_ref, first, count):
     places = first + lax.broadcasted_iota(jnp.int32, (1, count), 1)
     begins = jnp.zeros((1, count), jnp.int32)
@@ -608,16 +611,29 @@
 
 
 def gather_attend_kernel(
-    levels, starts_ref, tok_ref, vec_ref, aw_ref, ew_ref, cot_ref,
-    all_ref, attend_ref, expand_ref, gtwo_ref, vec_out, q_out, k_out, v_out, o_out, lse_out,
-    staged, vec_in, begins, qm, vt, acc, peak, total,
-    vec_send, vec_recv, att_send, att_recv, exp_send, exp_recv, two_send, two_recv,
-    x_send, x_recv, z_send, z_recv, y_send, y_recv, core_send, core_recv, local_sem,
+    levels, starts_ref, tok_hbm, aw_hbm, ew_ref, cot_hbm, *rest_refs,
 ):
+    vector_hbm, vector_refs = rest_refs[:7], rest_refs[-7:]
+    (
+        all_ref, attend_ref, expand_ref, gtwo_ref, vec_out, q_out, k_out, v_out, o_out, lse_out,
+        tok_ref, aw_ref, cot_ref, vec_ref, staged, vec_in, begins, qm, vt, acc, peak, total,
+        vec_send, vec_recv, att_send, att_recv, exp_send, exp_recv, two_send, two_recv,
+        x_send, x_recv, z_send, z_recv, y_send, y_recv, core_send, core_recv, r_send, r_recv, rc_send, rc_recv, local_sem,
+    ) = rest_refs[7:-7]
     me = Place()
     mine, z, side = me.part, me.level, me.side
     top = levels - 1
     block = gtwo_ref.shape[0]
+    fetched = (
+        pltpu.make_async_copy(tok_hbm, tok_ref, local_sem.at[1]),
+        pltpu.make_async_copy(aw_hbm, aw_ref, local_sem.at[2]),
+        pltpu.make_async_copy(cot_hbm, cot_ref, local_sem.at[3]),
+    ) + tuple(
+        pltpu.make_async_copy(source, target, local_sem.at[4 + i])
+        for i, (source, target) in enumerate(zip(vector_hbm, vector_refs))
+    )
+    for copy in fetched:
+        copy.start()
     barrier = pltpu.get_barrier_semaphore()
     for device in (me.twin, me.across, me.corner, me.beside):
         signal(barrier, device)
@@ -630,6 +646,13 @@
     def _():
         signal(barrier, me.at(level=z + 1))
 
+    for copy in fetched:
+        copy.wait()
+    both = vector_refs[0][...].astype(F32).reshape(1, 384)
+    vec_ref[0:1, :] = both[:, 0:192]
+    vec_ref[1:2, :] = both[:, 192:384]
+    for i, ref in enumerate(vector_refs[1:]):
+        vec_ref[2 + i : 3 + i, :] = ref[...].astype(F32).reshape(1, 192)
     for part in range(4):
         for kind in range(3):
             staged[part, :, kind * 192 : kind * 192 + 192] = aw_ref[:, kind * D + part * 192 : kind * D + part * 192 + 192]
@@ -648,9 +671,10 @@
 
     vecs = [go(remote(vec_ref, vec_in.at[mine], vec_send.at[i], vec_recv.at[i], d)) for i, (d, p) in enumerate(peers)]
     atts = [
-        go(remote(staged.at[p], rows_of(attend_ref, mine), att_send.at[i], att_recv.at[i], d))
-        for i, (d, p) in enumerate(peers)
+        remote(staged.at[p], rows_of(attend_ref, mine), att_send.at[i], att_recv.at[i], d) for i, (d, p) in enumerate(peers)
     ]
+    atts[0].start()
+    atts[1].start()
     vec_in[mine] = vec_ref[...]
     rows_of(attend_ref, mine)[...] = staged[mine]
     local = [
@@ -668,29 +692,54 @@
     own_rows = piece(all_ref, me.ctx, mine)
     own_rows[...] = out.astype(BF)
     across = go(remote(own_rows, own_rows, x_send.at[0], x_recv.at[0], me.across))
-
-    def spread(distance, slot):
-        half = me.half if slot == 0 else 1 - me.half
+    atts[2].start()
+
+    def most(ref):
+        return ref.at[pl.ds(0, SHARE)]
+
+    def rest(ref):
+        return ref.at[pl.ds(SHARE, 192 - SHARE)]
+
+    def held(distance, slot, where):
+        half = me.half + slot * (1 - 2 * me.half)
+        return piece(all_ref, (z - distance) * 2 + where, half * 2 + me.core)
+
+    def y_copy(distance, slot, where, whole):
+        got = held(distance, slot, where)
+        if not whole:
+            got = most(got)
+        return remote(got, got, y_send.at[distance, slot], y_recv.at[distance, slot], me.beside)
+
+    def rest_up(distance, slot):
+        got = rest(held(distance, slot, 1 - side))
+        return remote(got, got, r_send.at[distance, slot], r_recv.at[distance + 1, slot], me.at(level=z + 1))
+
+    def rest_twin(distance, slot):
+        got = rest(held(distance, slot, 1 - side))
+        return remote(got, got, rc_send.at[distance, slot], rc_recv.at[distance, slot], me.twin)
+
+    def spread(distance, slot, first):
+        half = me.half + slot * (1 - 2 * me.half)
         got = piece(all_ref, (z - distance) * 2 + side, half * 2 + me.core)
 
         @pl.when(z < top)
         def _():
             remote(got, got, z_send.at[distance, slot], z_recv.at[distance + 1, slot], me.at(level=z + 1)).start()
 
-        remote(got, got, y_send.at[distance, slot], y_recv.at[distance, slot], me.beside).start()
+        y_copy(distance, slot, side, first).start()
         remote(got, got, core_send.at[distance, 0, slot], core_recv.at[distance, 0, slot], me.twin).start()
 
-    def held(distance, slot, where):
-        half = me.half if slot == 0 else 1 - me.half
-        return piece(all_ref, (z - distance) * 2 + where, half * 2 + me.core)
-
-    def from_twin(distance, which, where):
+    def from_twin(distance, which, where, whole):
         for slot in range(2):
-            half = me.half if slot == 0 else 1 - me.half
+            half = me.half + slot * (1 - 2 * me.half)
             got = piece(all_ref, (z - distance) * 2 + where, half * 2 + 1 - me.core)
+            if not whole:
+                last = rest(got)
+                remote(last, last, rc_send.at[distance, slot], rc_recv.at[distance, slot], me.twin).wait_recv()
+                got = most(got)
             remote(got, got, core_send.at[distance, which, slot], core_recv.at[distance, which, slot], me.twin).wait_recv()
 
-    spread(0, 0)
+    spread(0, 0, True)
     two_x = go(remote(own_two, own_two, two_send.at[0], two_recv.at[0], me.across))
     two_c = go(remote(own_two, own_two, two_send.at[1], two_recv.at[1], me.twin))
     exps = [
@@ -700,10 +749,18 @@
     begins[...] = begins_of(starts_ref, me.ctx * block, block)
     got = held(0, 1, side)
     remote(got, got, x_send.at[0], x_recv.at[0], me.across).wait_recv()
-    spread(0, 1)
+    spread(0, 1, True)
+    def from_below(distance, slot):
+        @pl.when(distance <= z)
+        def _():
+            got = held(distance, slot, side)
+            remote(got, got, z_send.at[distance - 1, slot], z_recv.at[distance, slot], me.twin).wait_recv()
+            spread(distance, slot, False)
+
+    from_below(1, 0)
     for copy in atts:
         copy.wait_recv()
-    from_twin(0, 0, side)
+    from_twin(0, 0, side, True)
 
     first_query = me.ctx * block
     bias_q = vec_in[mine // 2, pl.ds(mine % 2, 1), :]
@@ -758,37 +815,56 @@
 
     attend(me.ctx, True)
 
-    @pl.loop(0, levels)
-    def _(step):
-        @pl.when(step + 1 <= z)
-        def _():
+    def take_side(distance, whole):
+        for slot in range(2):
+            y_copy(distance, slot, 1 - side, whole).wait_recv()
+            got = held(distance, slot, 1 - side)
+            if not whole:
+                got = most(got)
+            remote(got, got, core_send.at[distance, 1, slot], core_recv.at[distance, 1, slot], me.twin).start()
+
+    @pl.loop(1, 2 * levels)
+    def _(turn):
+        @pl.when(turn < 2 * levels - 2)
+        def _():
+            from_below(turn // 2 + 1, turn % 2)
+
+        distance = turn // 2
+
+        @pl.when(turn == 1)
+        def _():
+            take_side(0, True)
+
+            @pl.when(z < top)
+            def _():
+                for slot in range(2):
+                    rest_up(0, slot).start()
+
+            from_twin(0, 1, 1 - side, True)
+
+        @pl.when((turn > 1) & (turn % 2 == 1) & (distance <= z))
+        def _():
+            take_side(distance, False)
             for slot in range(2):
-                got = held(step + 1, slot, side)
-                remote(got, got, z_send.at[step, slot], z_recv.at[step + 1, slot], me.twin).wait_recv()
-                spread(step + 1, slot)
-
-        @pl.when(step <= z)
-        def _():
-            for slot in range(2):
-                got = held(step, slot, 1 - side)
-                remote(got, got, y_send.at[step, slot], y_recv.at[step, slot], me.beside).wait_recv()
-                remote(got, got, core_send.at[step, 1, slot], core_recv.at[step, 1, slot], me.twin).start()
-
-        @pl.loop(0, 2)
-        def _(turn):
-            ctx = me.ctx - 2 * step + (1 - turn) * (1 - 2 * side) - 2 * turn
-
-            @pl.when((turn == 0) & (step <= z))
-            def _():
-                from_twin(step, 1, 1 - side)
-
-            @pl.when((turn == 1) & (step + 1 <= z))
-            def _():
-                from_twin(step + 1, 0, side)
-
-            @pl.when((ctx >= 0) & (ctx < me.ctx))
-            def _():
-                attend(ctx, False)
+                got = rest(held(distance, slot, 1 - side))
+                remote(got, got, r_send.at[distance - 1, slot], r_recv.at[distance, slot], me.twin).wait_recv()
+                rest_twin(distance, slot).start()
+
+                @pl.when(z < top)
+                def _():
+                    rest_up(distance, slot).start()
+
+            from_twin(distance, 1, 1 - side, False)
+
+        @pl.when((turn % 2 == 0) & (distance <= z))
+        def _():
+            from_twin(distance, 0, side, True)
+
+        ctx = me.ctx - 2 * distance + (turn % 2) * (1 - 2 * side)
+
+        @pl.when((ctx >= 0) & (ctx < me.ctx))
+        def _():
+            attend(ctx, False)
 
     for head in range(3):
         part = slice(head * HD, head * HD + HD)
@@ -806,23 +882,32 @@
     for copy in exps + [two_c, two_f]:
         copy.wait()
 
-    @pl.loop(0, levels)
+    def left(distance, whole):
+        for slot in range(2):
+            got = held(distance, slot, side)
+
+            @pl.when(z < top)
+            def _():
+                remote(got, got, z_send.at[distance, slot], z_recv.at[distance, slot], me.twin).wait_send()
+                rest_up(distance, slot).wait_send()
+
+            y_copy(distance, slot, side, whole).wait_send()
+            remote(got, got, core_send.at[distance, 0, slot], core_recv.at[distance, 0, slot], me.twin).wait_send()
+            if not whole:
+                rest_twin(distance, slot).wait_send()
+                got = most(got)
+            remote(got, got, core_send.at[distance, 1, slot], core_recv.at[distance, 1, slot], me.twin).wait_send()
+
+    left(0, True)
+
+    @pl.loop(1, levels)
     def _(step):
         @pl.when(step <= z)
         def _():
-            for slot in range(2):
-                got = held(step, slot, side)
-
-                @pl.when(z < top)
-                def _():
-                    remote(got, got, z_send.at[step, slot], z_recv.at[step, slot], me.twin).wait_send()
-
-                remote(got, got, y_send.at[step, slot], y_recv.at[step, slot], me.beside).wait_send()
-                for which in range(2):
-                    remote(got, got, core_send.at[step, which, slot], core_recv.at[step, which, slot], me.twin).wait_send()
-
-
-def gather_attend(starts, tokens, vectors, attend_weight, expand_weight, cotangent):
+            left(step, False)
+
+
+def gather_attend(starts, tokens, attend_weight, expand_weight, cotangent, vectors):
     levels = lax.axis_size("ctx") // 2
     rows = tokens.shape[0]
     block = rows * 4
@@ -831,7 +916,7 @@
     dma = pltpu.SemaphoreType.DMA
     return pl.pallas_call(
         functools.partial(gather_attend_kernel, levels),
-        in_specs=[pl.BlockSpec(memory_space=pltpu.SMEM), vmem, vmem, vmem, pl.BlockSpec(memory_space=pl.ANY), vmem],
+        in_specs=[pl.BlockSpec(memory_space=pltpu.SMEM)] + [pl.BlockSpec(memory_space=pl.ANY)] * 11,
         out_specs=[vmem] * 10,
         out_shape=[
             jax.ShapeDtypeStruct((length, D), BF),
@@ -846,6 +931,10 @@
             jax.ShapeDtypeStruct((8, block), F32),
         ],
         scratch_shapes=[
+            pltpu.VMEM((rows, D), BF),
+            pltpu.VMEM((rows, 3 * D), BF),
+            pltpu.VMEM((rows, D), BF),
+            pltpu.VMEM((8, 192), F32),
             pltpu.VMEM((4, rows, 576), BF),
             pltpu.VMEM((4, 8, 192), F32),
             pltpu.VMEM((1, block), jnp.int32),
@@ -859,11 +948,14 @@
             dma((levels, 2)), dma((levels + 1, 2)),
             dma((levels, 2)), dma((levels, 2)),
             dma((levels, 2, 2)), dma((levels, 2, 2)),
-            dma((1,)),
-        ],
-        compiler_params=pltpu.CompilerParams(collective_id=4, has_side_effects=True, vmem_limit_bytes=48 << 20),
+            dma((levels, 2)), dma((levels + 1, 2)), dma((levels, 2)), dma((levels, 2)),
+            dma((11,)),
+            pltpu.VMEM((2 * rows,), BF),
+        ]
+        + [pltpu.VMEM((rows,), BF)] * 6,
+        compiler_params=pltpu.CompilerParams(collective_id=4, has_side_effects=True, vmem_limit_bytes=60 << 20),
         name="gather_attend",
-    )(starts, tokens, vectors, attend_weight, expand_weight, cotangent)
+    )(starts, tokens, attend_weight, expand_weight, cotangent, *vectors)
 
 
 def gelu_pair(t):
@@ -875,14 +967,23 @@
 
 
 def mlp_kernel(
-    o_ref, wp_ref, expand_ref, contract_ref, ebias_ref, tok_ref, cot_ref, gtwo_ref, vec_ref,
+    o_ref, wp_hbm, expand_ref, contract_hbm, ebias_hbm, tok_hbm, cot_hbm, gtwo_ref, vec_ref,
     block_out, gmid_out, gone_out, cpart_out, epart_out, sums_out,
-    o_rows, gact, n2, act, gexp, held, unit,
+    wp_ref, contract_ref, tok_ref, cot_ref, ebias_ref, bias_row, o_rows, gact, n2, act, gexp, held, unit,
     c_send_buf, c_recv_buf, x_send_buf, x_recv_buf,
-    c_send, c_recv, x_send, x_recv, ag_send, ag_recv,
+    c_send, c_recv, x_send, x_recv, ag_send, ag_recv, local_sem,
 ):
     me = Place()
     mine = me.part
+    fetched = [
+        pltpu.make_async_copy(source, target, local_sem.at[i])
+        for i, (source, target) in enumerate(
+            ((wp_hbm, wp_ref), (contract_hbm, contract_ref), (tok_hbm, tok_ref), (cot_hbm, cot_ref), (ebias_hbm, ebias_ref))
+        )
+    ]
+    for copy in fetched:
+        copy.start()
+    o_rows[...] = o_ref[...].T.astype(BF)
     barrier = pltpu.get_barrier_semaphore()
     signal(barrier, me.twin)
     signal(barrier, me.across)
@@ -928,11 +1029,14 @@
         got = rows_of(ref, p_corner)
         remote(got, got, ag_send.at[i, 2], ag_recv.at[i, 2], me.twin).wait_recv()
 
-    o_rows[...] = o_ref[...].T.astype(BF)
+    fetched[0].wait()
     to_twin(0, 0, mm(part(o_rows, p_corner), wp_ref[...]))
     to_twin(0, 1, mm(part(o_rows, p_twin), wp_ref[...]))
     value = mm(part(o_rows, p_across), wp_ref[...])
     to_across(0, value + from_twin(0, 0))
+    for copy in fetched[1:]:
+        copy.wait()
+    bias_row[...] = ebias_ref[...].astype(F32).reshape(1, D)
     for p in range(4):
         gact[p * 192 : p * 192 + 192, :] = mm_nt(gtwo_ref[p * 192 : p * 192 + 192, :], contract_ref[...])
     value = mm(part(o_rows, mine), wp_ref[...]) + from_twin(0, 1)
@@ -946,7 +1050,7 @@
 
     def through(p):
         at = pl.ds(pl.multiple_of(p * 192, 192), 192)
-        expanded = mm(n2[at, :], expand_ref[...]) + ebias_ref[...]
+        expanded = mm(n2[at, :], expand_ref[...]) + bias_row[...]
         activation, slope = gelu_pair(expanded)
         act[at, :] = activation.astype(BF)
         low = (gact[at, :] * slope).astype(BF)
@@ -1006,10 +1110,11 @@
     rows = tokens.shape[0]
     block = rows * 4
     vmem = pl.BlockSpec(memory_space=pltpu.VMEM)
+    anywhere = pl.BlockSpec(memory_space=pl.ANY)
     dma = pltpu.SemaphoreType.DMA
     return pl.pallas_call(
         mlp_kernel,
-        in_specs=[vmem] * 9,
+        in_specs=[vmem, anywhere, vmem, anywhere, anywhere, anywhere, anywhere, vmem, vmem],
         out_specs=[vmem] * 6,
         out_shape=[
             jax.ShapeDtypeStruct((rows, D), BF),
@@ -1020,6 +1125,12 @@
             jax.ShapeDtypeStruct((8, D), F32),
         ],
         scratch_shapes=[
+            pltpu.VMEM((192, D), BF),
+            pltpu.VMEM((D, D), BF),
+            pltpu.VMEM((rows, D), BF),
+            pltpu.VMEM((rows, D), BF),
+            pltpu.VMEM((D,), BF),
+            pltpu.VMEM((1, D), F32),
             pltpu.VMEM((block, 192), BF),
             pltpu.VMEM((block, D), F32),
             pltpu.VMEM((block, D), BF),
@@ -1031,9 +1142,9 @@
             pltpu.VMEM((3, 2, rows, D), BF),
             pltpu.VMEM((3, rows, D), BF),
             pltpu.VMEM((3, rows, D), BF),
-            dma((3, 2)), dma((3, 2)), dma((3,)), dma((3,)), dma((2, 3)), dma((2, 3)),
+            dma((3, 2)), dma((3, 2)), dma((3,)), dma((3,)), dma((2, 3)), dma((2, 3)), dma((5,)),
         ],
-        compiler_params=pltpu.CompilerParams(collective_id=2, has_side_effects=True, vmem_limit_bytes=48 << 20),
+        compiler_params=pltpu.CompilerParams(collective_id=2, has_side_effects=True, vmem_limit_bytes=58 << 20),
         name="feed_forward",
     )(o, wp, expand, contract, ebias, tokens, cotangent, gtwo, vectors)
 
@@ -1140,16 +1251,16 @@
 
 
 def attend_reduce_kernel(
-    levels, starts_ref, all_ref, k_ref, v_ref, q_ref, o_ref, lse_ref, g_ref, wp_ref, aw_ref,
-    c_ref, e_ref, tok_ref, gmid_ref, vec_ref, sums_ref,
-    tg_out, cg_out, eg_out, ag_out, pg_out, vec_out, hid_out,
-    rows_in, keys_in, values_in, begins, qm, dm, qn, dn, delta, dqt, kt, dk, dv, gt, a_part, p_part,
-    dnb, far, keep, x_out, x_in, y_out, y_in, d_out, d_in,
-    yc, ye, ya, yp, zc_out, ze_out, za_out, zp_out, zc_in, ze_in, za_in, zp_in, v_out, v_in, e_move, a_move, a_rows,
+    levels, starts_ref, all_ref, k_ref, v_ref, q_ref, o_ref, lse_ref, g_ref, wp_hbm, aw_ref,
+    c_ref, e_ref, tok_hbm, gmid_ref, vec_ref, sums_ref,
+    tg_out, cg_out, eg_out, a_rows, pg_out, vec_out,
+    wp_ref, tok_ref, rows_in, keys_in, values_in, begins, qm, dm, qn, dn, delta, dqt, kt, dk, dv, gt, a_part, p_part,
+    dnb, far, keep, x_in, y_out, y_in, d_out, d_in,
+    yc, ye, ya, yp, zc_out, ze_out, za_out, zp_out, zc_in, ze_in, za_in, zp_in, v_out, v_in, e_move, a_move,
     pre_sem, far_send, far_recv, x_send, x_recv, y_send, y_recv, d_send, d_recv,
     gy_send, gy_recv, gz_send, gz_recv, ay_send, ay_recv, az_send, az_recv,
     me_send, me_recv, ma_send, ma_recv, u_send, u_recv, w_send, w_recv,
-    be_send, be_recv, ba_send, ba_recv, te_send, te_recv, ta_send, ta_recv, v_send, v_recv,
+    be_send, be_recv, ba_send, ba_recv, te_send, te_recv, ta_send, ta_recv, v_send, v_recv, local_sem,
 ):
     me = Place()
     z, side, mine, ctx = me.level, me.side, me.part, me.ctx
@@ -1179,6 +1290,11 @@
             act(copy)
 
     all_of(prefetch(0), start)
+    fetched = (
+        pltpu.make_async_copy(wp_hbm, wp_ref, local_sem.at[0]),
+        pltpu.make_async_copy(tok_hbm, tok_ref, local_sem.at[1]),
+    )
+    all_of(fetched, start)
 
     def corner_of(ref, level, where):
         return ref.at[pl.ds(pl.multiple_of(level * 48, 48), 48), pl.ds(pl.multiple_of(where * 384, 128), 384)]
@@ -1198,6 +1314,7 @@
     grads_in = g_ref[...]
     exact = o_ref[...]
     p_part[...] = mm(exact.astype(BF), grads_in).astype(BF)
+    all_of(fetched, lambda copy: copy.wait())
     outer = mm_nt(grads_in, wp_ref[...]).astype(BF)
     pl.semaphore_wait(barrier, levels + 3)
     for step in range(levels - 1):
@@ -1288,7 +1405,7 @@
         )
 
     def x_copy(index):
-        return remote(x_out.at[index], x_in.at[index], x_send.at[index], x_recv.at[index], me.across)
+        return remote(far.at[index, 0], x_in.at[index], x_send.at[index], x_recv.at[index], me.across)
 
     def y_copy(level):
         return remote(y_out.at[level], y_in.at[level], y_send.at[level], y_recv.at[level], me.beside)
@@ -1304,9 +1421,9 @@
             own = dnb[slot, pl.ds(pl.multiple_of((half * 2 + me.core) * 192, 192), 192), :]
             return own.astype(F32) + far[index, half].astype(F32)
 
-        x_out[index] = rows(1 - me.half).astype(BF)
+        keep[index] = rows(me.half)
+        far[index, 0] = rows(1 - me.half).astype(BF)
         x_copy(index).start()
-        keep[index] = rows(me.half)
 
     def with_across(index):
         x_copy(index).wait_recv()
@@ -1561,29 +1678,13 @@
     total = v_in[3]
     for level in range(1, levels):
         total = total + v_in[3 + level]
-    v_out[4] = total
-    hid_out[...] = v_out[4, pl.ds(8 + mine, 1), :]
-    for part in range(4):
-
-        @pl.when(mine == part)
-        def _():
-            source, lane = part // 2, (part % 2) * 384
-            vec_out[0:1, :] = total[source : source + 1, lane : lane + 192]
-            vec_out[1:2, :] = total[source : source + 1, lane + 192 : lane + 384]
-            vec_out[2:8, :] = total[2:8, part * 192 : part * 192 + 192]
+    vec_out[...] = total
 
     for level in range(levels):
         all_of(side_copies(level, 1 - side), wait_recv)
     for flow in (e_flow, a_flow):
         for origin in range(4):
             flow.turn(origin, 1 - side).wait_recv()
-    for where in range(2):
-        for part in range(4):
-            for kind in range(3):
-                lane = kind * D + part * 192
-                ag_out[where * 96 : where * 96 + 96, lane : lane + 192] = a_rows[
-                    where, part, :, kind * 192 : kind * 192 + 192
-                ].astype(F32)
     grads.drain()
     attends.drain()
     e_flow.drain()
@@ -1636,28 +1737,28 @@
 
     return pl.pallas_call(
         functools.partial(attend_reduce_kernel, levels),
-        in_specs=[pl.BlockSpec(memory_space=pltpu.SMEM)] + [anywhere] * 3 + [vmem] * 12,
-        out_specs=[vmem] * 7,
+        in_specs=[pl.BlockSpec(memory_space=pltpu.SMEM)] + [anywhere] * 3 + [vmem] * 4 + [anywhere] + [vmem] * 3 + [anywhere] + [vmem] * 3,
+        out_specs=[vmem] * 6,
         out_shape=[
             jax.ShapeDtypeStruct((rows, D), BF),
             jax.ShapeDtypeStruct((2 * n, 96, D), BF),
             jax.ShapeDtypeStruct((192, 4 * D), BF),
-            jax.ShapeDtypeStruct((192, 3 * D), F32),
+            jax.ShapeDtypeStruct((2, 4, 96, 576), BF),
             jax.ShapeDtypeStruct((192, D), BF),
-            jax.ShapeDtypeStruct((8, 192), F32),
-            jax.ShapeDtypeStruct((1, D), F32),
+            jax.ShapeDtypeStruct((16, D), F32),
         ],
         scratch_shapes=[
+            buf(192, D), buf(rows, D),
             buf(2, block, D), buf(2, block, 192), buf(2, block, 192), pltpu.VMEM((1, block), jnp.int32),
             buf(3, 128, block), buf(3, 128, block), buf(3, block, 128), buf(3, block, 128),
             wide(8, block), wide(192, block), buf(192, block), wide(block, 192), wide(block, 192), wide(576, D),
             buf(2 * n, 96, 576), buf(192, D),
-            buf(3, block, D), buf(2 * n, 2, rows, D), wide(2 * n, rows, D), buf(2 * n, rows, D), buf(2 * n, rows, D),
+            buf(3, block, D), buf(2 * n, 2, rows, D), wide(2 * n, rows, D), buf(2 * n, rows, D),
             buf(n, rows, D), buf(n, rows, D), buf(n, rows, D), buf(n, rows, D),
             buf(n, 96, D), buf(n, 96, D), buf(n, 96, 576), buf(n, 48, 384),
             buf(n, 96, D), buf(n, 96, D), buf(n, 96, 576), buf(n, 48, 384),
             buf(n + 1, 96, D), buf(n + 1, 96, D), buf(n + 1, 96, 576), buf(n + 1, 48, 384),
-            wide(5, 16, D), wide(3 + n, 16, D), buf(96, D), buf(96, 576), buf(2, 4, 96, 576),
+            wide(4, 16, D), wide(3 + n, 16, D), buf(96, D), buf(96, 576),
             dma((2, 3)), dma((2 * n, 2)), dma((2 * n, 2)), dma((2 * n,)), dma((2 * n,)),
             dma((n,)), dma((n,)), dma((n,)), dma((n,)),
             dma((n, 3)), dma((n, 3)), dma((n, 3)), dma((n + 1, 3)),
@@ -1665,11 +1766,63 @@
             dma((1,)), dma((4,)), dma((1,)), dma((4,)),
             dma((2, n, 2)), dma((2, n, 2)), dma((n, 2)), dma((n, 2)),
             dma((2, 4)), dma((2, 4)), dma((2, 4)), dma((2, 4)), dma((4,)), dma((4,)), dma((4,)), dma((4,)),
-            dma((2 + n,)), dma((3 + n,)),
+            dma((2 + n,)), dma((3 + n,)), dma((2,)),
         ],
         compiler_params=pltpu.CompilerParams(collective_id=5, has_side_effects=True, vmem_limit_bytes=60 << 20),
         name="attend_reduce",
     )(starts, rows_all, k, v, q, o, lse, g, wp, aw, contract, expand, tokens, grad_middle, vectors, sums)
+
+
+def finish_kernel(
+    tg_ref, c_ref, e_ref, a_ref, p_ref, vec_ref, block_ref,
+    block_out, tg_out, a_out, ab_out, p_out, pb_out, e_out, hid_out, c_out, cb_out, gf_out, sf_out, gs_out, ss_out,
+):
+    mine = lax.axis_index("fsdp")
+    block_out[...] = block_ref[...]
+    tg_out[...] = tg_ref[...]
+    p_out[...] = p_ref[...].astype(F32)
+    e_out[...] = e_ref[...].astype(F32)
+    for chunk in range(8):
+        c_out[chunk * 96 : chunk * 96 + 96, :] = c_ref[chunk].astype(F32)
+    for where in range(2):
+        for part in range(4):
+            for kind in range(3):
+                lane = kind * D + part * 192
+                a_out[where * 96 : where * 96 + 96, lane : lane + 192] = a_ref[
+                    where, part, :, kind * 192 : kind * 192 + 192
+                ].astype(F32)
+    hid_out[...] = vec_ref[pl.ds(8 + mine, 1), :].reshape(D)
+    for part in range(4):
+
+        @pl.when(mine == part)
+        def _():
+            source, lane = part // 2, (part % 2) * 384
+            ab_out[...] = vec_ref[source : source + 1, lane : lane + 384].reshape(384)
+            for i, ref in enumerate((pb_out, cb_out, gf_out, sf_out, gs_out, ss_out)):
+                ref[...] = vec_ref[2 + i : 3 + i, part * 192 : part * 192 + 192].reshape(192)
+
+
+def finish(tokens_grad, contract, expand, attend, project, vectors, block_output):
+    rows = tokens_grad.shape[0]
+    one = jax.ShapeDtypeStruct((192,), F32)
+    return pl.pallas_call(
+        finish_kernel,
+        in_specs=[pl.BlockSpec(memory_space=pltpu.VMEM)] * 7,
+        out_shape=[
+            jax.ShapeDtypeStruct((rows, D), BF),
+            jax.ShapeDtypeStruct((rows, D), BF),
+            jax.ShapeDtypeStruct((192, 3 * D), F32),
+            jax.ShapeDtypeStruct((384,), F32),
+            jax.ShapeDtypeStruct((192, D), F32),
+            one,
+            jax.ShapeDtypeStruct((192, 4 * D), F32),
+            jax.ShapeDtypeStruct((D,), F32),
+            jax.ShapeDtypeStruct((D, D), F32),
+            one, one, one, one, one,
+        ],
+        compiler_params=pltpu.CompilerParams(vmem_limit_bytes=32 << 20),
+        name="finish",
+    )(tokens_grad, contract, expand, attend, project, vectors, block_output)
 
 
 def normalize(rows_in, gain, shift):
@@ -1732,12 +1885,9 @@
         return forward_plain(
             tokens, document_starts, attend_weight, attend_bias, expand_weight, cotangent, own_vectors
         )
-    listed = [attend_bias[:rows], attend_bias[rows:]] + list(own_vectors)
-    line = lax.broadcasted_iota(jnp.int32, (8, rows), 0)
-    vectors = jnp.zeros((8, rows), F32)
-    for i, vector in enumerate(listed):
-        vectors = jnp.where(line == i, vector.astype(F32)[None, :], vectors)
-    return gather_attend(document_starts, tokens, vectors, attend_weight, expand_weight, cotangent)
+    return gather_attend(
+        document_starts, tokens, attend_weight, expand_weight, cotangent, (attend_bias,) + tuple(own_vectors)
+    )
 
 
 def backward_plain(
@@ -1806,22 +1956,18 @@
         (project_bias, contract_bias, gain_first, shift_first, gain_second, shift_second),
     )
     block_output, grad_middle, g1, contract_part, expand_part, mlp_sums = feed_forward(
-        o, project_weight, expand_cols, contract_weight, expand_bias.astype(F32).reshape(1, D), tokens, cotangent, g2, vectors
+        o, project_weight, expand_cols, contract_weight, expand_bias, tokens, cotangent, g2, vectors
     )
     if lax.axis_size("ctx") != 8:
         return (block_output,) + backward_plain(
             document_starts, normed_all, k, v, q, o, lse, g1, project_weight, attend_cols,
             contract_part, expand_part, tokens, grad_middle, vectors, mlp_sums,
         )
-    tokens_grad, contract_grad, expand_grad, attend_grad, project_grad, small, hidden = attend_reduce(
+    reduced = attend_reduce(
         document_starts, normed_all, k, v, q, o, lse, g1, project_weight, attend_cols,
         contract_part.reshape(8, 96, D), expand_part.reshape(8, 96, D), tokens, grad_middle, vectors, mlp_sums,
     )
-    return (
-        block_output, tokens_grad, attend_grad, small[:2].reshape(-1), project_grad.astype(F32), small[2],
-        expand_grad.astype(F32), hidden.reshape(-1), contract_grad.reshape(D, D).astype(F32),
-        small[3], small[4], small[5], small[6], small[7],
-    )
+    return tuple(finish(*reduced, block_output))
 
 
 def solution(mesh):

time: 311 us -> 292 us (0.939)
  other arithmetic: 12 us -> 0 us
  local copies, waits for them, and re-layouts: 18.1 us -> 6.46 us
  Pallas kernels: 276 us -> 281 us
    convert_element_type x10 -> x0, other arithmetic: 11.3 us -> none  [the longest x7 4.77 us: forward(): vectors = jnp.where(line == i, vector.astype(F32)[None, :], vectors)]
    unnamed x51 -> x14, local copies, waits for them, and re-layouts: 15.2 us -> 6.46 us
    pallas_call x1 -> x2, Pallas kernels: 48.2 us -> 53.6 us  [the longest x1 49.8 us: feed_forward(): pl.pallas_call(mlp_kernel, in_specs=[vmem, anywhere, vmem, anywhere, anyw...]
where the time goes in v4:
time: 292 us; the launch traced here: 288 us
  Pallas kernels  281 us (96%)
  local copies, waits for them, and re-layouts  6.46 us (2%)
    pallas_call x1, Pallas kernels, attend_reduce(): pl.pallas_call(functools.partial(attend_reduce_kernel, levels), in_specs=...  179 us
    pallas_call x1, Pallas kernels, feed_forward(): pl.pallas_call(mlp_kernel, in_specs=[vmem, anywhere, vmem, anywhere, anyw...  49.8 us
    pallas_call x1, Pallas kernels, gather_attend(): pl.pallas_call(functools.partial(gather_attend_kernel, levels), in_specs=...  48.1 us
    unnamed x14, local copies, waits for them, and re-layouts  6.46 us

profile of v4, /device:TPU:3, one launch (start us, length us, event | category | flops | bytes accessed | tf_op | source)
XLA Modules:
  0.0 288.0 jit_solution(5189307196229315853)
XLA Ops:
  0.6 48.1 %gather_attend.1 = (bf16[6144,768]{1,0:T(8,128)(2,1)}, bf16[768,576]{1,0:T(8,128)(2,1)}, bf16[768,768]{1,0:T(8,128)(2,1)}, bf16[768,768]{1,0:T(8,128)(2,1)}, f32...) custom-call(s32[8]{0:T(128)} %starts_ref.3, ...), custom_call_target="tpu_custom_call" | custom-call | tf_op jit(solution)/shard_map/gather_attend/pallas_call | solution.py:917
  48.8 49.8 %feed_forward.1 = (bf16[192,768]{1,0:T(8,128)(2,1)}, f32[192,768]{1,0:T(8,128)}, bf16[768,768]{1,0:T(8,128)(2,1)}, bf16[768,768]{1,0:T(8,128)(2,1)}, bf16[768,768]{1,0:T(8,128)(2,1)}, /*index=5*/f32[8,768]{1,0:T(8,128)}) custom-call(f32[192,768]{1,0:T(8,128)} %get-tuple-element.40.o_ref, bf16[192,768]{1,0:T(8,128)(2,1)} %wp_hbm.3, ...), custom_call_target="tpu_custom_call" | custom-call | tf_op jit(solution)/shard_map/feed_forward/pallas_call | solution.py:1115
  98.6 0.0 copy-start.3
  98.6 179.1 %attend_reduce.1 = (bf16[192,768]{1,0:T(8,128)(2,1)}, bf16[8,96,768]{2,1,0:T(8,128)(2,1)}, bf16[192,3072]{1,0:T(8,128)(2,1)}, bf16[2,4,96,576]{3,2,1,0:T(8,128)(...) custom-call(s32[8]{0:T(128)} %starts_ref.3, bf16[6144,768]{1,0:T(8,128)(2,1)} %get-tuple-element.36.all_ref, ...), custom_call_target="tpu_custom_call" | custom-call | tf_op jit(solution)/shard_map/attend_reduce/pallas_call | solution.py:1738
  277.7 0.0 copy-done.3
  277.7 0.0 copy-start
  277.7 1.3 copy-done
  279.0 0.0 copy-start.1
  279.0 1.3 copy-done.1
  280.3 0.0 copy-start.2
  280.3 1.2 copy-done.2
  281.5 0.0 copy-start.4
  281.5 1.0 copy-done.4
  282.4 0.0 copy-start.5
  282.4 1.0 copy-done.5
  283.4 0.0 copy-start.6
  283.4 0.8 copy-done.6
  284.2 3.8 %finish.1 = (bf16[192,768]{1,0:T(8,128)(2,1)}, bf16[192,768]{1,0:T(8,128)(2,1)}, f32[192,2304]{1,0:T(8,128)}, f32[384]{0:T(512)}, f32[192,768]{1,0:T(8,128)}, /*...) custom-call(bf16[192,768]{1,0:T(8,128)(2,1)S(1)} %copy-done.4, ...), custom_call_target="tpu_custom_call" | custom-call | tf_op jit(solution)/shard_map/finish/pallas_call | solution.py:1808
Async XLA Ops:
  98.6 179.2 %copy-start.3 = (bf16[192,768]{1,0:T(8,128)(2,1)S(1)}, bf16[192,768]{1,0:T(8,128)(2,1)}, u32[]{:S(2)}) copy-start(bf16[192,768]{1,0:T(8,128)(2,1)} %get-tuple-element.57.block_ref) | copy-start | bytes 884740
  277.7 1.3 copy-start
  279.0 1.3 copy-start.1
  280.3 1.2 copy-start.2
  281.5 1.0 copy-start.4
  282.4 1.0 copy-start.5
  283.4 0.8 copy-start.6

commit v5 on v4

--- a/solution.py
+++ b/solution.py
@@ -1149,6 +1149,32 @@
     )(o, wp, expand, contract, ebias, tokens, cotangent, gtwo, vectors)
 
 
+ORDERS = (
+    (
+        "g0", "A0", "A1", "g1", "g2", "W0", "d0", "X0", "d1", "s0", "s1", "W1",
+        "gf", "X1", "E", "d2", "dn", "s2", "v0", "r1", "v1", "af", "r2", "v2",
+        "r3", "a", "v3",
+    ),
+    (
+        "A0", "g0", "d0", "A1", "W0", "d1", "A2", "W1", "A3", "g1", "W2", "X0",
+        "g2", "X1", "gf", "s0", "r1", "X2", "W3", "X3", "d2", "s1", "E", "s2",
+        "r2", "dn", "af", "a", "v0", "v1", "v2", "r3", "v3",
+    ),
+    (
+        "A0", "A1", "W0", "W1", "A2", "g0", "W2", "A3", "X0", "g1", "X1", "W3",
+        "X2", "d0", "g2", "A4", "gf", "A5", "s0", "d1", "r1", "W4", "X3", "X4",
+        "W5", "E", "d2", "r2", "r3", "s1", "s2", "X5", "af", "dn", "v0", "a",
+        "v1", "v2", "v3",
+    ),
+    (
+        "A0", "A1", "W0", "g0", "A2", "X0", "W1", "A3", "X1", "g1", "W2", "A4",
+        "W3", "g2", "d0", "X2", "A5", "W4", "X3", "gf", "A6", "W5", "X4", "A7",
+        "W6", "d1", "W7", "s0", "X5", "X6", "E", "s1", "d2", "X7", "s2", "dn",
+        "v0", "r1", "r2", "af", "v1", "r3", "v2", "a", "v3",
+    ),
+)
+
+
 class Exchange:
     def __init__(self, me, levels, items, y_send, y_recv, z_send, z_recv):
         self.me, self.top, self.items = me, levels - 1, items
@@ -1571,107 +1597,156 @@
     e_flow = Rows(e_move, e_chunk, me_send, me_recv, be_send, be_recv, te_send, te_recv)
     a_flow = Rows(a_move, a_chunk, ma_send, ma_recv, ba_send, ba_recv, ta_send, ta_recv)
 
-    @pl.loop(0, 2 * levels + 3)
-    def _(turn):
-        @pl.when(turn <= ctx)
+    def finish_rows():
+        @pl.when(side == 0)
+        def _():
+            with_beside(z)
+
+        @pl.when(z < top)
+        def _():
+            down_copy(z).wait_recv()
+            keep[ctx] += d_in[z].astype(F32)
+
+        grad = keep[ctx]
+        gain = vec_ref[4:5, :]
+        normed, unit, inverse = layer_norm(tok_ref[...].astype(F32), gain, vec_ref[5:6, :])
+        scaled = grad * gain
+        spread = (
+            scaled - jnp.mean(scaled, axis=1, keepdims=True) - unit * jnp.mean(scaled * unit, axis=1, keepdims=True)
+        )
+        tg_out[...] = (gmid_ref[...] + inverse * spread).astype(BF)
+        for part in range(4):
+
+            @pl.when(mine == part)
+            def _():
+                v_out[0, 0:1, part * 192 : part * 192 + 192] = v_out[0, 13:14, 0:192]
+                v_out[0, 1:2, part * 192 : part * 192 + 192] = v_out[0, 12:13, 0:192]
+                v_out[0, 8 + part : 9 + part, :] = sums_ref[4:5, :]
+
+        v_out[0, 12:16, :] = jnp.zeros((4, D), F32)
+        v_out[0, 2:4, :] = sums_ref[0:2, :]
+        v_out[0, 4:5, :] = jnp.sum(grad * unit, axis=0, keepdims=True)
+        v_out[0, 5:6, :] = jnp.sum(grad, axis=0, keepdims=True)
+        v_out[0, 6:8, :] = sums_ref[2:4, :]
+
+    def v_copy(i):
+        return remote(v_out.at[i], v_in.at[i], v_send.at[i], v_recv.at[i], (me.twin, me.across, me.beside)[i])
+
+    def vectors_on(i):
+        if i > 0:
+            v_copy(i - 1).wait_recv()
+            v_out[i] = v_out[i - 1] + v_in[i - 1]
+        if i < 3:
+            v_copy(i).start()
+        else:
+            v_in[3 + z] = v_out[3]
+            for step in range(1, levels):
+                remote(
+                    v_out.at[3], v_in.at[3 + z], v_send.at[2 + step], v_recv.at[3 + z], me.at(level=(z + step) % levels)
+                ).start()
+
+
+    def slot_of(name):
+        spots = [order.index(name) if name in order else -1 for order in ORDERS]
+        spot = jnp.int32(spots[0])
+        for level in range(1, levels):
+            spot = jnp.where(z == level, jnp.int32(spots[level]), spot)
+        return spot
+
+    def spots_of(kind, count):
+        return [slot_of(kind + str(i)) for i in range(count)]
+
+    spots = {kind: spots_of(kind, count) for kind, count in (("A", 8), ("W", 8), ("X", 8), ("g", 3), ("d", 3), ("s", 3), ("v", 4))}
+    spots["r"] = [slot_of("r" + str(i + 1)) for i in range(3)]
+    single = {name: slot_of(name) for name in ("gf", "af", "dn", "E", "a")}
+
+    @pl.loop(0, max(len(order) for order in ORDERS))
+    def _(slot):
+        def number(kind):
+            found = jnp.int32(-1)
+            for i, spot in enumerate(spots[kind]):
+                found = jnp.where(slot == spot, jnp.int32(i), found)
+            return found
+
+        turn = number("A")
+
+        @pl.when((turn >= 0) & (turn <= ctx))
         def _():
             all_of(prefetch(turn), lambda copy: copy.wait())
 
-        @pl.when(turn + 1 <= ctx)
-        def _():
-            all_of(prefetch(turn + 1), start)
-
-        @pl.when(turn < ctx)
-        def _():
-            attend(turn, False)
-
-        @pl.when(turn == ctx)
-        def _():
-            attend(turn, True)
-            flipped = gt[...].T.astype(BF)
-            for chunk in range(8):
-                a_part[chunk] = flipped[chunk * 96 : chunk * 96 + 96]
-            for step in range(levels - 1):
-                attends.steps(step, lambda level, way: attends.beside(level, start))
-            attends.beside(z, start)
-
-        @pl.when(turn <= ctx)
-        def _():
+            @pl.when(turn + 1 <= ctx)
+            def _():
+                all_of(prefetch(turn + 1), start)
+
+            @pl.when(turn < ctx)
+            def _():
+                attend(turn, False)
+
+            @pl.when(turn == ctx)
+            def _():
+                attend(turn, True)
+                flipped = gt[...].T.astype(BF)
+                for chunk in range(8):
+                    a_part[chunk] = flipped[chunk * 96 : chunk * 96 + 96]
+                for step in range(levels - 1):
+                    attends.steps(step, lambda level, way: attends.beside(level, start))
+                attends.beside(z, start)
+
             all_of(to_twin(turn), start)
 
-        @pl.when((turn >= 1) & (turn - 1 <= ctx))
-        def _():
-            with_twin(turn - 1)
-
-        @pl.when((turn % 2 == 1) & (turn < 2 * levels - 1))
-        def _():
-            grads.step(turn // 2)
-
-        @pl.when(turn == 2 * levels - 1)
+        after = number("W")
+
+        @pl.when((after >= 0) & (after <= ctx))
+        def _():
+            with_twin(after)
+
+        last = number("X")
+
+        @pl.when((last >= 0) & (last <= ctx))
+        def _():
+            with_across(last)
+
+        for kind, act in (("g", grads.step), ("d", dn_step), ("s", attends.step)):
+            step = number(kind)
+
+            @pl.when(step >= 0)
+            def _():
+                act(step)
+
+        distance = number("r")
+
+        @pl.when(distance >= 0)
+        def _():
+            arrivals(distance + 1)
+
+        @pl.when(slot == single["gf"])
         def _():
             grads.final((cg_out.at[ctx], e_move, corner_of(pg_out, z, side)))
             e_flow.begin()
             pass_on(0, 2)
 
-        @pl.when((turn >= 3) & (turn - 3 <= ctx))
-        def _():
-            with_across(turn - 3)
-
-        @pl.when((turn >= 6) & (turn % 2 == 0))
-        def _():
-            dn_step((turn - 6) // 2)
-
-    attends.step(0)
-    arrivals(1)
-    attends.step(1)
-    for origin in range(4):
-        e_flow.spread(origin)
-    attends.step(2)
-    arrivals(2)
-    attends.final((a_move,))
-    a_flow.begin()
-
-    @pl.when(side == 0)
-    def _():
-        with_beside(z)
-
-    @pl.when(z < top)
-    def _():
-        down_copy(z).wait_recv()
-        keep[ctx] += d_in[z].astype(F32)
-
-    grad = keep[ctx]
-    gain = vec_ref[4:5, :]
-    normed, unit, inverse = layer_norm(tok_ref[...].astype(F32), gain, vec_ref[5:6, :])
-    scaled = grad * gain
-    spread = (
-        scaled - jnp.mean(scaled, axis=1, keepdims=True) - unit * jnp.mean(scaled * unit, axis=1, keepdims=True)
-    )
-    tg_out[...] = (gmid_ref[...] + inverse * spread).astype(BF)
-    for part in range(4):
-
-        @pl.when(mine == part)
-        def _():
-            v_out[0, 0:1, part * 192 : part * 192 + 192] = v_out[0, 13:14, 0:192]
-            v_out[0, 1:2, part * 192 : part * 192 + 192] = v_out[0, 12:13, 0:192]
-            v_out[0, 8 + part : 9 + part, :] = sums_ref[4:5, :]
-
-    v_out[0, 12:16, :] = jnp.zeros((4, D), F32)
-    v_out[0, 2:4, :] = sums_ref[0:2, :]
-    v_out[0, 4:5, :] = jnp.sum(grad * unit, axis=0, keepdims=True)
-    v_out[0, 5:6, :] = jnp.sum(grad, axis=0, keepdims=True)
-    v_out[0, 6:8, :] = sums_ref[2:4, :]
-    for origin in range(4):
-        a_flow.spread(origin)
-    for i, device in enumerate((me.twin, me.across, me.beside)):
-        copy = remote(v_out.at[i], v_in.at[i], v_send.at[i], v_recv.at[i], device)
-        copy.start()
-        copy.wait_recv()
-        v_out[i + 1] = v_out[i] + v_in[i]
-    v_in[3 + z] = v_out[3]
-    for step in range(1, levels):
-        remote(v_out.at[3], v_in.at[3 + z], v_send.at[2 + step], v_recv.at[3 + z], me.at(level=(z + step) % levels)).start()
-    arrivals(3)
+        @pl.when(slot == single["af"])
+        def _():
+            attends.final((a_move,))
+            a_flow.begin()
+
+        for name, flow in (("E", e_flow), ("a", a_flow)):
+
+            @pl.when(slot == single[name])
+            def _():
+                for origin in range(4):
+                    flow.spread(origin)
+
+        @pl.when(slot == single["dn"])
+        def _():
+            finish_rows()
+
+        for i in range(4):
+
+            @pl.when(slot == spots["v"][i])
+            def _():
+                vectors_on(i)
+
     for step in range(1, levels):
         level = (z + step) % levels
         remote(v_out.at[3], v_in.at[3 + level], v_send.at[2 + step], v_recv.at[3 + level], me.twin).wait_recv()

time: 292 us -> 274 us (0.938)
  Pallas kernels: 281 us -> 263 us
    pallas_call x1, Pallas kernels: 179 us -> 162 us  [attend_reduce(): pl.pallas_call(functools.partial(attend_reduce_kernel, levels), in_specs=...]
where the time goes in v5:
time: 274 us; the launch traced here: 271 us
  Pallas kernels  263 us (96%)
  local copies, waits for them, and re-layouts  6.46 us (2%)
    pallas_call x1, Pallas kernels, attend_reduce(): pl.pallas_call(functools.partial(attend_reduce_kernel, levels), in_specs=...  162 us
    pallas_call x1, Pallas kernels, feed_forward(): pl.pallas_call(mlp_kernel, in_specs=[vmem, anywhere, vmem, anywhere, anyw...  49.8 us
    pallas_call x1, Pallas kernels, gather_attend(): pl.pallas_call(functools.partial(gather_attend_kernel, levels), in_specs=...  48.1 us
    unnamed x14, local copies, waits for them, and re-layouts  6.46 us

profile of v5, /device:TPU:3, one launch (start us, length us, event | category | flops | bytes accessed | tf_op | source)
XLA Modules:
  0.0 270.6 jit_solution(16773707243264350692)
XLA Ops:
  0.6 48.1 %gather_attend.1 = (bf16[6144,768]{1,0:T(8,128)(2,1)}, bf16[768,576]{1,0:T(8,128)(2,1)}, bf16[768,768]{1,0:T(8,128)(2,1)}, bf16[768,768]{1,0:T(8,128)(2,1)}, f32...) custom-call(s32[8]{0:T(128)} %starts_ref.3, ...), custom_call_target="tpu_custom_call" | custom-call | tf_op jit(solution)/shard_map/gather_attend/pallas_call | solution.py:917
  48.8 49.8 %feed_forward.1 = (bf16[192,768]{1,0:T(8,128)(2,1)}, f32[192,768]{1,0:T(8,128)}, bf16[768,768]{1,0:T(8,128)(2,1)}, bf16[768,768]{1,0:T(8,128)(2,1)}, bf16[768,768]{1,0:T(8,128)(2,1)}, /*index=5*/f32[8,768]{1,0:T(8,128)}) custom-call(f32[192,768]{1,0:T(8,128)} %get-tuple-element.40.o_ref, bf16[192,768]{1,0:T(8,128)(2,1)} %wp_hbm.3, ...), custom_call_target="tpu_custom_call" | custom-call | tf_op jit(solution)/shard_map/feed_forward/pallas_call | solution.py:1115
  98.6 0.0 copy-start.3
  98.6 161.7 %attend_reduce.1 = (bf16[192,768]{1,0:T(8,128)(2,1)}, bf16[8,96,768]{2,1,0:T(8,128)(2,1)}, bf16[192,3072]{1,0:T(8,128)(2,1)}, bf16[2,4,96,576]{3,2,1,0:T(8,128)(...) custom-call(s32[8]{0:T(128)} %starts_ref.3, bf16[6144,768]{1,0:T(8,128)(2,1)} %get-tuple-element.36.all_ref, ...), custom_call_target="tpu_custom_call" | custom-call | tf_op jit(solution)/shard_map/attend_reduce/pallas_call | solution.py:1813
  260.3 0.0 copy-done.3
  260.3 0.0 copy-start
  260.3 1.3 copy-done
  261.6 0.0 copy-start.1
  261.6 1.3 copy-done.1
  262.9 0.0 copy-start.2
  262.9 1.2 copy-done.2
  264.1 0.0 copy-start.4
  264.1 1.0 copy-done.4
  265.0 0.0 copy-start.5
  265.0 1.0 copy-done.5
  266.0 0.0 copy-start.6
  266.0 0.8 copy-done.6
  266.8 3.8 %finish.1 = (bf16[192,768]{1,0:T(8,128)(2,1)}, bf16[192,768]{1,0:T(8,128)(2,1)}, f32[192,2304]{1,0:T(8,128)}, f32[384]{0:T(512)}, f32[192,768]{1,0:T(8,128)}, /*...) custom-call(bf16[192,768]{1,0:T(8,128)(2,1)S(1)} %copy-done.4, ...), custom_call_target="tpu_custom_call" | custom-call | tf_op jit(solution)/shard_map/finish/pallas_call | solution.py:1883
Async XLA Ops:
  98.6 161.7 %copy-start.3 = (bf16[192,768]{1,0:T(8,128)(2,1)S(1)}, bf16[192,768]{1,0:T(8,128)(2,1)}, u32[]{:S(2)}) copy-start(bf16[192,768]{1,0:T(8,128)(2,1)} %get-tuple-element.57.block_ref) | copy-start | bytes 884740
  260.3 1.3 copy-start
  261.6 1.3 copy-start.1
  262.9 1.2 copy-start.2
  264.1 1.0 copy-start.4
  265.0 1.0 copy-start.5
  266.0 0.8 copy-start.6

commit v6 on v5

--- a/solution.py
+++ b/solution.py
@@ -1149,6 +1149,190 @@
     )(o, wp, expand, contract, ebias, tokens, cotangent, gtwo, vectors)
 
 
+def mlp_near_kernel(
+    o_ref, wp_hbm, expand_ref, contract_hbm, ebias_hbm, tok_hbm, cot_hbm, gtwo_ref, vec_ref,
+    block_out, over_out, gmid_out, gone_out, cpart_out, epart_out, sums_out,
+    wp_ref, contract_ref, tok_ref, cot_ref, ebias_ref, bias_row, o_rows, gact, n2, act, gexp, held, unit,
+    c_send_buf, c_recv_buf, x_send_buf, x_recv_buf,
+    c_send, c_recv, x_send, x_recv, ag_send, ag_recv, local_sem,
+):
+    me = Place()
+    mine = me.part
+    fetched = [
+        pltpu.make_async_copy(source, target, local_sem.at[i])
+        for i, (source, target) in enumerate(
+            ((wp_hbm, wp_ref), (contract_hbm, contract_ref), (tok_hbm, tok_ref), (cot_hbm, cot_ref), (ebias_hbm, ebias_ref))
+        )
+    ]
+    for copy in fetched:
+        copy.start()
+    o_rows[...] = o_ref[...].T.astype(BF)
+    barrier = pltpu.get_barrier_semaphore()
+    signal(barrier, me.twin)
+    signal(barrier, me.across)
+    pl.semaphore_wait(barrier, 2)
+    p_across = (1 - me.half) * 2 + me.core
+    p_twin = me.half * 2 + 1 - me.core
+    p_corner = (1 - me.half) * 2 + 1 - me.core
+
+    def part(ref, p):
+        return ref[pl.ds(pl.multiple_of(p * 192, 192), 192), :]
+
+    def to_twin(i, slot, value):
+        c_send_buf[i, slot] = value.astype(BF)
+        remote(c_send_buf.at[i, slot], c_recv_buf.at[i, slot], c_send.at[i, slot], c_recv.at[i, slot], me.twin).start()
+
+    def from_twin(i, slot):
+        remote(c_send_buf.at[i, slot], c_recv_buf.at[i, slot], c_send.at[i, slot], c_recv.at[i, slot], me.twin).wait_recv()
+        return c_recv_buf[i, slot].astype(F32)
+
+    def to_across(i, value):
+        x_send_buf[i] = value.astype(BF)
+        remote(x_send_buf.at[i], x_recv_buf.at[i], x_send.at[i], x_recv.at[i], me.across).start()
+
+    def from_across(i):
+        remote(x_send_buf.at[i], x_recv_buf.at[i], x_send.at[i], x_recv.at[i], me.across).wait_recv()
+        return x_recv_buf[i].astype(F32)
+
+    def share(i, ref):
+        own = rows_of(ref, mine)
+        remote(own, own, ag_send.at[i, 0], ag_recv.at[i, 0], me.across).start()
+        remote(own, own, ag_send.at[i, 1], ag_recv.at[i, 1], me.twin).start()
+
+    def share_across(i, ref):
+        got = rows_of(ref, p_across)
+        remote(got, got, ag_send.at[i, 0], ag_recv.at[i, 0], me.across).wait_recv()
+        remote(got, got, ag_send.at[i, 2], ag_recv.at[i, 2], me.twin).start()
+
+    def share_twin(i, ref):
+        got = rows_of(ref, p_twin)
+        remote(got, got, ag_send.at[i, 1], ag_recv.at[i, 1], me.twin).wait_recv()
+
+    def share_corner(i, ref):
+        got = rows_of(ref, p_corner)
+        remote(got, got, ag_send.at[i, 2], ag_recv.at[i, 2], me.twin).wait_recv()
+
+    fetched[0].wait()
+    to_twin(0, 0, mm(part(o_rows, p_corner), wp_ref[...]))
+    to_twin(0, 1, mm(part(o_rows, p_twin), wp_ref[...]))
+    value = mm(part(o_rows, p_across), wp_ref[...])
+    to_across(0, value + from_twin(0, 0))
+    for copy in fetched[1:]:
+        copy.wait()
+    bias_row[...] = ebias_ref[...].astype(F32).reshape(1, D)
+    for p in range(4):
+        gact[p * 192 : p * 192 + 192, :] = mm_nt(gtwo_ref[p * 192 : p * 192 + 192, :], contract_ref[...])
+    value = mm(part(o_rows, mine), wp_ref[...]) + from_twin(0, 1)
+    value = value + from_across(0)
+    middle = tok_ref[...].astype(F32) + BRANCH * (value + vec_ref[2:3, :])
+    out, unit_two, inverse = layer_norm(middle, vec_ref[6:7, :], vec_ref[7:8, :])
+    n2[pl.ds(pl.multiple_of(mine * 192, 192), 192), :] = out.astype(BF)
+    share(0, n2)
+    unit[...] = unit_two
+    held[...] = middle
+
+    def through(p):
+        at = pl.ds(pl.multiple_of(p * 192, 192), 192)
+        expanded = mm(n2[at, :], expand_ref[...]) + bias_row[...]
+        activation, slope = gelu_pair(expanded)
+        act[at, :] = activation.astype(BF)
+        low = (gact[at, :] * slope).astype(BF)
+        gexp[at, :] = low
+        return mm_nt(low, expand_ref[...])
+
+    own_value = through(mine)
+    share_twin(0, n2)
+    to_twin(1, 1, through(p_twin))
+    share_across(0, n2)
+    across_value = through(p_across)
+    share_corner(0, n2)
+    to_twin(1, 0, through(p_corner))
+    to_across(1, across_value + from_twin(1, 0))
+    own_value = own_value + from_twin(1, 1)
+    to_twin(2, 0, mm(part(act, p_corner), contract_ref[...]))
+    to_twin(2, 1, mm(part(act, p_twin), contract_ref[...]))
+    cpart_out[...] = mm_tn(act[...], gtwo_ref[...]).astype(BF)
+    grad = own_value + from_across(1)
+    unit_two = unit[...]
+    scaled = grad * vec_ref[6:7, :]
+    spread = (
+        scaled
+        - jnp.mean(scaled, axis=1, keepdims=True)
+        - unit_two * jnp.mean(scaled * unit_two, axis=1, keepdims=True)
+    )
+    grad_middle = cot_ref[...].astype(F32) + inverse * spread
+    gmid_out[...] = grad_middle
+    low = (BRANCH * grad_middle).astype(BF)
+    gone_out[pl.ds(pl.multiple_of(mine * 192, 192), 192), :] = low
+    share(1, gone_out)
+    sums_out[0:1, :] = jnp.sum(low.astype(F32), axis=0, keepdims=True)
+    sums_out[1:2, :] = jnp.sum(part(gtwo_ref, mine).astype(F32), axis=0, keepdims=True)
+    sums_out[2:3, :] = jnp.sum(grad * unit_two, axis=0, keepdims=True)
+    sums_out[3:4, :] = jnp.sum(grad, axis=0, keepdims=True)
+    sums_out[4:5, :] = jnp.sum(gexp[...].astype(F32), axis=0, keepdims=True)
+    sums_out[5:8, :] = jnp.zeros((3, D), F32)
+    epart_out[...] = mm_tn(n2[...], gexp[...]).astype(BF)
+    value = mm(part(act, mine), contract_ref[...]) + from_twin(2, 1)
+    block_out[...] = held[...] + BRANCH * (value + vec_ref[3:4, :])
+    over_out[...] = (mm(part(act, p_across), contract_ref[...]) + from_twin(2, 0)).astype(BF)
+    share_across(1, gone_out)
+    share_twin(1, gone_out)
+    share_corner(1, gone_out)
+    for i in range(3):
+        for slot in range(2):
+            remote(c_send_buf.at[i, slot], c_recv_buf.at[i, slot], c_send.at[i, slot], c_recv.at[i, slot], me.twin).wait_send()
+    for i in range(2):
+        remote(x_send_buf.at[i], x_recv_buf.at[i], x_send.at[i], x_recv.at[i], me.across).wait_send()
+    for i, ref in ((0, n2), (1, gone_out)):
+        own = rows_of(ref, mine)
+        for j in range(3):
+            remote(own, own, ag_send.at[i, j], ag_recv.at[i, j], me.twin).wait_send()
+
+
+def feed_forward_near(o, wp, expand, contract, ebias, tokens, cotangent, gtwo, vectors):
+    rows = tokens.shape[0]
+    block = rows * 4
+    vmem = pl.BlockSpec(memory_space=pltpu.VMEM)
+    anywhere = pl.BlockSpec(memory_space=pl.ANY)
+    dma = pltpu.SemaphoreType.DMA
+    return pl.pallas_call(
+        mlp_near_kernel,
+        in_specs=[vmem, anywhere, vmem, anywhere, anywhere, anywhere, anywhere, vmem, vmem],
+        out_specs=[vmem] * 7,
+        out_shape=[
+            jax.ShapeDtypeStruct((rows, D), F32),
+            jax.ShapeDtypeStruct((rows, D), BF),
+            jax.ShapeDtypeStruct((rows, D), F32),
+            jax.ShapeDtypeStruct((block, D), BF),
+            jax.ShapeDtypeStruct((D, D), BF),
+            jax.ShapeDtypeStruct((D, D), BF),
+            jax.ShapeDtypeStruct((8, D), F32),
+        ],
+        scratch_shapes=[
+            pltpu.VMEM((192, D), BF),
+            pltpu.VMEM((D, D), BF),
+            pltpu.VMEM((rows, D), BF),
+            pltpu.VMEM((rows, D), BF),
+            pltpu.VMEM((D,), BF),
+            pltpu.VMEM((1, D), F32),
+            pltpu.VMEM((block, 192), BF),
+            pltpu.VMEM((block, D), F32),
+            pltpu.VMEM((block, D), BF),
+            pltpu.VMEM((block, D), BF),
+            pltpu.VMEM((block, D), BF),
+            pltpu.VMEM((rows, D), F32),
+            pltpu.VMEM((rows, D), F32),
+            pltpu.VMEM((3, 2, rows, D), BF),
+            pltpu.VMEM((3, 2, rows, D), BF),
+            pltpu.VMEM((2, rows, D), BF),
+            pltpu.VMEM((2, rows, D), BF),
+            dma((3, 2)), dma((3, 2)), dma((2,)), dma((2,)), dma((2, 3)), dma((2, 3)), dma((5,)),
+        ],
+        compiler_params=pltpu.CompilerParams(collective_id=7, has_side_effects=True, vmem_limit_bytes=58 << 20),
+        name="feed_forward_near",
+    )(o, wp, expand, contract, ebias, tokens, cotangent, gtwo, vectors)
+
+
 ORDERS = (
     (
         "g0", "A0", "A1", "g1", "g2", "W0", "d0", "X0", "d1", "s0", "s1", "W1",
@@ -1278,15 +1462,15 @@
 
 def attend_reduce_kernel(
     levels, starts_ref, all_ref, k_ref, v_ref, q_ref, o_ref, lse_ref, g_ref, wp_hbm, aw_ref,
-    c_ref, e_ref, tok_hbm, gmid_ref, vec_ref, sums_ref,
-    tg_out, cg_out, eg_out, a_rows, pg_out, vec_out,
-    wp_ref, tok_ref, rows_in, keys_in, values_in, begins, qm, dm, qn, dn, delta, dqt, kt, dk, dv, gt, a_part, p_part,
+    c_ref, e_ref, tok_hbm, gmid_ref, vec_ref, sums_ref, near_ref, over_ref,
+    tg_out, cg_out, eg_out, a_rows, pg_out, vec_out, block_out,
+    over_in, wp_ref, tok_ref, rows_in, keys_in, values_in, begins, qm, dm, qn, dn, delta, dqt, kt, dk, dv, gt, a_part, p_part,
     dnb, far, keep, x_in, y_out, y_in, d_out, d_in,
     yc, ye, ya, yp, zc_out, ze_out, za_out, zp_out, zc_in, ze_in, za_in, zp_in, v_out, v_in, e_move, a_move,
     pre_sem, far_send, far_recv, x_send, x_recv, y_send, y_recv, d_send, d_recv,
     gy_send, gy_recv, gz_send, gz_recv, ay_send, ay_recv, az_send, az_recv,
     me_send, me_recv, ma_send, ma_recv, u_send, u_recv, w_send, w_recv,
-    be_send, be_recv, ba_send, ba_recv, te_send, te_recv, ta_send, ta_recv, v_send, v_recv, local_sem,
+    be_send, be_recv, ba_send, ba_recv, te_send, te_recv, ta_send, ta_recv, v_send, v_recv, local_sem, o_send, o_recv,
 ):
     me = Place()
     z, side, mine, ctx = me.level, me.side, me.part, me.ctx
@@ -1343,6 +1527,8 @@
     all_of(fetched, lambda copy: copy.wait())
     outer = mm_nt(grads_in, wp_ref[...]).astype(BF)
     pl.semaphore_wait(barrier, levels + 3)
+    over = remote(over_ref, over_in, o_send.at[0], o_recv.at[0], me.across)
+    over.start()
     for step in range(levels - 1):
         grads.steps(step, lambda level, way: grads.beside(level, start))
     grads.beside(z, start)
@@ -1755,6 +1941,8 @@
         total = total + v_in[3 + level]
     vec_out[...] = total
 
+    over.wait()
+    block_out[...] = (near_ref[...] + BRANCH * over_in[...].astype(F32)).astype(BF)
     for level in range(levels):
         all_of(side_copies(level, 1 - side), wait_recv)
     for flow in (e_flow, a_flow):
@@ -1795,7 +1983,7 @@
         remote(v_out.at[0], v_in.at[0], v_send.at[i], v_recv.at[0], me.twin).wait_send()
 
 
-def attend_reduce(starts, rows_all, k, v, q, o, lse, g, wp, aw, contract, expand, tokens, grad_middle, vectors, sums):
+def attend_reduce(starts, rows_all, k, v, q, o, lse, g, wp, aw, contract, expand, tokens, grad_middle, vectors, sums, near, over):
     levels = lax.axis_size("ctx") // 2
     rows = tokens.shape[0]
     block = rows * 4
@@ -1812,8 +2000,8 @@
 
     return pl.pallas_call(
         functools.partial(attend_reduce_kernel, levels),
-        in_specs=[pl.BlockSpec(memory_space=pltpu.SMEM)] + [anywhere] * 3 + [vmem] * 4 + [anywhere] + [vmem] * 3 + [anywhere] + [vmem] * 3,
-        out_specs=[vmem] * 6,
+        in_specs=[pl.BlockSpec(memory_space=pltpu.SMEM)] + [anywhere] * 3 + [vmem] * 4 + [anywhere] + [vmem] * 3 + [anywhere] + [vmem] * 5,
+        out_specs=[vmem] * 7,
         out_shape=[
             jax.ShapeDtypeStruct((rows, D), BF),
             jax.ShapeDtypeStruct((2 * n, 96, D), BF),
@@ -1821,9 +2009,10 @@
             jax.ShapeDtypeStruct((2, 4, 96, 576), BF),
             jax.ShapeDtypeStruct((192, D), BF),
             jax.ShapeDtypeStruct((16, D), F32),
+            jax.ShapeDtypeStruct((rows, D), BF),
         ],
         scratch_shapes=[
-            buf(192, D), buf(rows, D),
+            buf(rows, D), buf(192, D), buf(rows, D),
             buf(2, block, D), buf(2, block, 192), buf(2, block, 192), pltpu.VMEM((1, block), jnp.int32),
             buf(3, 128, block), buf(3, 128, block), buf(3, block, 128), buf(3, block, 128),
             wide(8, block), wide(192, block), buf(192, block), wide(block, 192), wide(block, 192), wide(576, D),
@@ -1841,11 +2030,11 @@
             dma((1,)), dma((4,)), dma((1,)), dma((4,)),
             dma((2, n, 2)), dma((2, n, 2)), dma((n, 2)), dma((n, 2)),
             dma((2, 4)), dma((2, 4)), dma((2, 4)), dma((2, 4)), dma((4,)), dma((4,)), dma((4,)), dma((4,)),
-            dma((2 + n,)), dma((3 + n,)), dma((2,)),
+            dma((2 + n,)), dma((3 + n,)), dma((2,)), dma((1,)), dma((1,)),
         ],
         compiler_params=pltpu.CompilerParams(collective_id=5, has_side_effects=True, vmem_limit_bytes=60 << 20),
         name="attend_reduce",
-    )(starts, rows_all, k, v, q, o, lse, g, wp, aw, contract, expand, tokens, grad_middle, vectors, sums)
+    )(starts, rows_all, k, v, q, o, lse, g, wp, aw, contract, expand, tokens, grad_middle, vectors, sums, near, over)
 
 
 def finish_kernel(
@@ -1895,7 +2084,7 @@
             jax.ShapeDtypeStruct((D, D), F32),
             one, one, one, one, one,
         ],
-        compiler_params=pltpu.CompilerParams(vmem_limit_bytes=32 << 20),
+        compiler_params=pltpu.CompilerParams(vmem_limit_bytes=58 << 20),
         name="finish",
     )(tokens_grad, contract, expand, attend, project, vectors, block_output)
 
@@ -2030,19 +2219,19 @@
         tokens, document_starts, attend_weight, attend_bias, expand_weight, cotangent,
         (project_bias, contract_bias, gain_first, shift_first, gain_second, shift_second),
     )
-    block_output, grad_middle, g1, contract_part, expand_part, mlp_sums = feed_forward(
-        o, project_weight, expand_cols, contract_weight, expand_bias, tokens, cotangent, g2, vectors
-    )
+    mlp_args = (o, project_weight, expand_cols, contract_weight, expand_bias, tokens, cotangent, g2, vectors)
     if lax.axis_size("ctx") != 8:
+        block_output, grad_middle, g1, contract_part, expand_part, mlp_sums = feed_forward(*mlp_args)
         return (block_output,) + backward_plain(
             document_starts, normed_all, k, v, q, o, lse, g1, project_weight, attend_cols,
             contract_part, expand_part, tokens, grad_middle, vectors, mlp_sums,
         )
+    near, over, grad_middle, g1, contract_part, expand_part, mlp_sums = feed_forward_near(*mlp_args)
     reduced = attend_reduce(
         document_starts, normed_all, k, v, q, o, lse, g1, project_weight, attend_cols,
-        contract_part.reshape(8, 96, D), expand_part.reshape(8, 96, D), tokens, grad_middle, vectors, mlp_sums,
+        contract_part.reshape(8, 96, D), expand_part.reshape(8, 96, D), tokens, grad_middle, vectors, mlp_sums, near, over,
     )
-    return tuple(finish(*reduced, block_output))
+    return tuple(finish(*reduced))
 
 
 def solution(mesh):

time: 274 us -> 265 us (0.967)
  local copies, waits for them, and re-layouts: 6.46 us -> 0 us
    unnamed x14 -> x0, local copies, waits for them, and re-layouts: 6.46 us -> none
    pallas_call x1, Pallas kernels: 49.8 us -> 44.8 us  [feed_forward_near(): pl.pallas_call(mlp_near_kernel, in_specs=[vmem, anywhere, vmem, anywhere,...]
where the time goes in v6:
time: 265 us; the launch traced here: 262 us
  Pallas kernels  261 us (98%)
    pallas_call x1, Pallas kernels, attend_reduce(): pl.pallas_call(functools.partial(attend_reduce_kernel, levels), in_specs=...  162 us
    pallas_call x1, Pallas kernels, gather_attend(): pl.pallas_call(functools.partial(gather_attend_kernel, levels), in_specs=...  48.2 us
    pallas_call x1, Pallas kernels, feed_forward_near(): pl.pallas_call(mlp_near_kernel, in_specs=[vmem, anywhere, vmem, anywhere,...  44.8 us
    pallas_call x1, Pallas kernels, finish(): pl.pallas_call(finish_kernel, in_specs=[pl.BlockSpec(memory_space=pltpu.V...  6.04 us

profile of v6, /device:TPU:3, one launch (start us, length us, event | category | flops | bytes accessed | tf_op | source)
XLA Modules:
  0.0 262.1 jit_solution(17792279702618010233)
XLA Ops:
  0.6 48.2 %gather_attend.1 = (bf16[6144,768]{1,0:T(8,128)(2,1)}, bf16[768,576]{1,0:T(8,128)(2,1)}, bf16[768,768]{1,0:T(8,128)(2,1)}, bf16[768,768]{1,0:T(8,128)(2,1)}, f32...) custom-call(s32[8]{0:T(128)} %starts_ref.3, ...), custom_call_target="tpu_custom_call" | custom-call | tf_op jit(solution)/shard_map/gather_attend/pallas_call | solution.py:917
  48.9 44.8 %feed_forward_near.1 = (f32[192,768]{1,0:T(8,128)}, bf16[192,768]{1,0:T(8,128)(2,1)}, f32[192,768]{1,0:T(8,128)}, bf16[768,768]{1,0:T(8,128)(2,1)}, bf16[768,768...) custom-call(f32[192,768]{1,0:T(8,128)} %get-tuple-element.42.o_ref, bf16[192,768]{1,0:T(8,128)(2,1)} %wp_hbm.3, ...), custom_call_target="tpu_custom_call" | custom-call | tf_op jit(solution)/shard_map/feed_forward_near/pallas_call | solution.py:1298
  93.7 162.1 %attend_reduce.1 = (bf16[192,768]{1,0:T(8,128)(2,1)}, bf16[8,96,768]{2,1,0:T(8,128)(2,1)}, bf16[192,3072]{1,0:T(8,128)(2,1)}, bf16[2,4,96,576]{3,2,1,0:T(8,128)(...) custom-call(s32[8]{0:T(128)} %starts_ref.3, ...), custom_call_target="tpu_custom_call" | custom-call | tf_op jit(solution)/shard_map/attend_reduce/pallas_call | solution.py:2001
  255.8 6.0 %finish.1 = (bf16[192,768]{1,0:T(8,128)(2,1)}, bf16[192,768]{1,0:T(8,128)(2,1)}, f32[192,2304]{1,0:T(8,128)}, f32[384]{0:T(512)}, f32[192,768]{1,0:T(8,128)}, /*...) custom-call(bf16[192,768]{1,0:T(8,128)(2,1)} %get-tuple-element.55.t, ...), custom_call_target="tpu_custom_call" | custom-call | tf_op jit(solution)/shard_map/finish/pallas_call | solution.py:2072

commit v7 on v6

--- a/solution.py
+++ b/solution.py
@@ -598,7 +598,7 @@
     )(tokens, vectors, attend_cols, expand_weight, cotangent)
 
 
-SHARE = 160
+SHARE = 176
 
 
 def begins_of(starts_ref, first, count):
@@ -740,24 +740,24 @@
             remote(got, got, core_send.at[distance, which, slot], core_recv.at[distance, which, slot], me.twin).wait_recv()
 
     spread(0, 0, True)
+    begins[...] = begins_of(starts_ref, me.ctx * block, block)
+    got = held(0, 1, side)
+    remote(got, got, x_send.at[0], x_recv.at[0], me.across).wait_recv()
+    spread(0, 1, True)
+    def from_below(distance, slot):
+        @pl.when(distance <= z)
+        def _():
+            got = held(distance, slot, side)
+            remote(got, got, z_send.at[distance - 1, slot], z_recv.at[distance, slot], me.twin).wait_recv()
+            spread(distance, slot, False)
+
+    from_below(1, 0)
     two_x = go(remote(own_two, own_two, two_send.at[0], two_recv.at[0], me.across))
     two_c = go(remote(own_two, own_two, two_send.at[1], two_recv.at[1], me.twin))
     exps = [
         go(remote(ew_ref.at[:, pl.ds(pl.multiple_of(p * D, D), D)], rows_of(expand_ref, mine), exp_send.at[i], exp_recv.at[i], d))
         for i, (d, p) in enumerate(peers)
     ]
-    begins[...] = begins_of(starts_ref, me.ctx * block, block)
-    got = held(0, 1, side)
-    remote(got, got, x_send.at[0], x_recv.at[0], me.across).wait_recv()
-    spread(0, 1, True)
-    def from_below(distance, slot):
-        @pl.when(distance <= z)
-        def _():
-            got = held(distance, slot, side)
-            remote(got, got, z_send.at[distance - 1, slot], z_recv.at[distance, slot], me.twin).wait_recv()
-            spread(distance, slot, False)
-
-    from_below(1, 0)
     for copy in atts:
         copy.wait_recv()
     from_twin(0, 0, side, True)

time: 265 us -> 263 us (level)
  no operation moved by 1% of the time
where the time goes in v7:
time: 263 us; the launch traced here: 260 us
  Pallas kernels  259 us (98%)
    pallas_call x1, Pallas kernels, attend_reduce(): pl.pallas_call(functools.partial(attend_reduce_kernel, levels), in_specs=...  160 us
    pallas_call x1, Pallas kernels, gather_attend(): pl.pallas_call(functools.partial(gather_attend_kernel, levels), in_specs=...  48.2 us
    pallas_call x1, Pallas kernels, feed_forward_near(): pl.pallas_call(mlp_near_kernel, in_specs=[vmem, anywhere, vmem, anywhere,...  44.8 us
    pallas_call x1, Pallas kernels, finish(): pl.pallas_call(finish_kernel, in_specs=[pl.BlockSpec(memory_space=pltpu.V...  6.04 us

profile of v7, /device:TPU:3, one launch (start us, length us, event | category | flops | bytes accessed | tf_op | source)
XLA Modules:
  0.0 260.1 jit_solution(4211990081613949306)
XLA Ops:
  0.6 48.2 %gather_attend.1 = (bf16[6144,768]{1,0:T(8,128)(2,1)}, bf16[768,576]{1,0:T(8,128)(2,1)}, bf16[768,768]{1,0:T(8,128)(2,1)}, bf16[768,768]{1,0:T(8,128)(2,1)}, f32...) custom-call(s32[8]{0:T(128)} %starts_ref.3, ...), custom_call_target="tpu_custom_call" | custom-call | tf_op jit(solution)/shard_map/gather_attend/pallas_call | solution.py:917
  48.9 44.8 %feed_forward_near.1 = (f32[192,768]{1,0:T(8,128)}, bf16[192,768]{1,0:T(8,128)(2,1)}, f32[192,768]{1,0:T(8,128)}, bf16[768,768]{1,0:T(8,128)(2,1)}, bf16[768,768...) custom-call(f32[192,768]{1,0:T(8,128)} %get-tuple-element.42.o_ref, bf16[192,768]{1,0:T(8,128)(2,1)} %wp_hbm.3, ...), custom_call_target="tpu_custom_call" | custom-call | tf_op jit(solution)/shard_map/feed_forward_near/pallas_call | solution.py:1298
  93.7 160.2 %attend_reduce.1 = (bf16[192,768]{1,0:T(8,128)(2,1)}, bf16[8,96,768]{2,1,0:T(8,128)(2,1)}, bf16[192,3072]{1,0:T(8,128)(2,1)}, bf16[2,4,96,576]{3,2,1,0:T(8,128)(...) custom-call(s32[8]{0:T(128)} %starts_ref.3, ...), custom_call_target="tpu_custom_call" | custom-call | tf_op jit(solution)/shard_map/attend_reduce/pallas_call | solution.py:2001
  253.9 6.0 %finish.1 = (bf16[192,768]{1,0:T(8,128)(2,1)}, bf16[192,768]{1,0:T(8,128)(2,1)}, f32[192,2304]{1,0:T(8,128)}, f32[384]{0:T(512)}, f32[192,768]{1,0:T(8,128)}, /*...) custom-call(bf16[192,768]{1,0:T(8,128)(2,1)} %get-tuple-element.55.t, ...), custom_call_target="tpu_custom_call" | custom-call | tf_op jit(solution)/shard_map/finish/pallas_call | solution.py:2072
